TPU v7x, 32 devices: a whole 2x2x4 slice. The times are simulated.
32 devices in a mesh: section: 2 (over core), shard: 2 (over x), replica: 8 (over z, y).
Axes of the slice: x: 2, y: 2, z: 4, core: 2. Of those that a mesh axis runs over, the one named last changes fastest.
Arguments:
- tokens: bfloat16 [8, 2, 512, 1024], P('replica', None, 'shard'), may hold values from -6 to 6
- cotangent: bfloat16 [8, 2, 512, 1024], P('replica', None, 'shard'), may hold values from -6 to 6
- attn_gain: bfloat16 [2, 1024], P('section', 'shard'), may hold values from 0.25 to 1.75
- attn_shift: bfloat16 [2, 1024], P('section', 'shard'), may hold values from -3 to 3
- qkv_weight: bfloat16 [2, 1024, 3072], P('section', 'shard'), may hold values from -0.1875 to 0.1875
- query_bias: bfloat16 [2, 1024], P('section', 'shard'), may hold values from -3 to 3
- value_bias: bfloat16 [2, 1024], P('section', 'shard'), may hold values from -0.59765625 to 0.59765625
- out_weight: bfloat16 [2, 1024, 1024], P('section', 'shard'), may hold values from -1 to 1
- out_bias: bfloat16 [2, 1024], P('section', 'shard'), may hold values from -1.796875 to 1.796875
- mlp_gain: bfloat16 [2, 1024], P('section', 'shard'), may hold values from 0.25 to 1.75
- mlp_shift: bfloat16 [2, 1024], P('section', 'shard'), may hold values from -3 to 3
- fc_weight: bfloat16 [2, 1024, 4096], P('section', 'shard'), may hold values from -0.1875 to 0.1875
- fc_bias: bfloat16 [2, 4096], P('section', 'shard'), may hold values from -3 to 3
- proj_weight: bfloat16 [2, 4096, 1024], P('section', 'shard'), may hold values from -0.09375 to 0.09375
- proj_bias: bfloat16 [2, 1024], P('section', 'shard'), may hold values from -1.796875 to 1.796875
Outputs:
- activations: bfloat16 [2, 8, 2, 512, 1024], P('section', 'replica', None, 'shard')
- input_grads: bfloat16 [2, 8, 2, 512, 1024], P('section', 'replica', None, 'shard')
- attn_gain_grad: float32 [2, 1024], P('section', 'shard')
- attn_shift_grad: float32 [2, 1024], P('section', 'shard')
- qkv_weight_grad: float32 [2, 1024, 3072], P('section', 'shard')
- query_bias_grad: float32 [2, 1024], P('section', 'shard')
- value_bias_grad: float32 [2, 1024], P('section', 'shard')
- out_weight_grad: float32 [2, 1024, 1024], P('section', 'shard')
- out_bias_grad: float32 [2, 1024], P('section', 'shard')
- mlp_gain_grad: float32 [2, 1024], P('section', 'shard')
- mlp_shift_grad: float32 [2, 1024], P('section', 'shard')
- fc_weight_grad: float32 [2, 1024, 4096], P('section', 'shard')
- fc_bias_grad: float32 [2, 4096], P('section', 'shard')
- proj_weight_grad: float32 [2, 4096, 1024], P('section', 'shard')
- proj_bias_grad: float32 [2, 1024], P('section', 'shard')
All inputs are finite; a program needn't handle non-finite values.
Results may differ from a plain program's by a relative error of at most 0.023.
Values may be sent and summed in bfloat16 or wider, within the bound.
A program may use at most 320 MiB of HBM per device.

v0:
```python
import jax
import jax.numpy as jnp
from jax import lax
from jax.sharding import PartitionSpec as P

HEAD_DIM = 64


EPSILON = 1e-05
GELU_SCALE = 0.7978845608028654
GELU_CUBIC = 0.044715
ROWS_CONTRACT = (((0,), (0,)), ((), ()))
COLS_CONTRACT = (((1,), (1,)), ((), ()))


def shifted(shard, axis, by):
    size = lax.axis_size(axis)
    pairs = [(i, i + by) for i in range(size) if 0 <= i + by < size]
    return lax.ppermute(shard, axis, pairs)


def rows_product(left, right):
    return lax.dot_general(left, right, ROWS_CONTRACT, preferred_element_type=jnp.float32)


def cols_product(left, right):
    return lax.dot_general(left, right, COLS_CONTRACT, preferred_element_type=jnp.float32)


def norm_forward(inputs, gain, shift):
    mean = jnp.mean(inputs, axis=-1, keepdims=True)
    centered = inputs - mean
    inverse = lax.rsqrt(jnp.mean(centered * centered, axis=-1, keepdims=True) + EPSILON)
    scaled = centered * inverse
    normed = (scaled * gain.astype(jnp.float32) + shift.astype(jnp.float32)).astype(jnp.bfloat16)
    return (normed, scaled, inverse)


def norm_backward(d_normed, scaled, inverse, gain):
    d_scaled = d_normed * gain.astype(jnp.float32)
    d_inputs = inverse * (
        d_scaled
        - jnp.mean(d_scaled, axis=-1, keepdims=True)
        - scaled * jnp.mean(d_scaled * scaled, axis=-1, keepdims=True)
    )
    return (d_inputs, jnp.sum(d_normed * scaled, axis=0), jnp.sum(d_normed, axis=0))


def gelu_pair(pre):
    tangent = jnp.tanh(GELU_SCALE * (pre + GELU_CUBIC * pre * pre * pre))
    value = 0.5 * pre * (1.0 + tangent)
    slope = 0.5 * (1.0 + tangent) + 0.5 * pre * (1.0 - tangent * tangent) * GELU_SCALE * (
        1.0 + 3.0 * GELU_CUBIC * pre * pre
    )
    return (value, slope)


def attention_scores(query, keys_all, offset, scale):
    scores = jnp.einsum("qhe,khe->hqk", query, keys_all, preferred_element_type=jnp.float32) * scale
    key_pos = jnp.arange(keys_all.shape[0], dtype=jnp.int32)
    query_pos = offset + jnp.arange(query.shape[0], dtype=jnp.int32)
    allowed = key_pos[None, :] <= query_pos[:, None]
    return jnp.where(allowed[None], scores, -jnp.inf)


def forward_layer(inputs, weights, offset, buffers, start):
    (
        attn_gain,
        attn_shift,
        qkv_weight,
        query_bias,
        value_bias,
        out_weight,
        out_bias,
        mlp_gain,
        mlp_shift,
        fc_weight,
        fc_bias,
        proj_weight,
        proj_bias,
    ) = weights
    count, width = inputs.shape
    heads = width // HEAD_DIM
    scale = HEAD_DIM ** (-0.5)
    normed1, scaled1, inverse1 = norm_forward(inputs, attn_gain, attn_shift)
    qkv = jnp.dot(normed1, qkv_weight, preferred_element_type=jnp.float32)
    query = (qkv[:, :width] + query_bias.astype(jnp.float32)).astype(jnp.bfloat16)
    keys = qkv[:, width : 2 * width].astype(jnp.bfloat16)
    values = (qkv[:, 2 * width :] + value_bias.astype(jnp.float32)).astype(jnp.bfloat16)
    keys_block, values_block = (
        lax.all_gather(keys, "shard", axis=0, tiled=True),
        lax.all_gather(values, "shard", axis=0, tiled=True),
    )
    keys_buffer = lax.dynamic_update_slice_in_dim(buffers[0], keys_block, start, 0)
    values_buffer = lax.dynamic_update_slice_in_dim(buffers[1], values_block, start, 0)
    query = query.reshape(count, heads, HEAD_DIM)
    keys_all = keys_buffer.reshape(-1, heads, HEAD_DIM)
    values_all = values_buffer.reshape(-1, heads, HEAD_DIM)
    scores = attention_scores(query, keys_all, offset, scale)
    top = jnp.max(scores, axis=-1, keepdims=True)
    total = jnp.sum(jnp.exp(scores - top), axis=-1, keepdims=True)
    log_total = top + jnp.log(total)
    probs = jnp.exp(scores - log_total).astype(jnp.bfloat16)
    mixed = jnp.einsum("hqk,khe->qhe", probs, values_all, preferred_element_type=jnp.float32)
    mixed = mixed.reshape(count, width).astype(jnp.bfloat16)
    hidden = (
        inputs
        + jnp.dot(mixed, out_weight, preferred_element_type=jnp.float32)
        + out_bias.astype(jnp.float32)
    )
    normed2, scaled2, inverse2 = norm_forward(hidden, mlp_gain, mlp_shift)
    pre = jnp.dot(normed2, fc_weight, preferred_element_type=jnp.float32) + fc_bias.astype(
        jnp.float32
    )
    activated, slope = gelu_pair(pre)
    act = activated.astype(jnp.bfloat16)
    output = (
        hidden
        + jnp.dot(act, proj_weight, preferred_element_type=jnp.float32)
        + proj_bias.astype(jnp.float32)
    )
    kept = (
        scaled1,
        inverse1,
        normed1,
        query,
        log_total,
        mixed,
        scaled2,
        inverse2,
        normed2,
        slope,
        act,
    )
    return (output, kept, (keys_buffer, values_buffer))


def mlp_backward(grad_out, kept, weights):
    (
        attn_gain,
        attn_shift,
        qkv_weight,
        query_bias,
        value_bias,
        out_weight,
        out_bias,
        mlp_gain,
        mlp_shift,
        fc_weight,
        fc_bias,
        proj_weight,
        proj_bias,
    ) = weights
    scaled1, inverse1, normed1, query, log_total, mixed, scaled2, inverse2, normed2, slope, act = (
        kept
    )
    grad_low = grad_out.astype(jnp.bfloat16)
    proj_weight_grad = rows_product(act, grad_low)
    proj_bias_grad = jnp.sum(grad_out, axis=0)
    d_pre = (cols_product(grad_low, proj_weight) * slope).astype(jnp.bfloat16)
    fc_weight_grad = rows_product(normed2, d_pre)
    fc_bias_grad = jnp.sum(d_pre.astype(jnp.float32), axis=0)
    d_normed2 = cols_product(d_pre, fc_weight)
    d_norm, mlp_gain_grad, mlp_shift_grad = norm_backward(d_normed2, scaled2, inverse2, mlp_gain)
    return (
        grad_out + d_norm,
        (
            mlp_gain_grad,
            mlp_shift_grad,
            fc_weight_grad,
            fc_bias_grad,
            proj_weight_grad,
            proj_bias_grad,
        ),
    )


def attn_backward(d_hidden, kept, weights, offset, buffers, pending, start, block, active):
    (
        attn_gain,
        attn_shift,
        qkv_weight,
        query_bias,
        value_bias,
        out_weight,
        out_bias,
        mlp_gain,
        mlp_shift,
        fc_weight,
        fc_bias,
        proj_weight,
        proj_bias,
    ) = weights
    scaled1, inverse1, normed1, query, log_total, mixed, scaled2, inverse2, normed2, slope, act = (
        kept
    )
    count, width = d_hidden.shape
    heads = width // HEAD_DIM
    scale = HEAD_DIM ** (-0.5)
    keys_all = buffers[0].reshape(-1, heads, HEAD_DIM)
    values_all = buffers[1].reshape(-1, heads, HEAD_DIM)
    d_branch = d_hidden.astype(jnp.bfloat16)
    out_weight_grad = rows_product(mixed, d_branch)
    out_bias_grad = jnp.sum(d_branch.astype(jnp.float32), axis=0)
    d_mixed = (
        cols_product(d_branch, out_weight).astype(jnp.bfloat16).reshape(count, heads, HEAD_DIM)
    )
    scores = attention_scores(query, keys_all, offset, scale)
    weights_full = jnp.exp(scores - log_total)
    probs = weights_full.astype(jnp.bfloat16)
    d_probs = jnp.einsum(
        "qhe,khe->hqk", d_mixed, values_all, preferred_element_type=jnp.float32
    ).astype(jnp.bfloat16)
    row_total = jnp.sum(d_probs * weights_full, axis=-1, keepdims=True)
    d_scores = (weights_full * (d_probs - row_total)).astype(jnp.bfloat16)
    d_values = jnp.einsum(
        "hqk,qhe->khe", probs, d_mixed, preferred_element_type=jnp.float32
    ).reshape(-1, width)
    d_query = (
        (jnp.einsum("hqk,khe->qhe", d_scores, keys_all, preferred_element_type=jnp.float32) * scale)
        .reshape(count, width)
        .astype(jnp.bfloat16)
    )
    d_keys = (
        jnp.einsum("hqk,qhe->khe", d_scores, query, preferred_element_type=jnp.float32) * scale
    ).reshape(-1, width)
    keys_pending = pending[0] + active * d_keys
    values_pending = pending[1] + active * d_values
    keys_slice = lax.dynamic_slice_in_dim(keys_pending, start, block, 0)
    values_slice = lax.dynamic_slice_in_dim(values_pending, start, block, 0)
    d_keys_own, d_values_own = (
        lax.psum_scatter(
            keys_slice.astype(jnp.bfloat16), "shard", scatter_dimension=0, tiled=True
        ).astype(jnp.float32),
        lax.psum_scatter(
            values_slice.astype(jnp.bfloat16), "shard", scatter_dimension=0, tiled=True
        ).astype(jnp.float32),
    )
    d_values_low = d_values_own.astype(jnp.bfloat16)
    d_qkv = jnp.concatenate([d_query, d_keys_own.astype(jnp.bfloat16), d_values_low], axis=1)
    qkv_weight_grad = rows_product(normed1, d_qkv)
    query_bias_grad = jnp.sum(d_query.astype(jnp.float32), axis=0)
    value_bias_grad = jnp.sum(d_values_low.astype(jnp.float32), axis=0)
    d_normed1 = cols_product(d_qkv, qkv_weight)
    d_norm, attn_gain_grad, attn_shift_grad = norm_backward(d_normed1, scaled1, inverse1, attn_gain)
    grads = (
        attn_gain_grad,
        attn_shift_grad,
        qkv_weight_grad,
        query_bias_grad,
        value_bias_grad,
        out_weight_grad,
        out_bias_grad,
    )
    return (d_hidden + d_norm, grads, (keys_pending, values_pending))


def shards(
    tokens,
    cotangent,
    attn_gain,
    attn_shift,
    qkv_weight,
    query_bias,
    value_bias,
    out_weight,
    out_bias,
    mlp_gain,
    mlp_shift,
    fc_weight,
    fc_bias,
    proj_weight,
    proj_bias,
):
    gathered = (
        lax.all_gather(attn_gain, "shard", axis=1, tiled=True),
        lax.all_gather(attn_shift, "shard", axis=1, tiled=True),
        lax.all_gather(qkv_weight, "shard", axis=1, tiled=True),
        lax.all_gather(query_bias, "shard", axis=1, tiled=True),
        lax.all_gather(value_bias, "shard", axis=1, tiled=True),
        lax.all_gather(out_weight, "shard", axis=1, tiled=True),
        lax.all_gather(out_bias, "shard", axis=1, tiled=True),
        lax.all_gather(mlp_gain, "shard", axis=1, tiled=True),
        lax.all_gather(mlp_shift, "shard", axis=1, tiled=True),
        lax.all_gather(fc_weight, "shard", axis=1, tiled=True),
        lax.all_gather(fc_bias, "shard", axis=1, tiled=True),
        lax.all_gather(proj_weight, "shard", axis=1, tiled=True),
        lax.all_gather(proj_bias, "shard", axis=1, tiled=True),
    )
    weights = tuple((piece[0] for piece in gathered))
    section = lax.axis_index("section")
    first = section == 0
    micro = tokens.shape[1]
    count = tokens.shape[2]
    width = tokens.shape[3]
    block = count * lax.axis_size("shard")
    shard_offset = lax.axis_index("shard") * count
    received = jnp.zeros((count, width), jnp.bfloat16)
    buffers = (
        jnp.zeros((micro * block, width), jnp.bfloat16),
        jnp.zeros((micro * block, width), jnp.bfloat16),
    )
    kept_list = []
    outputs = []
    for step in range(micro + 1):
        micro_index = jnp.where(first, min(step, micro - 1), max(step - 1, 0)).astype(jnp.int32)
        start = micro_index * block
        layer_in = jnp.where(first, tokens[0, min(step, micro - 1)], received)
        output, kept, buffers = forward_layer(
            layer_in.astype(jnp.float32), weights, start + shard_offset, buffers, start
        )
        output_low = output.astype(jnp.bfloat16)
        kept_list.append(kept)
        outputs.append(output_low)
        if step < micro:
            received = shifted(output_low, "section", 1)
    activations = jnp.stack(
        [jnp.where(first, outputs[index], outputs[index + 1]) for index in range(micro)]
    )[None, None]
    regathered = (
        lax.all_gather(attn_gain, "shard", axis=1, tiled=True),
        lax.all_gather(attn_shift, "shard", axis=1, tiled=True),
        lax.all_gather(qkv_weight, "shard", axis=1, tiled=True),
        lax.all_gather(query_bias, "shard", axis=1, tiled=True),
        lax.all_gather(value_bias, "shard", axis=1, tiled=True),
        lax.all_gather(out_weight, "shard", axis=1, tiled=True),
        lax.all_gather(out_bias, "shard", axis=1, tiled=True),
        lax.all_gather(mlp_gain, "shard", axis=1, tiled=True),
        lax.all_gather(mlp_shift, "shard", axis=1, tiled=True),
        lax.all_gather(fc_weight, "shard", axis=1, tiled=True),
        lax.all_gather(fc_bias, "shard", axis=1, tiled=True),
        lax.all_gather(proj_weight, "shard", axis=1, tiled=True),
        lax.all_gather(proj_bias, "shard", axis=1, tiled=True),
    )
    back_weights = tuple((piece[0] for piece in regathered))
    attn_sums = tuple((jnp.zeros(item.shape, jnp.float32) for item in back_weights[:7]))
    mlp_sums = tuple((jnp.zeros(item.shape, jnp.float32) for item in back_weights[7:]))
    pending = (
        jnp.zeros((micro * block, width), jnp.float32),
        jnp.zeros((micro * block, width), jnp.float32),
    )
    grad_received = jnp.zeros((count, width), jnp.bfloat16)
    input_list = []
    for step in range(micro + 1):
        grad_in = jnp.where(first, grad_received, cotangent[0, max(micro - 1 - step, 0)])
        kept = kept_list[micro - step]
        micro_index = jnp.where(
            first, min(micro - step, micro - 1), max(micro - 1 - step, 0)
        ).astype(jnp.int32)
        start = micro_index * block
        active = jnp.where(first, 1.0 if step >= 1 else 0.0, 1.0 if step < micro else 0.0).astype(
            jnp.float32
        )
        d_hidden, mlp_terms = mlp_backward(grad_in.astype(jnp.float32), kept, back_weights)
        mlp_sums = tuple((total + active * term for total, term in zip(mlp_sums, mlp_terms)))
        d_inputs, attn_terms, pending = attn_backward(
            d_hidden,
            kept,
            back_weights,
            start + shard_offset,
            buffers,
            pending,
            start,
            block,
            active,
        )
        attn_sums = tuple((total + active * term for total, term in zip(attn_sums, attn_terms)))
        inputs_low = d_inputs.astype(jnp.bfloat16)
        input_list.append(inputs_low)
        if step < micro:
            grad_received = shifted(inputs_low, "section", -1)
    input_grads = jnp.stack(
        [
            jnp.where(first, input_list[micro - index], input_list[micro - 1 - index])
            for index in range(micro)
        ]
    )[None, None]
    owned = (
        lax.psum_scatter(
            attn_sums[0].astype(jnp.bfloat16), "shard", scatter_dimension=0, tiled=True
        ).astype(jnp.float32),
        lax.psum_scatter(
            attn_sums[1].astype(jnp.bfloat16), "shard", scatter_dimension=0, tiled=True
        ).astype(jnp.float32),
        lax.psum_scatter(
            attn_sums[2].astype(jnp.bfloat16), "shard", scatter_dimension=0, tiled=True
        ).astype(jnp.float32),
        lax.psum_scatter(
            attn_sums[3].astype(jnp.bfloat16), "shard", scatter_dimension=0, tiled=True
        ).astype(jnp.float32),
        lax.psum_scatter(
            attn_sums[4].astype(jnp.bfloat16), "shard", scatter_dimension=0, tiled=True
        ).astype(jnp.float32),
        lax.psum_scatter(
            attn_sums[5].astype(jnp.bfloat16), "shard", scatter_dimension=0, tiled=True
        ).astype(jnp.float32),
        lax.psum_scatter(
            attn_sums[6].astype(jnp.bfloat16), "shard", scatter_dimension=0, tiled=True
        ).astype(jnp.float32),
        lax.psum_scatter(
            mlp_sums[0].astype(jnp.bfloat16), "shard", scatter_dimension=0, tiled=True
        ).astype(jnp.float32),
        lax.psum_scatter(
            mlp_sums[1].astype(jnp.bfloat16), "shard", scatter_dimension=0, tiled=True
        ).astype(jnp.float32),
        lax.psum_scatter(
            mlp_sums[2].astype(jnp.bfloat16), "shard", scatter_dimension=0, tiled=True
        ).astype(jnp.float32),
        lax.psum_scatter(
            mlp_sums[3].astype(jnp.bfloat16), "shard", scatter_dimension=0, tiled=True
        ).astype(jnp.float32),
        lax.psum_scatter(
            mlp_sums[4].astype(jnp.bfloat16), "shard", scatter_dimension=0, tiled=True
        ).astype(jnp.float32),
        lax.psum_scatter(
            mlp_sums[5].astype(jnp.bfloat16), "shard", scatter_dimension=0, tiled=True
        ).astype(jnp.float32),
    )
    final_grads = (
        lax.psum(owned[0].astype(jnp.bfloat16), "replica").astype(jnp.float32),
        lax.psum(owned[1].astype(jnp.bfloat16), "replica").astype(jnp.float32),
        lax.psum(owned[2].astype(jnp.bfloat16), "replica").astype(jnp.float32),
        lax.psum(owned[3].astype(jnp.bfloat16), "replica").astype(jnp.float32),
        lax.psum(owned[4].astype(jnp.bfloat16), "replica").astype(jnp.float32),
        lax.psum(owned[5].astype(jnp.bfloat16), "replica").astype(jnp.float32),
        lax.psum(owned[6].astype(jnp.bfloat16), "replica").astype(jnp.float32),
        lax.psum(owned[7].astype(jnp.bfloat16), "replica").astype(jnp.float32),
        lax.psum(owned[8].astype(jnp.bfloat16), "replica").astype(jnp.float32),
        lax.psum(owned[9].astype(jnp.bfloat16), "replica").astype(jnp.float32),
        lax.psum(owned[10].astype(jnp.bfloat16), "replica").astype(jnp.float32),
        lax.psum(owned[11].astype(jnp.bfloat16), "replica").astype(jnp.float32),
        lax.psum(owned[12].astype(jnp.bfloat16), "replica").astype(jnp.float32),
    )
    shaped = tuple((item[None] for item in final_grads))
    return (activations, input_grads) + shaped


def solution(mesh):
    in_specs = (
        P("replica", None, "shard", None),
        P("replica", None, "shard", None),
        P("section", "shard"),
        P("section", "shard"),
        P("section", "shard", None),
        P("section", "shard"),
        P("section", "shard"),
        P("section", "shard", None),
        P("section", "shard"),
        P("section", "shard"),
        P("section", "shard"),
        P("section", "shard", None),
        P("section", "shard"),
        P("section", "shard", None),
        P("section", "shard"),
    )
    out_specs = (
        P("section", "replica", None, "shard", None),
        P("section", "replica", None, "shard", None),
        P("section", "shard"),
        P("section", "shard"),
        P("section", "shard", None),
        P("section", "shard"),
        P("section", "shard"),
        P("section", "shard", None),
        P("section", "shard"),
        P("section", "shard"),
        P("section", "shard"),
        P("section", "shard", None),
        P("section", "shard"),
        P("section", "shard", None),
        P("section", "shard"),
    )
    return jax.shard_map(shards, mesh=mesh, in_specs=in_specs, out_specs=out_specs, check_vma=False)
```

profile of v0, /device:TPU:1, one launch (start us, length us, event | category | flops | bytes accessed | tf_op | source)
XLA Modules:
  0.0 1611.0 jit_solution(934981670217003239)
XLA Ops:
  24.6 67.5 %all-gather.11.cloned.1.call-done = bf16[1,1024,3072]{2,1,0:T(8,128)(2,1)} async-done(((bf16[1,512,3072]{2,1,0:T(8,128)(2,1)}), bf16[1,1024,3072]{2,1,0:T(8,128)(2,1)}) %all-gather.11.cloned.1.call-update) | async-done | bytes 6291472 | tf_op jit(solution)/shard_map/all_gather | solution.py:278
  92.1 4.7 fusion.55
  125.7 19.0 %all-gather.15.cloned.1.call-done = bf16[512,1024]{1,0:T(8,128)(2,1)} async-done(((bf16[256,1024]{1,0:T(8,128)(2,1)}), bf16[512,1024]{1,0:T(8,128)(2,1)}) %all-gather.15.cloned.1.call-update) | async-done | bytes 1048592 | tf_op jit(solution)/shard_map/all_gather | solution.py:91
  151.5 4.4 fusion.9
  155.9 4.3 exponential_reduce_fusion.2
  160.3 5.2 fusion.164
  165.6 13.7 all-gather.17.cloned.1.call-done
  182.2 102.5 %all-gather.19.cloned.1.call-done = bf16[1,1024,4096]{2,1,0:T(8,128)(2,1)} async-done(((bf16[1,512,4096]{2,1,0:T(8,128)(2,1)}), bf16[1,1024,4096]{2,1,0:T(8,128)(2,1)}) %all-gather.19.cloned.1.call-update) | async-done | bytes 8388624 | tf_op jit(solution)/shard_map/all_gather | solution.py:285
  284.7 7.8 fusion.66
  292.5 97.7 %all-gather.21.cloned.1.call-done = bf16[1,4096,1024]{2,1,0:T(8,128)(2,1)} async-done(((bf16[1,2048,1024]{2,1,0:T(8,128)(2,1)}), bf16[1,4096,1024]{2,1,0:T(8,128)(2,1)}) %all-gather.21.cloned.1.call-update) | async-done | bytes 8388624 | tf_op jit(solution)/shard_map/all_gather | solution.py:287
  390.2 7.5 fusion.160
  402.0 4.7 fusion.53
  412.5 17.8 %all-gather.25.cloned.1.call-done = bf16[512,1024]{1,0:T(8,128)(2,1)} async-done(((bf16[256,1024]{1,0:T(8,128)(2,1)}), bf16[512,1024]{1,0:T(8,128)(2,1)}) %all-gather.25.cloned.1.call-update) | async-done | bytes 1048592 | tf_op jit(solution)/shard_map/all_gather | solution.py:91
  430.3 23.5 %all-gather.23.cloned.1.call-done = bf16[512,1024]{1,0:T(8,128)(2,1)} async-done(((bf16[256,1024]{1,0:T(8,128)(2,1)}), bf16[512,1024]{1,0:T(8,128)(2,1)}) %all-gather.23.cloned.1.call-update) | async-done | bytes 1048592 | tf_op jit(solution)/shard_map/all_gather | solution.py:92
  463.1 4.3 fusion.10
  471.8 4.5 fusion.163
  477.5 6.2 fusion.69
  499.5 16.4 %all-gather.27.cloned.1.call-done = bf16[512,1024]{1,0:T(8,128)(2,1)} async-done(((bf16[256,1024]{1,0:T(8,128)(2,1)}), bf16[512,1024]{1,0:T(8,128)(2,1)}) %all-gather.27.cloned.1.call-update) | async-done | bytes 1048592 | tf_op jit(solution)/shard_map/all_gather | solution.py:92
  522.2 17.1 %all-gather.29.cloned.1.call-done = bf16[512,1024]{1,0:T(8,128)(2,1)} async-done(((bf16[256,1024]{1,0:T(8,128)(2,1)}), bf16[512,1024]{1,0:T(8,128)(2,1)}) %all-gather.29.cloned.1.call-update) | async-done | bytes 1048592 | tf_op jit(solution)/shard_map/all_gather | solution.py:91
  545.5 4.8 fusion.11
  550.3 4.3 exponential_reduce_fusion
  556.6 4.5 convolution_convert_fusion.3
  562.3 6.5 fusion.72
  568.8 5.3 convert_reduce_fusion.2
  574.2 7.4 multiply_reduce_fusion.2
  587.2 8.3 fusion.256
  595.5 13.6 fusion
  610.8 10.8 fusion.2
  627.5 8.2 convert_reduce_fusion.17
  635.7 18.2 %reduce-scatter.11.cloned.1.call-done = bf16[256,1024]{0,1:T(8,128)(2,1)} async-done(((bf16[512,1024]{0,1:T(8,128)(2,1)}), bf16[256,1024]{0,1:T(8,128)(2,1)}) %reduce-scatter.11.cloned.1.call-update) | async-done | bytes 524304 | tf_op jit(solution)/shard_map/reduce_scatter | solution.py:232
  653.9 6.2 fusion.208
  665.7 8.1 convert_reduce_fusion.1
  682.7 7.7 convolution_convert_fusion.1
  690.3 8.8 fusion.3
  699.1 9.6 multiply_add_fusion.4
  711.6 10.2 fusion.5
  728.5 8.1 convert_reduce_fusion.16
  736.6 17.6 %reduce-scatter.15.cloned.1.call-done = bf16[256,1024]{0,1:T(8,128)(2,1)} async-done(((bf16[512,1024]{0,1:T(8,128)(2,1)}), bf16[256,1024]{0,1:T(8,128)(2,1)}) %reduce-scatter.15.cloned.1.call-update) | async-done | bytes 524304 | tf_op jit(solution)/shard_map/reduce_scatter | solution.py:232
  754.2 6.2 fusion.217
  768.5 11.6 convert_reduce_fusion
  780.1 6.8 multiply_reduce_fusion
  792.0 7.7 convolution_convert_fusion
  799.7 9.2 fusion.6
  819.6 9.5 fusion.8
  841.8 8.3 fusion.239
  850.1 6.6 fusion.238
  863.0 14.0 add_convert_fusion.2
  878.2 10.0 fusion.288
  888.2 8.3 fusion.287
  896.5 17.1 %add_convert_fusion.1 = bf16[1024,4096]{1,0:T(8,128)(2,1)} fusion(f32[1024,4096]{1,0:T(8,128)} %fusion.287, f32[1024,4096]{1,0:T(8,128)} %fusion.288, bf16[256,4096]{1,0:T(8,128)(2,1)} %copy-done.71, f32[]{:T(128)S(6)} %select_n.119, f32[]{:T(128)S(6)} %select_n.114, f32[256,1024]{1,0:T(8,128)S(1)} %copy-done.22, f32[1024]{0:T(1024)S(1)} %bitcast.409, ...), kind=kOutput, calls=%fused_computation.16 | convolution fusion | flops 2169765888 | bytes 45099016 | tf_op jit(solution)/shard_map/dot_general | solution.py:23
  914.8 10.9 fusion.244
  925.8 8.6 fusion.289
  934.4 19.0 %add_convert_fusion = bf16[4096,1024]{1,0:T(8,128)(2,1)} fusion(f32[4096,1024]{1,0:T(8,128)} %fusion.289, f32[4096,1024]{1,0:T(8,128)} %fusion.244, bf16[256,1024]{1,0:T(8,128)(2,1)S(1)} %copy-done.56, f32[]{:T(128)S(6)} %select_n.119, f32[]{:T(128)S(6)} %select_n.114, f32[256,4096]{1,0:T(8,128)} %fusion.66), kind=kOutput, calls=%fused_computation.15 | convolution fusion | flops 2177892352 | bytes 46661640 | tf_op jit(solution)/shard_map/dot_general | solution.py:23
  953.8 23.6 %reduce-scatter.23.cloned.1.call-done = bf16[512,3072]{1,0:T(8,128)(2,1)} async-done(((bf16[1024,3072]{1,0:T(8,128)(2,1)}), bf16[512,3072]{1,0:T(8,128)(2,1)}) %reduce-scatter.23.cloned.1.call-update) | async-done | bytes 3145744 | tf_op jit(solution)/shard_map/reduce_scatter | solution.py:385
  977.4 102.1 %reduce-scatter.27.cloned.1.call-done = bf16[512,4096]{1,0:T(8,128)(2,1)} async-done(((bf16[1024,4096]{1,0:T(8,128)(2,1)}), bf16[512,4096]{1,0:T(8,128)(2,1)}) %reduce-scatter.27.cloned.1.call-update) | async-done | bytes 4194320 | tf_op jit(solution)/shard_map/reduce_scatter | solution.py:406
  1079.6 102.1 %reduce-scatter.29.cloned.1.call-done = bf16[2048,1024]{1,0:T(8,128)(2,1)} async-done(((bf16[4096,1024]{1,0:T(8,128)(2,1)}), bf16[2048,1024]{1,0:T(8,128)(2,1)}) %reduce-scatter.29.cloned.1.call-update) | async-done | bytes 4194320 | tf_op jit(solution)/shard_map/reduce_scatter | solution.py:412
  1184.5 7.6 fusion.198
  1194.1 6.0 fusion.224
  1200.3 6.3 all-reduce.13
  1207.2 32.8 %all-reduce.11 = (bf16[1,512]{1,0:T(2,128)(2,1)S(1)}, bf16[1,512]{1,0:T(2,128)(2,1)S(1)}, bf16[1,512]{1,0:T(2,128)(2,1)S(1)}, bf16[1,512]{1,0:T(2,128)(2,1)S(1)}...) all-reduce(bf16[1,512]{1,0:T(2,128)(2,1)S(1)} %broadcast_in_dim.210, ...), channel_id=1, replica_groups=mesh['section'=2,'shard'=2,'replica'=8] {'replica'}, use_global_device_ids=true, to_apply=%region_43.44 | all-reduce | flops 6144 | bytes 24576 | tf_op jit(solution)/shard_map/psum | solution.py:420
  1248.3 339.3 %all-reduce.16.cloned.1.call-done = (bf16[1,512,3072]{2,1,0:T(8,128)(2,1)}, bf16[1,512,1024]{2,1,0:T(8,128)(2,1)}, bf16[1,512,4096]{2,1,0:T(8,128)(2,1)}, bf16[1,2048,1024]{2,1,0:T(8,128)(2,1)}) async-done(((bf16[1,512,3072]{2,1,0:T(8,128)(2,1)}, bf16[1,512,1024]{2,1,0:T(8,128)(2,1)}, bf16[1,512,4096]{2,1,0:T(8,128)(2,1)}, bf16[1,2048,1024]{2,1,0:T(8,128)(2,1)}), (bf16[1,512,3072]{2,1,0:T(8,128)(2,1)}, ...) | async-done | bytes 12582928 | tf_op jit(solution)/shard_map/psum | solution.py:422
  1587.6 5.5 broadcast_in_dim.215
  1594.7 4.5 broadcast_in_dim.229
  1599.2 4.4 broadcast_in_dim.233
  (527 shorter events, 207.7 us)
Async XLA Ops:
  7.2 84.9 %copy-start.37 = (bf16[1,2,256,1024]{3,2,1,0:T(8,128)(2,1)S(1)}, bf16[1,2,256,1024]{3,2,1,0:T(8,128)(2,1)}, u32[]{:S(2)}) copy-start(bf16[1,2,256,1024]{3,2,1,0:T(8,128)(2,1)} %param.15) | copy-start | bytes 3145732
  7.2 84.9 %all-gather.11.cloned.1.call-start = ((), (), s32[]{:S(2)}) async-start(), calls=%async_computation.10 | async-start | bytes 9437184 | tf_op jit(solution)/shard_map/all_gather | solution.py:278
  7.9 113.6 %all-gather.13.cloned.1.call-start = ((), (), s32[]{:S(2)}) async-start(), calls=%async_computation.11 | async-start | bytes 1572864 | tf_op jit(solution)/shard_map/all_gather | solution.py:92
  11.9 479.0 %copy-start.89 = (f32[1,1024]{1,0:T(1,128)}, f32[1,1024]{1,0:T(1,128)S(1)}, u32[]{:S(2)}) copy-start(f32[1,1024]{1,0:T(1,128)S(1)} %add.671) | copy-start | bytes 12292
  23.2 73.5 %copy-start.109 = (f32[256]{0:T(256)}, f32[256]{0:T(256)S(1)}, u32[]{:S(2)}) copy-start(f32[256]{0:T(256)S(1)} %broadcast_multiply_fusion.18) | copy-start | bytes 3076
  24.6 72.2 %copy-start.122 = (f32[256]{0:T(256)}, f32[256]{0:T(256)S(1)}, u32[]{:S(2)}) copy-start(f32[256]{0:T(256)S(1)} %add_rsqrt_fusion.5) | copy-start | bytes 3076
  99.5 45.2 %all-gather.15.cloned.1.call-start = ((), (), s32[]{:S(2)}) async-start(), calls=%async_computation.12 | async-start | bytes 1572864 | tf_op jit(solution)/shard_map/all_gather | solution.py:91
  101.7 77.6 %all-gather.17.cloned.1.call-start = ((), (), s32[]{:S(2)}) async-start(), calls=%async_computation.13 | async-start | bytes 3145728 | tf_op jit(solution)/shard_map/all_gather | solution.py:281
  102.3 11.4 copy-start.139
  102.3 14.9 copy-start.140
  102.3 182.4 %all-gather.19.cloned.1.call-start = ((), (), s32[]{:S(2)}) async-start(), calls=%async_computation.14 | async-start | bytes 12582912 | tf_op jit(solution)/shard_map/all_gather | solution.py:285
  102.9 287.2 %all-gather.21.cloned.1.call-start = ((), (), s32[]{:S(2)}) async-start(), calls=%async_computation.15 | async-start | bytes 12582912 | tf_op jit(solution)/shard_map/all_gather | solution.py:287
  103.5 326.8 %all-gather.25.cloned.1.call-start = ((), (), s32[]{:S(2)}) async-start(), calls=%async_computation.17 | async-start | bytes 1572864 | tf_op jit(solution)/shard_map/all_gather | solution.py:91
  110.0 373.7 %copy-start.127 = (f32[1,1024]{1,0:T(1,128)}, f32[1,1024]{1,0:T(1,128)S(1)}, u32[]{:S(2)}) copy-start(f32[1,1024]{1,0:T(1,128)S(1)} %add.677) | copy-start | bytes 12292
  117.3 444.9 %copy-start.91 = (f32[1,1024]{1,0:T(1,128)}, f32[1,1024]{1,0:T(1,128)S(1)}, u32[]{:S(2)}) copy-start(f32[1,1024]{1,0:T(1,128)S(1)} %add.675) | copy-start | bytes 12292
  121.3 39.1 %copy-start.62 = (pred[256,1024]{1,0:T(8,128)(4,1)}, pred[256,1024]{1,0:T(8,128)(4,1)S(1)}, u32[]{:S(2)}) copy-start(pred[256,1024]{1,0:T(8,128)(4,1)S(1)} %iota_compare_fusion.2) | copy-start | bytes 786436
  121.5 30.0 %copy-start.47 = (bf16[256,1024]{0,1:T(8,128)(2,1)}, bf16[256,1024]{0,1:T(8,128)(2,1)S(1)}, u32[]{:S(2)}) copy-start(bf16[256,1024]{0,1:T(8,128)(2,1)S(1)} %copy.71) | copy-start | bytes 1572868
  181.9 208.2 %copy-start.20 = (f32[256,1024]{1,0:T(8,128)}, f32[256,1024]{1,0:T(8,128)S(1)}, u32[]{:S(2)}) copy-start(f32[256,1024]{1,0:T(8,128)S(1)} %get-tuple-element.87) | copy-start | bytes 3145732
  181.9 110.5 %copy-start.119 = (f32[256]{0:T(256)}, f32[256]{0:T(256)S(1)}, u32[]{:S(2)}) copy-start(f32[256]{0:T(256)S(1)} %broadcast_multiply_fusion.17) | copy-start | bytes 3076
  182.2 110.3 %copy-start.124 = (f32[256]{0:T(256)}, f32[256]{0:T(256)S(1)}, u32[]{:S(2)}) copy-start(f32[256]{0:T(256)S(1)} %add_rsqrt_fusion.4) | copy-start | bytes 3076
  390.2 11.3 copy-start.38
  397.6 3.8 collective-permute-start
  409.3 44.4 %all-gather.23.cloned.1.call-start = ((), (), s32[]{:S(2)}) async-start(), calls=%async_computation.16 | async-start | bytes 1572864 | tf_op jit(solution)/shard_map/all_gather | solution.py:92
  412.0 103.9 %all-gather.27.cloned.1.call-start = ((), (), s32[]{:S(2)}) async-start(), calls=%async_computation.18 | async-start | bytes 1572864 | tf_op jit(solution)/shard_map/all_gather | solution.py:92
  412.3 59.5 %copy-start.64 = (pred[256,1024]{1,0:T(8,128)(4,1)}, pred[256,1024]{1,0:T(8,128)(4,1)S(1)}, u32[]{:S(2)}) copy-start(pred[256,1024]{1,0:T(8,128)(4,1)S(1)} %iota_compare_fusion.1) | copy-start | bytes 786436
  412.5 50.5 %copy-start.41 = (bf16[256,1024]{0,1:T(8,128)(2,1)}, bf16[256,1024]{0,1:T(8,128)(2,1)S(1)}, u32[]{:S(2)}) copy-start(bf16[256,1024]{0,1:T(8,128)(2,1)S(1)} %copy.74) | copy-start | bytes 1572868
  477.5 13.5 slice-start.8
  486.6 3.8 collective-permute-start.1
  495.0 44.3 %all-gather.29.cloned.1.call-start = ((), (), s32[]{:S(2)}) async-start(), calls=%async_computation.19 | async-start | bytes 1572864 | tf_op jit(solution)/shard_map/all_gather | solution.py:91
  497.2 138.6 %reduce-scatter.13.cloned.1.call-start = ((), (), s32[]{:S(2)}) async-start(), calls=%async_computation.21 | async-start | bytes 1572864 | tf_op jit(solution)/shard_map/reduce_scatter | solution.py:235
  561.9 19.7 %copy-start.16 = (f32[256,1024]{1,0:T(8,128)}, f32[256,1024]{1,0:T(8,128)S(1)}, u32[]{:S(2)}) copy-start(f32[256,1024]{1,0:T(8,128)S(1)} %get-tuple-element.95) | copy-start | bytes 3145732
  561.9 19.7 %copy-start.101 = (f32[256]{0:T(256)}, f32[256]{0:T(256)S(1)}, u32[]{:S(2)}) copy-start(f32[256]{0:T(256)S(1)} %broadcast_multiply_fusion.13) | copy-start | bytes 3076
  562.2 19.4 %copy-start.107 = (f32[256]{0:T(256)}, f32[256]{0:T(256)S(1)}, u32[]{:S(2)}) copy-start(f32[256]{0:T(256)S(1)} %add_rsqrt_fusion) | copy-start | bytes 3076
  595.5 13.6 copy-start.29
  610.8 43.1 %reduce-scatter.11.cloned.1.call-start = ((), (), s32[]{:S(2)}) async-start(), calls=%async_computation.20 | async-start | bytes 1572864 | tf_op jit(solution)/shard_map/reduce_scatter | solution.py:232
  610.8 10.9 copy-start.50
  627.5 109.1 %reduce-scatter.17.cloned.1.call-start = ((), (), s32[]{:S(2)}) async-start(), calls=%async_computation.23 | async-start | bytes 1572864 | tf_op jit(solution)/shard_map/reduce_scatter | solution.py:235
  653.9 11.0 copy-start.45
  653.9 19.9 %slice-start.6 = ((s8[8388608]{0:T(1024)(128)(4,1)}), s8[4194304]{0:T(1024)(128)(4,1)S(1)}, s32[]{:S(2)}) async-start(s8[8388608]{0:T(1024)(128)(4,1)} %bitcast.431), calls=%async_computation.37 | async-start | bytes 8388608
  660.5 4.3 collective-permute-start.2
  665.7 11.3 copy-start.57
  711.5 42.7 %reduce-scatter.15.cloned.1.call-start = ((), (), s32[]{:S(2)}) async-start(), calls=%async_computation.22 | async-start | bytes 1572864 | tf_op jit(solution)/shard_map/reduce_scatter | solution.py:232
  711.5 10.3 copy-start.5
  711.6 10.3 copy-start.43
  728.4 25.8 %copy-start.100 = (f32[256]{0:T(256)S(1)}, f32[256]{0:T(256)}, u32[]{:S(2)}) copy-start(f32[256]{0:T(256)} %copy-done.99) | copy-start | bytes 3076
  728.5 25.7 %copy-start.106 = (f32[256]{0:T(256)S(1)}, f32[256]{0:T(256)}, u32[]{:S(2)}) copy-start(f32[256]{0:T(256)} %copy-done.105) | copy-start | bytes 3076
  728.5 131.9 %reduce-scatter.21.cloned.1.call-start = ((), (), s32[]{:S(2)}) async-start(), calls=%async_computation.25 | async-start | bytes 1572864 | tf_op jit(solution)/shard_map/reduce_scatter | solution.py:235
  761.9 4.4 collective-permute-start.3
  768.5 18.5 %copy-start.55 = (bf16[256,1024]{1,0:T(8,128)(2,1)}, bf16[256,1024]{1,0:T(8,128)(2,1)S(1)}, u32[]{:S(2)}) copy-start(bf16[256,1024]{1,0:T(8,128)(2,1)S(1)} %get-tuple-element.64) | copy-start | bytes 1572868
  768.5 11.7 copy-start.21
  768.5 11.7 copy-start.120
  768.5 11.7 copy-start.125
  819.6 43.4 %reduce-scatter.19.cloned.1.call-start = ((), (), s32[]{:S(2)}) async-start(), calls=%async_computation.24 | async-start | bytes 1572864 | tf_op jit(solution)/shard_map/reduce_scatter | solution.py:232
  835.7 118.1 %reduce-scatter.25.cloned.1.call-start = ((), (), s32[]{:S(2)}) async-start(), calls=%async_computation.27 | async-start | bytes 3145728 | tf_op jit(solution)/shard_map/reduce_scatter | solution.py:394
  841.5 135.9 %reduce-scatter.23.cloned.1.call-start = ((), (), s32[]{:S(2)}) async-start(), calls=%async_computation.26 | async-start | bytes 9437184 | tf_op jit(solution)/shard_map/reduce_scatter | solution.py:385
  841.8 14.9 slice-start
  877.0 202.6 %reduce-scatter.27.cloned.1.call-start = ((), (), s32[]{:S(2)}) async-start(), calls=%async_computation.28 | async-start | bytes 12582912 | tf_op jit(solution)/shard_map/reduce_scatter | solution.py:406
  878.2 10.0 copy-start.87
  913.6 12.2 copy-start.58
  913.6 268.1 %reduce-scatter.29.cloned.1.call-start = ((), (), s32[]{:S(2)}) async-start(), calls=%async_computation.29 | async-start | bytes 12582912 | tf_op jit(solution)/shard_map/reduce_scatter | solution.py:412
  914.8 11.0 copy-start.54
  953.4 634.2 %all-reduce.16.cloned.1.call-start = ((), (), s32[]{:S(2)}) async-start(), calls=%async_computation.30 | async-start | bytes 25165824 | tf_op jit(solution)/shard_map/psum | solution.py:422
  1194.1 51.2 %copy-start.25 = (f32[256,1024]{1,0:T(8,128)S(1)}, f32[256,1024]{1,0:T(8,128)}, u32[]{:S(2)}) copy-start(f32[256,1024]{1,0:T(8,128)} %copy-done.23) | copy-start | bytes 3145732
  1200.2 47.0 %copy-start.79 = (bf16[1,256,1024]{2,1,0:T(8,128)(2,1)S(1)}, bf16[1,256,1024]{2,1,0:T(8,128)(2,1)}, u32[]{:S(2)}) copy-start(bf16[1,256,1024]{2,1,0:T(8,128)(2,1)} %get-tuple-element.71) | copy-start | bytes 1572868
  (113 other events, 669.1 us)
Sparse Core Ops, SparseCore 0:
  9.6 82.4 all-gather.10
  99.6 21.5 all-gather.12
  123.4 21.2 all-gather.14
  146.1 33.1 all-gather.16
  180.7 103.9 all-gather.18
  286.1 103.9 all-gather.20
  409.4 20.7 all-gather.24
  432.4 21.2 all-gather.22
  495.1 20.7 all-gather.26
  517.9 21.2 all-gather.28
  610.9 20.3 reduce-scatter.12
  633.4 20.3 reduce-scatter.10
  711.6 20.0 reduce-scatter.16
  733.8 20.3 reduce-scatter.14
  819.7 20.1 reduce-scatter.20
  842.7 20.3 reduce-scatter.18
  865.7 31.8 reduce-scatter.24
  900.4 77.0 reduce-scatter.22
  980.3 99.2 reduce-scatter.26
  1082.4 99.2 reduce-scatter.28
  1186.4 401.1 all-reduce.15
where the time goes:
time: 1620 us; the launch traced here: 1610 us
  waiting for transfers between devices  990 us (61%)
  matrix products  348 us (21%)
  other arithmetic  93.3 us (6%)
  local copies, waits for them, and re-layouts  79.2 us (5%)
  blocking collectives  70.4 us (4%)
  between operations  18.3 us (1%)
    psum x1, waiting for transfers between devices, shards(): lax.psum(owned[2].astype(jnp.bfloat16), 'replica').astype(jnp.float32)  339 us
    dot_general x12, matrix products, rows_product(): lax.dot_general(left, right, ROWS_CONTRACT, preferred_element_type=jnp.fl...  108 us
    all_gather x1, waiting for transfers between devices, shards(): lax.all_gather(fc_weight, 'shard', axis=1, tiled=True)  102 us
    reduce_scatter x1, waiting for transfers between devices, shards(): lax.psum_scatter(mlp_sums[2].astype(jnp.bfloat16), 'shard', scatter_dimen...  102 us
    reduce_scatter x1, waiting for transfers between devices, shards(): lax.psum_scatter(mlp_sums[4].astype(jnp.bfloat16), 'shard', scatter_dimen...  102 us
    all_gather x1, waiting for transfers between devices, shards(): lax.all_gather(proj_weight, 'shard', axis=1, tiled=True)  97.7 us
    all_gather x1, waiting for transfers between devices, shards(): lax.all_gather(qkv_weight, 'shard', axis=1, tiled=True)  67.5 us
    dot_general x12, matrix products, cols_product(): lax.dot_general(left, right, COLS_CONTRACT, preferred_element_type=jnp.fl...  65.5 us
  transfers between devices with their start and end apart: 25, of which 20 were waited for; matrix products, arithmetic and copies ran while one was open for 15% of the time, Pallas kernels for 0%

commit v1 on v0

v1 whole, which is shorter than its diff:
```python
import functools

import jax
import jax.numpy as jnp
from jax import lax
from jax.experimental import pallas as pl
from jax.experimental.pallas import tpu as pltpu
from jax.sharding import PartitionSpec as P

HEAD_DIM = 64
EPSILON = 1e-05
GELU_SCALE = 0.7978845608028654
GELU_CUBIC = 0.044715
ROWS_CONTRACT = (((0,), (0,)), ((), ()))
COLS_CONTRACT = (((1,), (1,)), ((), ()))
BF = jnp.bfloat16
F32 = jnp.float32
MESH = pl.DeviceIdType.MESH
QTILE = 256
VMEM_LIMIT = 56 * 1024 * 1024

CROSS_SAME = [(1, 0), (2, 3)]
CROSS_SWAP = [(1, 2), (2, 1)]
CORE_OUT = [(0, 2), (3, 1)]
CORE_IN = [(1, 3), (2, 0)]
CROSS_BACK = [(0, 1), (3, 2)]
PAIR = ("section", "shard")


def rows_product(left, right):
    return lax.dot_general(left, right, ROWS_CONTRACT, preferred_element_type=F32)


def cols_product(left, right):
    return lax.dot_general(left, right, COLS_CONTRACT, preferred_element_type=F32)


def core_swap(value):
    return lax.ppermute(value, "section", [(0, 1), (1, 0)])


def replica_swap(value):
    size = lax.axis_size("replica")
    return lax.ppermute(value, "replica", [(i, i ^ 1) for i in range(size)])


def ordered(flag, first, second, axis):
    return jnp.concatenate(
        [jnp.where(flag, first, second), jnp.where(flag, second, first)], axis=axis
    )


def norm_parts(inputs):
    mean = jnp.mean(inputs, axis=-1, keepdims=True)
    centered = inputs - mean
    inverse = lax.rsqrt(jnp.mean(centered * centered, axis=-1, keepdims=True) + EPSILON)
    return centered * inverse, inverse


def norm_backward(d_normed, scaled, inverse, gain):
    d_scaled = d_normed * gain
    return inverse * (
        d_scaled
        - jnp.mean(d_scaled, axis=-1, keepdims=True)
        - scaled * jnp.mean(d_scaled * scaled, axis=-1, keepdims=True)
    )


def gelu_pair(pre):
    tangent = jnp.tanh(GELU_SCALE * (pre + GELU_CUBIC * pre * pre * pre))
    value = 0.5 * pre * (1.0 + tangent)
    slope = 0.5 * (1.0 + tangent) + 0.5 * pre * (1.0 - tangent * tangent) * GELU_SCALE * (
        1.0 + 3.0 * GELU_CUBIC * pre * pre
    )
    return value, slope


def head_parts(pair):
    low = lax.broadcasted_iota(jnp.int32, pair.shape, 1) < HEAD_DIM
    zero = jnp.zeros_like(pair)
    return jnp.where(low, pair, zero), jnp.where(low, zero, pair)


def masked_scores(keys, query, length):
    scores = cols_product(keys, query)
    tail = scores[length - QTILE :]
    key_pos = lax.broadcasted_iota(jnp.int32, tail.shape, 0)
    query_pos = lax.broadcasted_iota(jnp.int32, tail.shape, 1)
    tail = jnp.where(key_pos <= query_pos, tail, -1e30)
    if length == QTILE:
        return tail
    return jnp.concatenate([scores[: length - QTILE], tail], axis=0)


def attend_kernel(block_ref, q_ref, k_ref, v_ref, out_ref, lse_ref):
    block = block_ref[0]
    rows = q_ref.shape[0]
    for index in range(k_ref.shape[0] // rows):

        @pl.when(block == index)
        def _(index=index):
            for tile in range(rows // QTILE):
                span = pl.ds(tile * QTILE, QTILE)
                length = index * rows + (tile + 1) * QTILE
                keys = k_ref[:length, :]
                values = v_ref[:length, :]
                mixed = []
                for head, part in enumerate(head_parts(q_ref[span, :])):
                    scores = masked_scores(keys, part * BF(HEAD_DIM**-0.5), length)
                    top = jnp.max(scores, axis=0, keepdims=True)
                    probs = jnp.exp(scores - top)
                    total = jnp.sum(probs, axis=0, keepdims=True)
                    lse_ref[0, pl.ds(head, 1), span] = top + jnp.log(total)
                    piece = rows_product(values, probs.astype(BF))
                    piece = piece[head * HEAD_DIM : (head + 1) * HEAD_DIM]
                    mixed.append(piece * (1.0 / total))
                mixed = jnp.concatenate(mixed, axis=0)
                out_ref[span, :] = jnp.transpose(mixed).astype(BF)


def attend(block, query, keys, values):
    rows, width = query.shape
    pairs = width // 128
    total = keys.shape[0]
    return pl.pallas_call(
        attend_kernel,
        grid_spec=pltpu.PrefetchScalarGridSpec(
            num_scalar_prefetch=1,
            grid=(pairs,),
            in_specs=[
                pl.BlockSpec((rows, 128), lambda i, b: (0, i)),
                pl.BlockSpec((total, 128), lambda i, b: (0, i)),
                pl.BlockSpec((total, 128), lambda i, b: (0, i)),
            ],
            out_specs=[
                pl.BlockSpec((rows, 128), lambda i, b: (0, i)),
                pl.BlockSpec((1, 8, rows), lambda i, b: (i, 0, 0)),
            ],
        ),
        out_shape=[
            jax.ShapeDtypeStruct((rows, width), BF),
            jax.ShapeDtypeStruct((pairs, 8, rows), F32),
        ],
        compiler_params=pltpu.CompilerParams(vmem_limit_bytes=VMEM_LIMIT),
        cost_estimate=pl.CostEstimate(
            flops=4 * rows * total * width, bytes_accessed=4 * total * width, transcendentals=0
        ),
        name="attend",
    )(block, query, keys, values)


def attend_back_kernel(
    block_ref,
    q_ref,
    k_ref,
    v_ref,
    o_ref,
    do_ref,
    lse_ref,
    pend_k_ref,
    pend_v_ref,
    dq_ref,
    dk_ref,
    dv_ref,
    new_k_ref,
    new_v_ref,
    sum_k,
    sum_v,
):
    block = block_ref[0]
    rows = q_ref.shape[0]
    scale = HEAD_DIM**-0.5
    for index in range(k_ref.shape[0] // rows):

        @pl.when(block == index)
        def _(index=index):
            end = (index + 1) * rows
            if index == 0:
                sum_k[:rows, :] = pend_k_ref[...]
                sum_v[:rows, :] = pend_v_ref[...]
            else:
                sum_k[:end, :] = jnp.zeros((end, 128), F32)
                sum_v[:end, :] = jnp.zeros((end, 128), F32)
            for tile in range(rows // QTILE):
                span = pl.ds(tile * QTILE, QTILE)
                length = index * rows + (tile + 1) * QTILE
                keys = k_ref[:length, :]
                values = v_ref[:length, :]
                grads = do_ref[span, :]
                products = jnp.transpose(grads.astype(F32) * o_ref[span, :].astype(F32))
                queries = head_parts(q_ref[span, :])
                grads = head_parts(grads)
                d_query = []
                d_keys = d_values = None
                for head in range(2):
                    take = slice(head * HEAD_DIM, (head + 1) * HEAD_DIM)
                    query = queries[head] * BF(scale)
                    scores = masked_scores(keys, query, length)
                    weights = jnp.exp(scores - lse_ref[0, pl.ds(head, 1), span])
                    d_probs = cols_product(values, grads[head])
                    delta = jnp.sum(products[take], axis=0, keepdims=True)
                    d_scores = (weights * (d_probs - delta)).astype(BF)
                    d_value = jnp.dot(weights.astype(BF), grads[head], preferred_element_type=F32)
                    d_key = jnp.dot(d_scores, query, preferred_element_type=F32)
                    d_values = d_value if head == 0 else d_values + d_value
                    d_keys = d_key if head == 0 else d_keys + d_key
                    d_query.append(rows_product(keys, d_scores)[take])
                sum_k[:length, :] += d_keys
                sum_v[:length, :] += d_values
                d_query = jnp.concatenate(d_query, axis=0) * scale
                dq_ref[span, :] = jnp.transpose(d_query).astype(BF)
            dk_ref[...] = sum_k[index * rows : end, :].astype(BF)
            dv_ref[...] = sum_v[index * rows : end, :].astype(BF)
            if index == 0:
                new_k_ref[...] = pend_k_ref[...]
                new_v_ref[...] = pend_v_ref[...]
            else:
                new_k_ref[...] = sum_k[:rows, :]
                new_v_ref[...] = sum_v[:rows, :]


def attend_back(block, query, keys, values, mixed, d_mixed, lse, pending):
    rows, width = query.shape
    pairs = width // 128
    total = keys.shape[0]
    assert total == 2 * rows
    small = pl.BlockSpec((rows, 128), lambda i, b: (0, i))
    large = pl.BlockSpec((total, 128), lambda i, b: (0, i))
    low = jax.ShapeDtypeStruct((rows, width), BF)
    wide = jax.ShapeDtypeStruct((rows, width), F32)
    return pl.pallas_call(
        attend_back_kernel,
        grid_spec=pltpu.PrefetchScalarGridSpec(
            num_scalar_prefetch=1,
            grid=(pairs,),
            in_specs=[
                small,
                large,
                large,
                small,
                small,
                pl.BlockSpec((1, 8, rows), lambda i, b: (i, 0, 0)),
                small,
                small,
            ],
            out_specs=[small] * 5,
            scratch_shapes=[pltpu.VMEM((total, 128), F32), pltpu.VMEM((total, 128), F32)],
        ),
        out_shape=[low, low, low, wide, wide],
        compiler_params=pltpu.CompilerParams(vmem_limit_bytes=VMEM_LIMIT),
        cost_estimate=pl.CostEstimate(
            flops=10 * rows * total * width, bytes_accessed=8 * total * width, transcendentals=0
        ),
        name="attend_back",
    )(block, query, keys, values, mixed, d_mixed, lse, *pending)


def ring_place(size):
    index = lax.axis_index("replica")
    odd = index % 2
    half = index // 2
    place = (1 - odd) * half + odd * (size - 1 - half)

    def device(spot):
        upper = spot // (size // 2)
        return (1 - upper) * (2 * spot) + upper * (2 * (size - 1 - spot) + 1)

    return place, device((place + 1) % size), device((place + size - 1) % size)


def ring_barrier(following, previous):
    barrier = pltpu.get_barrier_semaphore()
    for neighbour in (following, previous):
        pl.semaphore_signal(barrier, inc=1, device_id={"replica": neighbour}, device_id_type=MESH)
    pl.semaphore_wait(barrier, 2)


def scatter_kernel(size, count, *refs):
    own, out, landed = refs[:count], refs[count : 2 * count], refs[2 * count : 3 * count]
    send_sem, recv_sem = refs[3 * count :]
    place, following, previous = ring_place(size)
    targets = (following, previous)
    ring_barrier(following, previous)

    def send(way, item, source, slot):
        return pltpu.make_async_remote_copy(
            src_ref=source,
            dst_ref=landed[item].at[way, slot],
            send_sem=send_sem.at[way, item, slot],
            recv_sem=recv_sem.at[way, item, slot],
            device_id={"replica": targets[way]},
            device_id_type=MESH,
        )

    def chunk_of(way, slot):
        if way == 0:
            return (place + 2 * size - 2 - slot) % size
        return (place + 2 + slot) % size

    for item in range(count):
        send(0, item, own[item].at[0, (place + size - 1) % size], 0).start()
        send(1, item, own[item].at[1, (place + 1) % size], 0).start()

    def step(slot, carry):
        for item in range(count):
            for way in range(2):
                here = landed[item].at[way, slot]
                send(way, item, here, slot).wait_recv()
                here[...] += own[item][way, chunk_of(way, slot)]
                send(way, item, here, slot + 1).start()
        return carry

    lax.fori_loop(0, size - 2, step, 0)
    last = size - 2
    for item in range(count):
        for way in range(2):
            here = landed[item].at[way, last]
            send(way, item, here, last).wait_recv()
            out[item][way] = here[...] + own[item][way, place]

    def finish(slot, carry):
        for item in range(count):
            for way in range(2):
                send(way, item, landed[item].at[way, slot], slot).wait_send()
        return carry

    lax.fori_loop(0, size - 1, finish, 0)


def ring_scatter(pieces):
    size = pieces[0].shape[1]
    count = len(pieces)
    whole = pl.BlockSpec(memory_space=pltpu.VMEM)
    return pl.pallas_call(
        functools.partial(scatter_kernel, size, count),
        out_shape=[jax.ShapeDtypeStruct((2,) + item.shape[2:], BF) for item in pieces],
        in_specs=[whole] * count,
        out_specs=[whole] * count,
        scratch_shapes=[pltpu.VMEM((2, size - 1) + item.shape[2:], BF) for item in pieces]
        + [pltpu.SemaphoreType.DMA((2, count, size - 1))] * 2,
        compiler_params=pltpu.CompilerParams(
            collective_id=0, has_side_effects=True, vmem_limit_bytes=VMEM_LIMIT
        ),
        name="ring_scatter",
    )(*pieces)


def gather_kernel(size, count, *refs):
    own, out = refs[:count], refs[count : 2 * count]
    send_sem, recv_sem, local_sem = refs[2 * count :]
    place, following, previous = ring_place(size)
    targets = (following, previous)
    ring_barrier(following, previous)

    def send(way, item, source, chunk, slot):
        return pltpu.make_async_remote_copy(
            src_ref=source,
            dst_ref=out[item].at[way, chunk],
            send_sem=send_sem.at[way, item, slot],
            recv_sem=recv_sem.at[way, item, slot],
            device_id={"replica": targets[way]},
            device_id_type=MESH,
        )

    def chunk_of(way, slot):
        if way == 0:
            return (place + size - 1 - slot) % size
        return (place + 1 + slot) % size

    keep = []
    for item in range(count):
        for way in range(2):
            send(way, item, own[item].at[way], place, 0).start()
            copy = pltpu.make_async_copy(
                own[item].at[way], out[item].at[way, place], local_sem.at[way, item]
            )
            copy.start()
            keep.append(copy)

    def step(slot, carry):
        for item in range(count):
            for way in range(2):
                chunk = chunk_of(way, slot)
                here = out[item].at[way, chunk]
                send(way, item, here, chunk, slot).wait_recv()
                send(way, item, here, chunk, slot + 1).start()
        return carry

    lax.fori_loop(0, size - 2, step, 0)
    last = size - 2
    for item in range(count):
        for way in range(2):
            chunk = chunk_of(way, last)
            send(way, item, out[item].at[way, chunk], chunk, last).wait_recv()
    for copy in keep:
        copy.wait()

    def finish(slot, carry):
        for item in range(count):
            for way in range(2):
                send(way, item, own[item].at[way], place, slot).wait_send()
        return carry

    lax.fori_loop(0, size - 1, finish, 0)


def ring_gather(pieces, size):
    count = len(pieces)
    spot = pl.BlockSpec(memory_space=pl.ANY)
    return pl.pallas_call(
        functools.partial(gather_kernel, size, count),
        out_shape=[
            jax.ShapeDtypeStruct((2, size) + item.shape[1:], BF) for item in pieces
        ],
        in_specs=[spot] * count,
        out_specs=[spot] * count,
        scratch_shapes=[pltpu.SemaphoreType.DMA((2, count, size - 1))] * 2
        + [pltpu.SemaphoreType.DMA((2, count))],
        compiler_params=pltpu.CompilerParams(collective_id=1, has_side_effects=True),
        name="ring_gather",
    )(*pieces)


def shards(
    tokens,
    cotangent,
    attn_gain,
    attn_shift,
    qkv_weight,
    query_bias,
    value_bias,
    out_weight,
    out_bias,
    mlp_gain,
    mlp_shift,
    fc_weight,
    fc_bias,
    proj_weight,
    proj_bias,
):
    core = lax.axis_index("section")
    layer = lax.axis_index("shard")
    size = lax.axis_size("replica")
    parity = lax.axis_index("replica") % 2
    own = core == layer
    first = layer == 0
    left = core == 0
    micro, part, width = tokens.shape[1:]
    assert micro == 2
    rows = 2 * part
    half = width // 2
    hidden_half = fc_weight.shape[2] // 2

    def pair_permute(value, pairs):
        return lax.ppermute(value, PAIR, pairs)

    small = jnp.concatenate(
        [
            item[0]
            for item in (
                attn_gain,
                attn_shift,
                out_bias,
                mlp_gain,
                mlp_shift,
                proj_bias,
                query_bias,
                value_bias,
                fc_bias,
            )
        ]
    ).reshape(-1, 128)
    small = jnp.where(own, small, pair_permute(small, CROSS_SWAP))
    small_other = core_swap(small[: 6 * half // 128])
    full_small = jnp.concatenate(
        [
            jnp.where(left, small[: 6 * half // 128], small_other).reshape(6, half),
            jnp.where(left, small_other, small[: 6 * half // 128]).reshape(6, half),
        ],
        axis=1,
    ).astype(F32)
    gain1, shift1, bias_o, gain2, shift2, bias_p = (full_small[i] for i in range(6))
    flat = small.reshape(-1).astype(F32)
    bias_q = flat[6 * half : 7 * half]
    bias_v = flat[7 * half : 8 * half]
    bias_f = flat[8 * half :]

    def fetch(index):
        mine = jnp.where(first, tokens[0, index], cotangent[0, index])
        give = jnp.where(first, cotangent[0, index], tokens[0, index])
        give = lax.dynamic_slice_in_dim(give, core * (part // 2), part // 2, 0)
        got = lax.ppermute(give, "shard", [(0, 1), (1, 0)])
        other = ordered(left, got, core_swap(got), 0)
        return ordered(first, mine, other, 0)

    outer = [fetch(0)]

    def crossed(value, axis, pairs):
        length = value.shape[axis] // 2
        piece = lax.dynamic_slice_in_dim(value, parity * length, length, axis)
        pieces = [pair_permute(piece, each) for each in pairs]
        got = pieces[0] if len(pieces) == 1 else jnp.where(own, pieces[0], pieces[1])
        return ordered(parity == 0, got, replica_swap(got), axis)

    def column_halves(weight, groups):
        depth = weight.shape[0]
        parts = weight.reshape(depth, groups, 2, -1)
        mine = jnp.where(left, parts[:, :, 0], parts[:, :, 1]).reshape(depth, -1)
        other = jnp.where(left, parts[:, :, 1], parts[:, :, 0]).reshape(depth, -1)
        return mine, other

    def fetch_columns(weight, groups):
        mine, other = column_halves(weight, groups)
        sibling = pair_permute(other, CORE_OUT)
        length = mine.shape[0] // 2
        piece_mine = lax.dynamic_slice_in_dim(mine, parity * length, length, 0)
        piece_other = lax.dynamic_slice_in_dim(other, parity * length, length, 0)
        got = jnp.where(
            own, pair_permute(piece_mine, CROSS_SAME), pair_permute(piece_other, CROSS_SWAP)
        )
        far = ordered(parity == 0, got, replica_swap(got), 0)
        near = jnp.where(own, mine, sibling)
        return ordered(first, near, far, 0)

    def fetch_rows(weight):
        length = weight.shape[0] // 2
        piece = lax.dynamic_slice_in_dim(weight, parity * length, length, 0)
        got = pair_permute(piece, CROSS_SWAP)
        far = ordered(parity == 0, got, replica_swap(got), 0)
        return jnp.where(own, weight, far)

    w_qkv = fetch_columns(qkv_weight[0], 3)
    w_out = fetch_rows(out_weight[0])
    w_fc = fetch_columns(fc_weight[0], 1)
    w_proj = fetch_rows(proj_weight[0])
    outer.append(fetch(1))

    def exchanged(partial):
        return partial + core_swap(partial.astype(BF)).astype(F32)

    def passed(value, pairs):
        give = lax.dynamic_slice_in_dim(value, core * part, part, 0)
        got = lax.ppermute(give, "shard", pairs)
        return ordered(left, got, core_swap(got), 0)

    keys_all = jnp.zeros((micro * rows, half), BF)
    values_all = jnp.zeros((micro * rows, half), BF)
    received = [jnp.zeros((rows, width), BF)]
    kept_list, outputs = [], []
    for step in range(micro + 1):
        index = jnp.where(first, min(step, micro - 1), max(step - 1, 0)).astype(jnp.int32)
        inputs = jnp.where(first, outer[min(step, micro - 1)], received[step])
        scaled1, inverse1 = norm_parts(inputs.astype(F32))
        normed1 = (scaled1 * gain1 + shift1).astype(BF)
        qkv = jnp.dot(normed1, w_qkv, preferred_element_type=F32)
        query = (qkv[:, :half] + bias_q).astype(BF)
        keys = qkv[:, half : 2 * half].astype(BF)
        values = (qkv[:, 2 * half :] + bias_v).astype(BF)
        keys_all = lax.dynamic_update_slice_in_dim(keys_all, keys, index * rows, 0)
        values_all = lax.dynamic_update_slice_in_dim(values_all, values, index * rows, 0)
        mixed, lse = attend(index[None], query, keys_all, values_all)
        partial = jnp.dot(mixed, w_out, preferred_element_type=F32)
        hidden = inputs.astype(F32) + exchanged(partial) + bias_o
        scaled2, inverse2 = norm_parts(hidden)
        normed2 = (scaled2 * gain2 + shift2).astype(BF)
        pre = jnp.dot(normed2, w_fc, preferred_element_type=F32) + bias_f
        activated, slope = gelu_pair(pre)
        act = activated.astype(BF)
        partial = jnp.dot(act, w_proj, preferred_element_type=F32)
        output = (hidden + exchanged(partial) + bias_p).astype(BF)
        outputs.append(output)
        kept_list.append(
            (inputs, normed1, query, lse, mixed, scaled2.astype(BF), inverse2, normed2,
             slope.astype(BF), act)
        )
        if step < micro:
            received.append(passed(output, [(0, 1)]))

    pending = (jnp.zeros((rows, half), F32), jnp.zeros((rows, half), F32))
    grad_received = [jnp.zeros((rows, width), BF)]
    terms_list, results, sums = [], [], None
    for step in range(micro + 1):
        index = jnp.where(first, min(micro - step, micro - 1), max(micro - 1 - step, 0)).astype(
            jnp.int32
        )
        active = jnp.where(first, 1.0 if step >= 1 else 0.0, 1.0 if step < micro else 0.0)
        grad = jnp.where(first, grad_received[step], outer[max(micro - 1 - step, 0)])
        inputs, normed1, query, lse, mixed, scaled2, inverse2, normed2, slope, act = kept_list[
            micro - step
        ]
        d_pre = (cols_product(grad, w_proj) * slope.astype(F32)).astype(BF)
        d_normed2 = exchanged(cols_product(d_pre, w_fc))
        scaled2 = scaled2.astype(F32)
        d_hidden = grad.astype(F32) + norm_backward(d_normed2, scaled2, inverse2, gain2)
        d_branch = d_hidden.astype(BF)
        d_mixed = cols_product(d_branch, w_out).astype(BF)
        d_query, d_keys, d_values, *pending = attend_back(
            index[None], query, keys_all, values_all, mixed, d_mixed, lse, pending
        )
        d_qkv = jnp.concatenate([d_query, d_keys, d_values], axis=1)
        d_normed1 = exchanged(cols_product(d_qkv, w_qkv))
        scaled1, inverse1 = norm_parts(inputs.astype(F32))
        d_inputs = d_hidden + norm_backward(d_normed1, scaled1, inverse1, gain1)
        result = d_inputs.astype(BF)
        results.append(result)
        if step < micro:
            grad_received.append(passed(result, [(1, 0)]))
        full = jnp.stack(
            [
                jnp.sum(d_normed1 * scaled1, axis=0),
                jnp.sum(d_normed1, axis=0),
                jnp.sum(d_branch.astype(F32), axis=0),
                jnp.sum(d_normed2 * scaled2, axis=0),
                jnp.sum(d_normed2, axis=0),
                jnp.sum(grad.astype(F32), axis=0),
            ]
        )
        full = lax.dynamic_slice_in_dim(full, core * half, half, 1)
        vector = jnp.concatenate(
            [
                full.reshape(-1),
                jnp.sum(d_query.astype(F32), axis=0),
                jnp.sum(d_values.astype(F32), axis=0),
                jnp.sum(d_pre.astype(F32), axis=0),
            ]
        )
        sums = active * vector if sums is None else sums + active * vector
        terms_list.append((normed1, d_qkv, mixed, d_branch, normed2, d_pre, act, grad))

    late = [jnp.where(first, a, b) for a, b in zip(terms_list[2], terms_list[0])]
    both = [jnp.concatenate([a, b], axis=0) for a, b in zip(terms_list[1], late)]
    chunk = half // size
    wide = hidden_half // size
    pieces = [
        rows_product(both[0], both[1]).astype(BF).reshape(2, size, chunk, 3 * half),
        rows_product(both[4], both[5]).astype(BF).reshape(2, size, chunk, hidden_half),
        rows_product(both[2], both[3]).astype(BF).reshape(size, 2, chunk // 2, width),
        rows_product(both[6], both[7]).astype(BF).reshape(size, 2, wide // 2, width),
    ]
    pieces[2] = jnp.swapaxes(pieces[2], 0, 1)
    pieces[3] = jnp.swapaxes(pieces[3], 0, 1)
    g_qkv, g_fc, g_out, g_proj = ring_scatter(pieces)

    def return_columns(piece, groups):
        near = jnp.where(first, piece[0], piece[1])
        far = jnp.where(first, piece[1], piece[0])
        near_core = pair_permute(near, CORE_IN)
        far_same = pair_permute(far, CROSS_BACK)
        far_swap = pair_permute(far, CROSS_SWAP)
        mine = jnp.where(own, near, far_same).reshape(chunk, groups, 1, -1)
        other = jnp.where(own, near_core, far_swap).reshape(chunk, groups, 1, -1)
        return ordered(left, mine, other, 2).reshape(2, chunk // 2, -1)

    def return_rows(piece):
        return jnp.where(own, piece, pair_permute(piece, CROSS_SWAP))

    owned = [
        return_columns(g_qkv, 3),
        return_columns(g_fc, 1),
        return_rows(g_out),
        return_rows(g_proj),
    ]
    gathered = ring_gather(owned, size)

    def finished(item):
        full = jnp.swapaxes(item, 0, 1).astype(F32)
        return full.reshape(1, -1, item.shape[-1])

    qkv_grad, fc_grad, out_grad, proj_grad = (finished(item) for item in gathered)

    sums = lax.all_gather(sums.astype(BF).reshape(-1, 128), "replica", axis=0)
    sums = jnp.sum(sums.astype(F32), axis=0)
    sums = jnp.where(own, sums, pair_permute(sums, CROSS_SWAP)).reshape(-1)
    vectors = [sums[i * half : (i + 1) * half][None] for i in range(8)] + [sums[8 * half :][None]]

    def placed(mine, arrived, pairs, far):
        near = lax.dynamic_slice_in_dim(mine, layer * part, part, 0)
        give = lax.dynamic_slice_in_dim(mine, (1 - layer) * part, part, 0)
        sent = pair_permute(give, pairs)
        piped = lax.dynamic_slice_in_dim(arrived, layer * part, part, 0)
        return jnp.where(own, near, jnp.where(far, piped, sent))

    activations = jnp.stack(
        [
            placed(
                jnp.where(first, outputs[i], outputs[i + 1]),
                received[i + 1],
                [(3, 2)],
                layer == 1,
            )
            for i in range(micro)
        ]
    )[None, None]
    input_grads = jnp.stack(
        [
            placed(
                jnp.where(first, results[micro - i], results[micro - 1 - i]),
                grad_received[micro - i],
                [(0, 1)],
                layer == 0,
            )
            for i in range(micro)
        ]
    )[None, None]
    return (
        activations,
        input_grads,
        vectors[0],
        vectors[1],
        qkv_grad,
        vectors[6],
        vectors[7],
        out_grad,
        vectors[2],
        vectors[3],
        vectors[4],
        fc_grad,
        vectors[8],
        proj_grad,
        vectors[5],
    )


def solution(mesh):
    block = P("replica", None, "shard", None)
    layers = P("section", "replica", None, "shard", None)
    vector = P("section", "shard")
    matrix = P("section", "shard", None)
    kinds = (
        vector,
        vector,
        matrix,
        vector,
        vector,
        matrix,
        vector,
        vector,
        vector,
        matrix,
        vector,
        matrix,
        vector,
    )
    return jax.shard_map(
        shards,
        mesh=mesh,
        in_specs=(block, block) + kinds,
        out_specs=(layers, layers) + kinds,
        check_vma=False,
    )
```

time: 1620 us -> 876 us (0.54)
  waiting for transfers between devices: 990 us -> 154 us
  Pallas kernels: 0 us -> 311 us
  matrix products: 348 us -> 94.5 us
  starting transfers between devices: 11.3 us -> 85.1 us
  blocking collectives: 70.4 us -> 24.2 us
  local copies, waits for them, and re-layouts: 79.2 us -> 98.3 us
    all_gather x10 -> x0, waiting for transfers between devices: 375 us -> none  [the longest x1 102 us: shards(): lax.all_gather(fc_weight, 'shard', axis=1, tiled=True)]
    psum x1 -> x0, waiting for transfers between devices: 339 us -> none  [shards(): lax.psum(owned[2].astype(jnp.bfloat16), 'replica').astype(jnp.float32)]
    pallas_call x0 -> x8, Pallas kernels: none -> 311 us  [the longest x1 128 us: ring_scatter(): pl.pallas_call(functools.partial(scatter_kernel, size, count), out_shape=...]
    reduce_scatter x10 -> x0, waiting for transfers between devices: 266 us -> none  [the longest x1 102 us: shards(): lax.psum_scatter(mlp_sums[2].astype(jnp.bfloat16), 'shard', scatter_dimen...]
    dot_general x56 -> x28, matrix products: 348 us -> 94.5 us  [the longest x12 41.2 us: cols_product(): lax.dot_general(left, right, COLS_CONTRACT, preferred_element_type=F32)]
    ppermute x4 -> x51, waiting for transfers between devices: 6.88 us -> 154 us  [the longest x4 61.9 us: replica_swap(): return lax.ppermute(value, 'replica', [(i, i ^ 1) for i in range(size)])]
    ppermute x4 -> x51, starting transfers between devices: 9.48 us -> 85.1 us  [the longest x22 57.8 us: pair_permute(): return lax.ppermute(value, PAIR, pairs)]
    select_n x0 -> x36, other arithmetic: none -> 46.1 us  [the longest x15 19 us: ordered(): jnp.where(flag, first, second)]
  transfers between devices with their start and end apart: 25 -> 51, of which waited for: 20 -> 23; matrix products, arithmetic and copies ran while one was open for 15% -> 17% of each run, Pallas kernels for 0% -> 16%
where the time goes in v1:
time: 876 us; the launch traced here: 867 us
  Pallas kernels  311 us (36%)
  waiting for transfers between devices  154 us (18%)
  local copies, waits for them, and re-layouts  98.3 us (11%)
  other arithmetic  95.9 us (11%)
  matrix products  94.5 us (11%)
  starting transfers between devices  85.1 us (10%)
  blocking collectives  24.2 us (3%)
    pallas_call x1, Pallas kernels, ring_scatter(): pl.pallas_call(functools.partial(scatter_kernel, size, count), out_shape=...  128 us
    pallas_call x1, Pallas kernels, ring_gather(): pl.pallas_call(functools.partial(gather_kernel, size, count), out_shape=[...  117 us
    ppermute x4, waiting for transfers between devices, replica_swap(): return lax.ppermute(value, 'replica', [(i, i ^ 1) for i in range(size)])  61.9 us
    ppermute x22, starting transfers between devices, pair_permute(): return lax.ppermute(value, PAIR, pairs)  57.8 us
    unnamed x322, local copies, waits for them, and re-layouts  49 us
    ppermute x4, waiting for transfers between devices, passed(): got = lax.ppermute(give, 'shard', pairs)  43.8 us
    dot_general x12, matrix products, cols_product(): lax.dot_general(left, right, COLS_CONTRACT, preferred_element_type=F32)  41.2 us
    pallas_call x3, Pallas kernels, attend_back(): pl.pallas_call(attend_back_kernel, grid_spec=pltpu.PrefetchScalarGridSpec...  33.5 us
  transfers between devices with their start and end apart: 51, of which 23 were waited for; matrix products, arithmetic and copies ran while one was open for 17% of the time, Pallas kernels for 16%

profile of v1, /device:TPU:1, one launch (start us, length us, event | category | flops | bytes accessed | tf_op | source)
XLA Modules:
  0.0 866.6 jit_solution(10177070913772068593)
XLA Ops:
  8.7 4.5 collective-permute-start.2
  17.4 3.2 copy.66
  22.4 2.7 copy.67
  28.5 2.5 collective-permute-start.6
  32.8 6.4 copy.71
  39.2 3.8 fusion.195
  43.0 3.9 copy.83
  49.2 3.8 broadcast_select_fusion.2
  56.4 3.2 dynamic-slice_bitcast_fusion
  62.6 3.3 collective-permute-start.5
  67.9 3.2 collective-permute-start.12
  72.1 2.5 collective-permute-start.13
  78.8 3.1 collective-permute-start.8
  81.8 2.5 collective-permute-start.15
  85.6 18.9 %collective-permute-done.8 = bf16[256,1024]{1,0:T(8,128)(2,1)S(1)} collective-permute-done((bf16[256,1024]{1,0:T(8,128)(2,1)S(1)}, bf16[256,1024]{1,0:T(8,128)(2,1)S(1)}, u32[]{:S(2)}, u32[]{:S(2)}) %collective-permute-start.8) | collective-permute-done | bytes 524320 | tf_op jit(solution)/shard_map/ppermute | solution.py:455
  108.1 9.3 %collective-permute-done.9 = bf16[256,1024]{1,0:T(8,128)(2,1)S(1)} collective-permute-done((bf16[256,1024]{1,0:T(8,128)(2,1)S(1)}, bf16[256,1024]{1,0:T(8,128)(2,1)S(1)}, u32[]{:S(2)}, u32[]{:S(2)}) %collective-permute-start.9) | collective-permute-done | bytes 524320 | tf_op jit(solution)/shard_map/ppermute | solution.py:44
  119.2 15.1 %collective-permute-done.7 = bf16[256,1536]{1,0:T(8,128)(2,1)S(1)} collective-permute-done((bf16[256,1536]{1,0:T(8,128)(2,1)S(1)}, bf16[256,1536]{1,0:T(8,128)(2,1)S(1)}, u32[]{:S(2)}, u32[]{:S(2)}) %collective-permute-start.7) | collective-permute-done | bytes 786464 | tf_op jit(solution)/shard_map/ppermute | solution.py:44
  141.8 8.1 attend.3
  151.6 5.0 collective-permute-start.10
  159.3 3.1 broadcast_select_fusion.7
  164.4 2.5 fusion.171
  166.9 37.5 %collective-permute-done.16 = bf16[1024,1024]{1,0:T(8,128)(2,1)S(1)} collective-permute-done((bf16[1024,1024]{1,0:T(8,128)(2,1)}, bf16[1024,1024]{1,0:T(8,128)(2,1)S(1)}, u32[]{:S(2)}, u32[]{:S(2)}) %collective-permute-start.16) | collective-permute-done | bytes 2097184 | tf_op jit(solution)/shard_map/ppermute | solution.py:44
  207.2 2.5 maximum_select_fusion
  209.7 4.5 fusion.200
  215.0 2.6 collective-permute-done.17
  217.6 2.5 add_convert_fusion.4
  221.1 3.4 collective-permute-start.20
  224.4 10.3 %collective-permute-done.20 = bf16[256,1024]{1,0:T(8,128)(2,1)} collective-permute-done((bf16[256,1024]{1,0:T(8,128)(2,1)S(1)}, bf16[256,1024]{1,0:T(8,128)(2,1)}, u32[]{:S(2)}, u32[]{:S(2)}) %collective-permute-start.20) | collective-permute-done | bytes 524320 | tf_op jit(solution)/shard_map/ppermute | solution.py:543
  246.6 12.4 %attend.4 = (bf16[512,512]{1,0:T(8,128)(2,1)}, f32[4,8,512]{2,1,0:T(8,128)}) custom-call(s32[1]{0:T(128)} %bitcast.26.block_ref, bf16[512,512]{1,0:T(8,128)(2,1)} %fusion.120.q_ref, bf16[1024,512]{1,0:T(8,128)(2,1)} %copy-done.113, bf16[1024,512]{1,0:T(8,128)(2,1)} %copy-done.109), custom_call_target="tpu_custom_call" | custom-call | flops 1073741824 | bytes 2097152 | tf_op jit(solution)/shard_map/attend/pallas_call | solution.py:125
  267.1 4.7 multiply_convert_fusion.4
  280.0 11.2 %collective-permute-done.25 = bf16[256,1024]{1,0:T(8,128)(2,1)S(1)} collective-permute-done((bf16[256,1024]{1,0:T(8,128)(2,1)S(1)}, bf16[256,1024]{1,0:T(8,128)(2,1)S(1)}, u32[]{:S(2)}, u32[]{:S(2)}) %collective-permute-start.25) | collective-permute-done | bytes 524320 | tf_op jit(solution)/shard_map/ppermute | solution.py:543
  299.6 12.6 %attend.5 = (bf16[512,512]{1,0:T(8,128)(2,1)}, f32[4,8,512]{2,1,0:T(8,128)}) custom-call(s32[1]{0:T(128)} %constant.95.clone.1.block_ref, bf16[512,512]{1,0:T(8,128)(2,1)} %fusion.118.q_ref, bf16[1024,512]{1,0:T(8,128)(2,1)} %copy-done.115, bf16[1024,512]{1,0:T(8,128)(2,1)} %copy-done.111), custom_call_target="tpu_custom_call" | custom-call | flops 1073741824 | bytes 2097152 | tf_op jit(solution)/shard_map/attend/pallas_call | solution.py:125
  321.0 6.1 broadcast_select_fusion.4
  327.1 6.1 convert_reduce_fusion.2
  343.0 12.4 %attend_back.3 = (bf16[512,512]{1,0:T(8,128)(2,1)}, bf16[512,512]{1,0:T(8,128)(2,1)}, bf16[512,512]{1,0:T(8,128)(2,1)}, f32[512,512]{1,0:T(8,128)}, f32[512,512]{1,0:T(8,128)}) custom-call(s32[1]{0:T(128)} %constant.95.clone.1.block_ref, bf16[512,512]{1,0:T(8,128)(2,1)} %fusion.118.q_ref, bf16[1024,512]{1,0:T(8,128)(2,1)} %copy-done.115, ...), custom_call_target="tpu_custom_call" | custom-call | flops 2684354560 | bytes 4194304 | tf_op jit(solution)/shard_map/attend_back/pallas_call | solution.py:231
  366.9 13.9 %collective-permute-done.32 = bf16[256,1024]{1,0:T(8,128)(2,1)} collective-permute-done((bf16[256,1024]{1,0:T(8,128)(2,1)S(1)}, bf16[256,1024]{1,0:T(8,128)(2,1)}, u32[]{:S(2)}, u32[]{:S(2)}) %collective-permute-start.32) | collective-permute-done | bytes 524320 | tf_op jit(solution)/shard_map/ppermute | solution.py:543
  387.1 7.1 convert_reduce_fusion.1
  394.3 2.4 fusion.207
  398.4 4.5 fusion.204
  407.3 12.7 %attend_back.4 = (bf16[512,512]{1,0:T(8,128)(2,1)}, bf16[512,512]{1,0:T(8,128)(2,1)}, bf16[512,512]{1,0:T(8,128)(2,1)}, f32[512,512]{1,0:T(8,128)}, f32[512,512]{1,0:T(8,128)}) custom-call(s32[1]{0:T(128)} %bitcast.26.block_ref, bf16[512,512]{1,0:T(8,128)(2,1)} %fusion.120.q_ref, bf16[1024,512]{1,0:T(8,128)(2,1)} %copy-done.115, ...), custom_call_target="tpu_custom_call" | custom-call | flops 2684354560 | bytes 4194304 | tf_op jit(solution)/shard_map/attend_back/pallas_call | solution.py:231
  422.5 3.8 fusion.208
  427.7 3.3 broadcast_select_fusion.19
  445.3 8.5 collective-permute-done.36
  458.3 2.8 fusion.137
  465.0 7.3 convert_reduce_fusion
  477.2 5.0 fusion.26
  482.2 2.6 copy.86
  485.9 6.3 fusion.29
  499.1 8.4 attend_back.5
  509.9 3.3 fusion.210
  517.8 2.9 broadcast_select_fusion.20
  520.7 5.3 convolution_convert_fusion
  526.1 128.0 %ring_scatter.1 = (bf16[2,64,1536]{2,1,0:T(8,128)(2,1)}, bf16[2,64,2048]{2,1,0:T(8,128)(2,1)}, bf16[2,32,1024]{2,1,0:T(8,128)(2,1)}, bf16[2,128,1024]{2,1,0:T(8,128)(2,1)}) custom-call(bf16[2,8,64,1536]{3,2,1,0:T(8,128)(2,1)} %bitcast.164, bf16[2,8,64,2048]{3,2,1,0:T(8,128)(2,1)} %bitcast.161, bf16[2,8,32,1024]{3,2,1,0:T(8,128)(2,1)} %bitcast.162, ...), custom_call_target="tpu_custom_call" | custom-call | tf_op jit(solution)/shard_map/ring_scatter/pallas_call | solution.py:334
  655.3 2.6 collective-permute-start.45
  660.9 3.0 collective-permute-start.48
  665.5 24.2 %all_gather.3 = bf16[8,48,128]{2,1,0:T(8,128)(2,1)S(1)} all-gather(bf16[1,48,128]{2,1,0:T(8,128)(2,1)S(1)} %fusion.152), channel_id=1, replica_groups=mesh['section'=2,'shard'=2,'replica'=8] {'replica'}, dimensions={0}, use_global_device_ids=true | all-gather | bytes 110592 | tf_op jit(solution)/shard_map/all_gather | solution.py:671
  689.7 8.9 %collective-permute-start.42 = (f32[48,128]{1,0:T(8,128)S(1)}, f32[48,128]{1,0:T(8,128)S(1)}, u32[]{:S(2)}, u32[]{:S(2)}) collective-permute-start(f32[48,128]{1,0:T(8,128)S(1)} %convert_reduce_fusion.18), channel_id=1, source_target_pairs={{8,16},{16,8},{9,17},{17,9},{10,18},{18,10},{11,19},{19,11},{12,20... | collective-permute-start | bytes 73736 | tf_op jit(solution)/shard_map/ppermute | solution.py:455
  700.1 3.6 collective-permute-start.49
  711.8 3.5 collective-permute-start.50
  721.3 5.2 collective-permute-done.50
  727.4 116.8 %ring_gather.1 = (bf16[2,8,32,3072]{3,2,1,0:T(8,128)(2,1)}, bf16[2,8,32,4096]{3,2,1,0:T(8,128)(2,1)}, bf16[2,8,32,1024]{3,2,1,0:T(8,128)(2,1)}, bf16[2,8,128,1024]{3,2,1,0:T(8,128)(2,1)}) custom-call(bf16[2,32,3072]{2,1,0:T(8,128)(2,1)} %reshape.430.refs_0_, bf16[2,32,4096]{2,1,0:T(8,128)(2,1)} %reshape.431.refs_1_, ...), custom_call_target="tpu_custom_call" | custom-call | tf_op jit(solution)/shard_map/ring_gather/pallas_call | solution.py:410
  849.1 3.5 copy.78
  854.5 4.2 copy.80
  859.7 4.3 copy.81
  (577 shorter events, 216.2 us)
Async XLA Ops:
  8.7 51.7 %collective-permute-start.2 = (bf16[48,128]{1,0:T(8,128)(2,1)S(1)}, bf16[48,128]{1,0:T(8,128)(2,1)S(1)}, u32[]{:S(2)}, u32[]{:S(2)}) collective-permute-start(bf16[48,128]{1,0:T(8,128)(2,1)S(1)} %bitcast.218), channel_id=1, source_target_pairs={{8,16},{16,8},{9,17},{17,9},{10,18},{18,10},{11,19},{19,11},{12,20... | collective-permute-start | bytes 36872 | tf_op jit(solution)/shard_map/ppermute | solution.py:455
  15.8 50.2 %collective-permute-start = (bf16[128,1024]{1,0:T(8,128)(2,1)}, bf16[128,1024]{1,0:T(8,128)(2,1)}, u32[]{:S(2)}, u32[]{:S(2)}) collective-permute-start(bf16[128,1024]{1,0:T(8,128)(2,1)} %fusion.148), channel_id=1, source_target_pairs={{0,8},{8,0},{1,9},{9,1},{2,10},{10,2},{3,11},{11,3},{4,12},{12,4},... | collective-permute-start | bytes 786440 | tf_op jit(solution)/shard_map/ppermute | solution.py:492
  15.8 50.2 %collective-permute-start.18 = (bf16[128,1024]{1,0:T(8,128)(2,1)S(1)}, bf16[128,1024]{1,0:T(8,128)(2,1)}, u32[]{:S(2)}, u32[]{:S(2)}) collective-permute-start(bf16[128,1024]{1,0:T(8,128)(2,1)S(1)} %fusion.147), channel_id=1, source_target_pairs={{0,8},{8,0},{1,9},{9,1},{2,10},{10,2},{3,11},{11,3},{4,12},{12,4},... | collective-permute-start | bytes 786440 | tf_op jit(solution)/shard_map/ppermute | solution.py:492
  25.1 109.3 %collective-permute-start.4 = (bf16[512,1536]{1,0:T(8,128)(2,1)}, bf16[512,1536]{1,0:T(8,128)(2,1)}, u32[]{:S(2)}, u32[]{:S(2)}) collective-permute-start(bf16[512,1536]{1,0:T(8,128)(2,1)} %copy.67), channel_id=1, source_target_pairs={{0,16},{24,8},{1,17},{25,9},{2,18},{26,10},{3,19},{27,11},{4,20},{... | collective-permute-start | bytes 4718600 | tf_op jit(solution)/shard_map/ppermute | solution.py:455
  28.5 49.6 %collective-permute-start.6 = (bf16[256,1536]{1,0:T(8,128)(2,1)}, bf16[256,1536]{1,0:T(8,128)(2,1)}, u32[]{:S(2)}, u32[]{:S(2)}) collective-permute-start(bf16[256,1536]{1,0:T(8,128)(2,1)} %constant_dynamic-slice_fusion.11), channel_id=1, source_target_pairs={{8,16},{16,8},{9,17},{17,9},{10,18},{18,10},{11,19},{19,11},{12,20... | collective-permute-start | bytes 2359304 | tf_op jit(solution)/shard_map/ppermute | solution.py:455
  60.4 2.2 collective-permute-start.3
  62.6 19.2 %collective-permute-start.5 = (bf16[256,1536]{1,0:T(8,128)(2,1)}, bf16[256,1536]{1,0:T(8,128)(2,1)}, u32[]{:S(2)}, u32[]{:S(2)}) collective-permute-start(bf16[256,1536]{1,0:T(8,128)(2,1)} %constant_dynamic-slice_fusion.12), channel_id=1, source_target_pairs={{8,0},{16,24},{9,1},{17,25},{10,2},{18,26},{11,3},{19,27},{12,4},{... | collective-permute-start | bytes 2359304 | tf_op jit(solution)/shard_map/ppermute | solution.py:455
  66.0 1.9 collective-permute-start.1
  66.1 6.0 collective-permute-start.19
  66.6 228.0 %copy-start.125 = (f32[1,1024]{1,0:T(1,128)}, f32[1,1024]{1,0:T(1,128)S(1)}, u32[]{:S(2)}) copy-start(f32[1,1024]{1,0:T(1,128)S(1)} %get-tuple-element.198) | copy-start | bytes 12292
  67.9 38.6 %collective-permute-start.12 = (bf16[256,2048]{1,0:T(8,128)(2,1)}, bf16[256,2048]{1,0:T(8,128)(2,1)S(1)}, u32[]{:S(2)}, u32[]{:S(2)}) collective-permute-start(bf16[256,2048]{1,0:T(8,128)(2,1)} %dynamic-slice_bitcast_fusion.2), channel_id=1, source_target_pairs={{8,0},{16,24},{9,1},{17,25},{10,2},{18,26},{11,3},{19,27},{12,4},{... | collective-permute-start | bytes 3145736 | tf_op jit(solution)/shard_map/ppermute | solution.py:455
  72.1 35.6 %collective-permute-start.13 = (bf16[256,2048]{1,0:T(8,128)(2,1)}, bf16[256,2048]{1,0:T(8,128)(2,1)S(1)}, u32[]{:S(2)}, u32[]{:S(2)}) collective-permute-start(bf16[256,2048]{1,0:T(8,128)(2,1)} %dynamic-slice_bitcast_fusion.1), channel_id=1, source_target_pairs={{8,16},{16,8},{9,17},{17,9},{10,18},{18,10},{11,19},{19,11},{12,20... | collective-permute-start | bytes 3145736 | tf_op jit(solution)/shard_map/ppermute | solution.py:455
  78.8 25.7 %collective-permute-start.8 = (bf16[256,1024]{1,0:T(8,128)(2,1)S(1)}, bf16[256,1024]{1,0:T(8,128)(2,1)S(1)}, u32[]{:S(2)}, u32[]{:S(2)}) collective-permute-start(bf16[256,1024]{1,0:T(8,128)(2,1)S(1)} %copy-done.119), channel_id=1, source_target_pairs={{8,16},{16,8},{9,17},{17,9},{10,18},{18,10},{11,19},{19,11},{12,20... | collective-permute-start | bytes 1572872 | tf_op jit(solution)/shard_map/ppermute | solution.py:455
  81.8 74.8 %collective-permute-start.15 = (bf16[1024,1024]{1,0:T(8,128)(2,1)}, bf16[1024,1024]{1,0:T(8,128)(2,1)}, u32[]{:S(2)}, u32[]{:S(2)}) collective-permute-start(bf16[1024,1024]{1,0:T(8,128)(2,1)} %dynamic-slice_bitcast_fusion), channel_id=1, source_target_pairs={{8,16},{16,8},{9,17},{17,9},{10,18},{18,10},{11,19},{19,11},{12,20... | collective-permute-start | bytes 6291464 | tf_op jit(solution)/shard_map/ppermute | solution.py:455
  104.5 54.8 %collective-permute-start.11 = (bf16[512,2048]{1,0:T(8,128)(2,1)}, bf16[512,2048]{1,0:T(8,128)(2,1)}, u32[]{:S(2)}, u32[]{:S(2)}) collective-permute-start(bf16[512,2048]{1,0:T(8,128)(2,1)} %bitcast.17), channel_id=1, source_target_pairs={{0,16},{24,8},{1,17},{25,9},{2,18},{26,10},{3,19},{27,11},{4,20},{... | collective-permute-start | bytes 6291464 | tf_op jit(solution)/shard_map/ppermute | solution.py:455
  106.4 11.0 %collective-permute-start.9 = (bf16[256,1024]{1,0:T(8,128)(2,1)S(1)}, bf16[256,1024]{1,0:T(8,128)(2,1)S(1)}, u32[]{:S(2)}, u32[]{:S(2)}) collective-permute-start(bf16[256,1024]{1,0:T(8,128)(2,1)S(1)} %collective-permute-done.8), channel_id=1, source_target_pairs={{0,1},{1,0},{2,3},{3,2},{4,5},{5,4},{6,7},{7,6},{8,9},{9,8},{10,11... | collective-permute-start | bytes 1572872 | tf_op jit(solution)/shard_map/ppermute | solution.py:44
  107.7 26.6 %collective-permute-start.7 = (bf16[256,1536]{1,0:T(8,128)(2,1)S(1)}, bf16[256,1536]{1,0:T(8,128)(2,1)S(1)}, u32[]{:S(2)}, u32[]{:S(2)}) collective-permute-start(bf16[256,1536]{1,0:T(8,128)(2,1)S(1)} %broadcast_select_fusion.25), channel_id=1, source_target_pairs={{0,1},{1,0},{2,3},{3,2},{4,5},{5,4},{6,7},{7,6},{8,9},{9,8},{10,11... | collective-permute-start | bytes 2359304 | tf_op jit(solution)/shard_map/ppermute | solution.py:44
  117.5 40.5 %collective-permute-start.14 = (bf16[256,2048]{1,0:T(8,128)(2,1)S(1)}, bf16[256,2048]{1,0:T(8,128)(2,1)}, u32[]{:S(2)}, u32[]{:S(2)}) collective-permute-start(bf16[256,2048]{1,0:T(8,128)(2,1)S(1)} %broadcast_select_fusion.14), channel_id=1, source_target_pairs={{0,1},{1,0},{2,3},{3,2},{4,5},{5,4},{6,7},{7,6},{8,9},{9,8},{10,11... | collective-permute-start | bytes 3145736 | tf_op jit(solution)/shard_map/ppermute | solution.py:44
  119.2 139.8 %copy-start.4 = (bf16[512,1024]{1,0:T(8,128)(2,1)}, bf16[512,1024]{1,0:T(8,128)(2,1)S(1)}, u32[]{:S(2)}) copy-start(bf16[512,1024]{1,0:T(8,128)(2,1)S(1)} %maximum_select_fusion.1) | copy-start | bytes 3145732
  151.6 10.8 %collective-permute-start.10 = (bf16[512,1024]{1,0:T(8,128)(2,1)S(1)}, bf16[512,1024]{1,0:T(8,128)(2,1)S(1)}, u32[]{:S(2)}, u32[]{:S(2)}) collective-permute-start(bf16[512,1024]{1,0:T(8,128)(2,1)S(1)} %get-tuple-element.200), channel_id=1, source_target_pairs={{0,16},{16,0},{1,17},{17,1},{2,18},{18,2},{3,19},{19,3},{4,20},{20... | collective-permute-start | bytes 3145736 | tf_op jit(solution)/shard_map/ppermute | solution.py:39
  156.7 47.7 %collective-permute-start.16 = (bf16[1024,1024]{1,0:T(8,128)(2,1)}, bf16[1024,1024]{1,0:T(8,128)(2,1)S(1)}, u32[]{:S(2)}, u32[]{:S(2)}) collective-permute-start(bf16[1024,1024]{1,0:T(8,128)(2,1)} %collective-permute-done.15), channel_id=1, source_target_pairs={{0,1},{1,0},{2,3},{3,2},{4,5},{5,4},{6,7},{7,6},{8,9},{9,8},{10,11... | collective-permute-start | bytes 6291464 | tf_op jit(solution)/shard_map/ppermute | solution.py:44
  214.3 3.3 collective-permute-start.17
  221.1 13.6 %collective-permute-start.20 = (bf16[256,1024]{1,0:T(8,128)(2,1)S(1)}, bf16[256,1024]{1,0:T(8,128)(2,1)}, u32[]{:S(2)}, u32[]{:S(2)}) collective-permute-start(bf16[256,1024]{1,0:T(8,128)(2,1)S(1)} %constant_dynamic-slice_fusion.10), channel_id=1, source_target_pairs={{0,8},{1,9},{2,10},{3,11},{4,12},{5,13},{6,14},{7,15},{16,24},{17,... | collective-permute-start | bytes 1572872 | tf_op jit(solution)/shard_map/ppermute | solution.py:543
  234.7 2.8 collective-permute-start.21
  260.8 2.7 collective-permute-start.22
  274.1 2.7 collective-permute-start.23
  278.7 12.5 %collective-permute-start.25 = (bf16[256,1024]{1,0:T(8,128)(2,1)S(1)}, bf16[256,1024]{1,0:T(8,128)(2,1)S(1)}, u32[]{:S(2)}, u32[]{:S(2)}) collective-permute-start(bf16[256,1024]{1,0:T(8,128)(2,1)S(1)} %constant_dynamic-slice_fusion.7), channel_id=1, source_target_pairs={{0,8},{1,9},{2,10},{3,11},{4,12},{5,13},{6,14},{7,15},{16,24},{17,... | collective-permute-start | bytes 1572872 | tf_op jit(solution)/shard_map/ppermute | solution.py:543
  291.2 2.4 collective-permute-start.26
  314.0 2.7 collective-permute-start.27
  335.6 2.7 collective-permute-start.30
  359.6 2.7 collective-permute-start.31
  365.4 15.4 %collective-permute-start.32 = (bf16[256,1024]{1,0:T(8,128)(2,1)S(1)}, bf16[256,1024]{1,0:T(8,128)(2,1)}, u32[]{:S(2)}, u32[]{:S(2)}) collective-permute-start(bf16[256,1024]{1,0:T(8,128)(2,1)S(1)} %constant_dynamic-slice_fusion.4), channel_id=1, source_target_pairs={{8,0},{9,1},{10,2},{11,3},{12,4},{13,5},{14,6},{15,7},{24,16},{25,... | collective-permute-start | bytes 1572872 | tf_op jit(solution)/shard_map/ppermute | solution.py:543
  380.8 3.5 collective-permute-start.33
  383.0 13.8 %collective-permute-start.24 = (bf16[256,1024]{1,0:T(8,128)(2,1)S(1)}, bf16[256,1024]{1,0:T(8,128)(2,1)S(1)}, u32[]{:S(2)}, u32[]{:S(2)}) collective-permute-start(bf16[256,1024]{1,0:T(8,128)(2,1)S(1)} %constant_dynamic-slice_fusion.8), channel_id=1, source_target_pairs={{24,16},{25,17},{26,18},{27,19},{28,20},{29,21},{30,22},{31,23}} | collective-permute-start | bytes 1572872 | tf_op jit(solution)/shard_map/ppermute | solution.py:455
  396.7 6.7 collective-permute-start.34
  402.9 24.4 %collective-permute-start.28 = (bf16[512,1024]{1,0:T(8,128)(2,1)}, bf16[512,1024]{1,0:T(8,128)(2,1)}, u32[]{:S(2)}, u32[]{:S(2)}) collective-permute-start(bf16[512,1024]{1,0:T(8,128)(2,1)} %get-tuple-element.212), channel_id=1, source_target_pairs={{0,16},{16,0},{1,17},{17,1},{2,18},{18,2},{3,19},{19,3},{4,20},{20... | collective-permute-start | bytes 3145736 | tf_op jit(solution)/shard_map/ppermute | solution.py:39
  426.3 7.6 collective-permute-start.35
  431.1 10.1 %collective-permute-start.29 = (bf16[256,1024]{1,0:T(8,128)(2,1)S(1)}, bf16[256,1024]{1,0:T(8,128)(2,1)S(1)}, u32[]{:S(2)}, u32[]{:S(2)}) collective-permute-start(bf16[256,1024]{1,0:T(8,128)(2,1)S(1)} %constant_dynamic-slice_fusion.5), channel_id=1, source_target_pairs={{24,16},{25,17},{26,18},{27,19},{28,20},{29,21},{30,22},{31,23}} | collective-permute-start | bytes 1572872 | tf_op jit(solution)/shard_map/ppermute | solution.py:455
  437.6 16.2 %collective-permute-start.36 = (bf16[256,1024]{1,0:T(8,128)(2,1)}, bf16[256,1024]{1,0:T(8,128)(2,1)}, u32[]{:S(2)}, u32[]{:S(2)}) collective-permute-start(bf16[256,1024]{1,0:T(8,128)(2,1)} %constant_dynamic-slice_fusion.3), channel_id=1, source_target_pairs={{8,0},{9,1},{10,2},{11,3},{12,4},{13,5},{14,6},{15,7},{24,16},{25,... | collective-permute-start | bytes 1572872 | tf_op jit(solution)/shard_map/ppermute | solution.py:543
  442.7 15.6 %collective-permute-start.41 = (bf16[256,1024]{1,0:T(8,128)(2,1)}, bf16[256,1024]{1,0:T(8,128)(2,1)}, u32[]{:S(2)}, u32[]{:S(2)}) collective-permute-start(bf16[256,1024]{1,0:T(8,128)(2,1)} %constant_dynamic-slice_fusion), channel_id=1, source_target_pairs={{0,8},{1,9},{2,10},{3,11},{4,12},{5,13},{6,14},{7,15}} | collective-permute-start | bytes 1572872 | tf_op jit(solution)/shard_map/ppermute | solution.py:455
  453.8 7.3 collective-permute-start.37
  484.9 7.4 collective-permute-start.38
  513.2 2.7 collective-permute-start.39
  525.9 139.3 %copy-start.133 = (f32[1024]{0:T(1024)S(1)}, f32[1024]{0:T(1024)}, u32[]{:S(2)}) copy-start(f32[1024]{0:T(1024)} %get-tuple-element.91) | copy-start | bytes 12292
  525.9 139.4 %copy-start.124 = (f32[3072]{0:T(1024)S(1)}, f32[3072]{0:T(1024)}, u32[]{:S(2)}) copy-start(f32[3072]{0:T(1024)} %reshape.424) | copy-start | bytes 36868
  525.9 139.4 %copy-start.134 = (f32[512]{0:T(512)S(1)}, f32[512]{0:T(512)}, u32[]{:S(2)}) copy-start(f32[512]{0:T(512)} %convert_reduce_fusion.17) | copy-start | bytes 6148
  526.0 139.4 %copy-start.135 = (f32[512]{0:T(512)S(1)}, f32[512]{0:T(512)}, u32[]{:S(2)}) copy-start(f32[512]{0:T(512)} %convert_reduce_fusion.16) | copy-start | bytes 6148
  526.0 139.4 %copy-start.136 = (f32[512]{0:T(512)S(1)}, f32[512]{0:T(512)}, u32[]{:S(2)}) copy-start(f32[512]{0:T(512)} %convert_reduce_fusion.15) | copy-start | bytes 6148
  526.0 139.4 %copy-start.137 = (f32[512]{0:T(512)S(1)}, f32[512]{0:T(512)}, u32[]{:S(2)}) copy-start(f32[512]{0:T(512)} %convert_reduce_fusion.14) | copy-start | bytes 6148
  526.0 139.4 %copy-start.138 = (f32[512]{0:T(512)S(1)}, f32[512]{0:T(512)}, u32[]{:S(2)}) copy-start(f32[512]{0:T(512)} %convert_reduce_fusion.13) | copy-start | bytes 6148
  526.0 139.4 %copy-start.139 = (f32[512]{0:T(512)S(1)}, f32[512]{0:T(512)}, u32[]{:S(2)}) copy-start(f32[512]{0:T(512)} %convert_reduce_fusion.12) | copy-start | bytes 6148
  526.0 139.4 %copy-start.140 = (f32[2048]{0:T(1024)S(1)}, f32[2048]{0:T(1024)}, u32[]{:S(2)}) copy-start(f32[2048]{0:T(1024)} %get-tuple-element.230) | copy-start | bytes 24580
  526.0 139.4 %copy-start.141 = (f32[2048]{0:T(1024)S(1)}, f32[2048]{0:T(1024)}, u32[]{:S(2)}) copy-start(f32[2048]{0:T(1024)} %get-tuple-element.228) | copy-start | bytes 24580
  526.0 139.4 %copy-start.142 = (f32[2048]{0:T(1024)S(1)}, f32[2048]{0:T(1024)}, u32[]{:S(2)}) copy-start(f32[2048]{0:T(1024)} %get-tuple-element.226) | copy-start | bytes 24580
  655.3 53.1 %collective-permute-start.45 = (bf16[64,1536]{1,0:T(8,128)(2,1)S(1)}, bf16[64,1536]{1,0:T(8,128)(2,1)S(1)}, u32[]{:S(2)}, u32[]{:S(2)}) collective-permute-start(bf16[64,1536]{1,0:T(8,128)(2,1)S(1)} %get-tuple-element.180), channel_id=1, source_target_pairs={{8,16},{16,8},{9,17},{17,9},{10,18},{18,10},{11,19},{19,11},{12,20... | collective-permute-start | bytes 589832 | tf_op jit(solution)/shard_map/ppermute | solution.py:455
  657.9 52.5 %collective-permute-start.43 = (bf16[64,1536]{1,0:T(8,128)(2,1)S(1)}, bf16[64,1536]{1,0:T(8,128)(2,1)S(1)}, u32[]{:S(2)}, u32[]{:S(2)}) collective-permute-start(bf16[64,1536]{1,0:T(8,128)(2,1)S(1)} %get-tuple-element.180), channel_id=1, source_target_pairs={{0,8},{24,16},{1,9},{25,17},{2,10},{26,18},{3,11},{27,19},{4,12},{... | collective-permute-start | bytes 589832 | tf_op jit(solution)/shard_map/ppermute | solution.py:455
  660.9 57.6 %collective-permute-start.48 = (bf16[64,2048]{1,0:T(8,128)(2,1)}, bf16[64,2048]{1,0:T(8,128)(2,1)S(1)}, u32[]{:S(2)}, u32[]{:S(2)}) collective-permute-start(bf16[64,2048]{1,0:T(8,128)(2,1)} %get-tuple-element.174), channel_id=1, source_target_pairs={{8,16},{16,8},{9,17},{17,9},{10,18},{18,10},{11,19},{19,11},{12,20... | collective-permute-start | bytes 786440 | tf_op jit(solution)/shard_map/ppermute | solution.py:455
  663.9 54.6 %collective-permute-start.46 = (bf16[64,2048]{1,0:T(8,128)(2,1)}, bf16[64,2048]{1,0:T(8,128)(2,1)}, u32[]{:S(2)}, u32[]{:S(2)}) collective-permute-start(bf16[64,2048]{1,0:T(8,128)(2,1)} %get-tuple-element.174), channel_id=1, source_target_pairs={{0,8},{24,16},{1,9},{25,17},{2,10},{26,18},{3,11},{27,19},{4,12},{... | collective-permute-start | bytes 786440 | tf_op jit(solution)/shard_map/ppermute | solution.py:455
  689.7 10.4 %collective-permute-start.42 = (f32[48,128]{1,0:T(8,128)S(1)}, f32[48,128]{1,0:T(8,128)S(1)}, u32[]{:S(2)}, u32[]{:S(2)}) collective-permute-start(f32[48,128]{1,0:T(8,128)S(1)} %convert_reduce_fusion.18), channel_id=1, source_target_pairs={{8,16},{16,8},{9,17},{17,9},{10,18},{18,10},{11,19},{19,11},{12,20... | collective-permute-start | bytes 73736 | tf_op jit(solution)/shard_map/ppermute | solution.py:455
  700.1 6.3 collective-permute-start.49
  706.4 5.4 collective-permute-start.44
  708.4 10.2 %collective-permute-start.47 = (bf16[64,2048]{1,0:T(8,128)(2,1)S(1)}, bf16[64,2048]{1,0:T(8,128)(2,1)}, u32[]{:S(2)}, u32[]{:S(2)}) collective-permute-start(bf16[64,2048]{1,0:T(8,128)(2,1)S(1)} %get-tuple-element.175), channel_id=1, source_target_pairs={{8,24},{16,0},{9,25},{17,1},{10,26},{18,2},{11,27},{19,3},{12,28},... | collective-permute-start | bytes 786440 | tf_op jit(solution)/shard_map/ppermute | solution.py:455
  710.4 153.6 %collective-permute-start.40 = (bf16[256,1024]{1,0:T(8,128)(2,1)}, bf16[256,1024]{1,0:T(8,128)(2,1)}, u32[]{:S(2)}, u32[]{:S(2)}) collective-permute-start(bf16[256,1024]{1,0:T(8,128)(2,1)} %constant_dynamic-slice_fusion.2), channel_id=1, source_target_pairs={{0,8},{1,9},{2,10},{3,11},{4,12},{5,13},{6,14},{7,15}} | collective-permute-start | bytes 1572872 | tf_op jit(solution)/shard_map/ppermute | solution.py:455
  711.8 14.7 %collective-permute-start.50 = (bf16[2,128,1024]{2,1,0:T(8,128)(2,1)S(1)}, bf16[2,128,1024]{2,1,0:T(8,128)(2,1)S(1)}, u32[]{:S(2)}, u32[]{:S(2)}) collective-permute-start(bf16[2,128,1024]{2,1,0:T(8,128)(2,1)S(1)} %copy-done.118), channel_id=1, source_target_pairs={{8,16},{16,8},{9,17},{17,9},{10,18},{18,10},{11,19},{19,11},{12,20... | collective-permute-start | bytes 1572872 | tf_op jit(solution)/shard_map/ppermute | solution.py:455
  (139 other events, 1304.5 us)

commit v2 on v1

--- a/solution.py
+++ b/solution.py
@@ -19,11 +19,7 @@
 QTILE = 256
 VMEM_LIMIT = 56 * 1024 * 1024
 
-CROSS_SAME = [(1, 0), (2, 3)]
 CROSS_SWAP = [(1, 2), (2, 1)]
-CORE_OUT = [(0, 2), (3, 1)]
-CORE_IN = [(1, 3), (2, 0)]
-CROSS_BACK = [(0, 1), (3, 2)]
 PAIR = ("section", "shard")
 
 
@@ -37,11 +33,6 @@
 
 def core_swap(value):
     return lax.ppermute(value, "section", [(0, 1), (1, 0)])
-
-
-def replica_swap(value):
-    size = lax.axis_size("replica")
-    return lax.ppermute(value, "replica", [(i, i ^ 1) for i in range(size)])
 
 
 def ordered(flag, first, second, axis):
@@ -268,19 +259,30 @@
     return place, device((place + 1) % size), device((place + size - 1) % size)
 
 
-def ring_barrier(following, previous):
+def neighbours():
+    core, layer = lax.axis_index("section"), lax.axis_index("shard")
+    sibling = {"section": 1 - core}
+    across = {"shard": 1 - layer}
+    diagonal = {"section": 1 - core, "shard": 1 - layer}
+    return core, layer, sibling, across, diagonal
+
+
+def greet(devices):
     barrier = pltpu.get_barrier_semaphore()
-    for neighbour in (following, previous):
-        pl.semaphore_signal(barrier, inc=1, device_id={"replica": neighbour}, device_id_type=MESH)
-    pl.semaphore_wait(barrier, 2)
+    for device in devices:
+        pl.semaphore_signal(barrier, inc=1, device_id=device, device_id_type=MESH)
+    pl.semaphore_wait(barrier, len(devices))
 
 
 def scatter_kernel(size, count, *refs):
-    own, out, landed = refs[:count], refs[count : 2 * count], refs[2 * count : 3 * count]
-    send_sem, recv_sem = refs[3 * count :]
+    own, refs = refs[: count + 1], refs[count + 1 :]
+    out, refs = refs[: count + 1], refs[count + 1 :]
+    landed, refs = refs[:count], refs[count:]
+    send_sem, recv_sem, small_send, small_recv = refs
+    small, small_out = own[count], out[count]
     place, following, previous = ring_place(size)
-    targets = (following, previous)
-    ring_barrier(following, previous)
+    targets = ({"replica": following}, {"replica": previous})
+    greet(targets)
 
     def send(way, item, source, slot):
         return pltpu.make_async_remote_copy(
@@ -288,7 +290,17 @@
             dst_ref=landed[item].at[way, slot],
             send_sem=send_sem.at[way, item, slot],
             recv_sem=recv_sem.at[way, item, slot],
-            device_id={"replica": targets[way]},
+            device_id=targets[way],
+            device_id_type=MESH,
+        )
+
+    def send_small(chunk, slot):
+        return pltpu.make_async_remote_copy(
+            src_ref=small_out.at[chunk],
+            dst_ref=small_out.at[chunk],
+            send_sem=small_send.at[slot],
+            recv_sem=small_recv.at[slot],
+            device_id=targets[0],
             device_id_type=MESH,
         )
 
@@ -300,6 +312,8 @@
     for item in range(count):
         send(0, item, own[item].at[0, (place + size - 1) % size], 0).start()
         send(1, item, own[item].at[1, (place + 1) % size], 0).start()
+    small_out[place] = small[...]
+    send_small(place, 0).start()
 
     def step(slot, carry):
         for item in range(count):
@@ -308,6 +322,9 @@
                 send(way, item, here, slot).wait_recv()
                 here[...] += own[item][way, chunk_of(way, slot)]
                 send(way, item, here, slot + 1).start()
+        chunk = (place + size - 1 - slot) % size
+        send_small(chunk, slot).wait_recv()
+        send_small(chunk, slot + 1).start()
         return carry
 
     lax.fori_loop(0, size - 2, step, 0)
@@ -317,48 +334,104 @@
             here = landed[item].at[way, last]
             send(way, item, here, last).wait_recv()
             out[item][way] = here[...] + own[item][way, place]
+    send_small((place + 1) % size, last).wait_recv()
 
     def finish(slot, carry):
         for item in range(count):
             for way in range(2):
                 send(way, item, landed[item].at[way, slot], slot).wait_send()
+        send_small(place, slot).wait_send()
         return carry
 
     lax.fori_loop(0, size - 1, finish, 0)
 
 
-def ring_scatter(pieces):
+def ring_scatter(pieces, small):
     size = pieces[0].shape[1]
     count = len(pieces)
     whole = pl.BlockSpec(memory_space=pltpu.VMEM)
     return pl.pallas_call(
         functools.partial(scatter_kernel, size, count),
-        out_shape=[jax.ShapeDtypeStruct((2,) + item.shape[2:], BF) for item in pieces],
-        in_specs=[whole] * count,
-        out_specs=[whole] * count,
+        out_shape=[jax.ShapeDtypeStruct((2,) + item.shape[2:], BF) for item in pieces]
+        + [jax.ShapeDtypeStruct((size,) + small.shape, small.dtype)],
+        in_specs=[whole] * (count + 1),
+        out_specs=[whole] * (count + 1),
         scratch_shapes=[pltpu.VMEM((2, size - 1) + item.shape[2:], BF) for item in pieces]
-        + [pltpu.SemaphoreType.DMA((2, count, size - 1))] * 2,
+        + [pltpu.SemaphoreType.DMA((2, count, size - 1))] * 2
+        + [pltpu.SemaphoreType.DMA((size - 1,))] * 2,
         compiler_params=pltpu.CompilerParams(
             collective_id=0, has_side_effects=True, vmem_limit_bytes=VMEM_LIMIT
         ),
         name="ring_scatter",
-    )(*pieces)
-
-
-def gather_kernel(size, count, *refs):
+    )(*pieces, small)
+
+
+def gather_kernel(size, groups, *refs):
+    count = 4
     own, out = refs[:count], refs[count : 2 * count]
-    send_sem, recv_sem, local_sem = refs[2 * count :]
+    swap_send, swap_recv, send_sem, recv_sem = refs[2 * count :]
     place, following, previous = ring_place(size)
-    targets = (following, previous)
-    ring_barrier(following, previous)
-
-    def send(way, item, source, chunk, slot):
+    targets = ({"replica": following}, {"replica": previous})
+    core, layer, sibling, across, diagonal = neighbours()
+    same = core == layer
+    greet(targets + (sibling, across, diagonal))
+
+    def parts(item, source_half, sender):
+        if item < len(groups):
+            width = own[item].shape[2] // groups[item]
+            for group in range(groups[item]):
+                start = pl.multiple_of((2 * group + sender) * width, width)
+                yield (
+                    own[item].at[source_half, :, pl.ds(group * width, width)],
+                    out[item].at[place, :, pl.ds(start, width)],
+                )
+        else:
+            deep = own[item].shape[1]
+            for half in range(2):
+                yield own[item].at[half], out[item].at[place, pl.ds(half * deep, deep)]
+
+    def copies(item, source_half, lane, kind, device=None):
+        for number, (source, target) in enumerate(parts(item, source_half, core)):
+            send, recv = swap_send.at[item, lane, number], swap_recv.at[item, kind, number]
+            if device is None:
+                yield pltpu.make_async_copy(source, target, recv)
+            else:
+                yield pltpu.make_async_remote_copy(
+                    src_ref=source,
+                    dst_ref=target,
+                    send_sem=send,
+                    recv_sem=recv,
+                    device_id=device,
+                    device_id_type=MESH,
+                )
+
+    @pl.when(same)
+    def _():
+        for item in range(count):
+            for copy in copies(item, layer, 0, 0):
+                copy.start()
+            if item < len(groups):
+                for copy in copies(item, 1 - layer, 0, 2, across):
+                    copy.start()
+
+    @pl.when(core != layer)
+    def _():
+        for item in range(count):
+            for copy in copies(item, 1 - layer, 0, 3, diagonal):
+                copy.start()
+            if item < len(groups):
+                for copy in copies(item, layer, 1, 1, sibling):
+                    copy.start()
+
+    def send(way, item, chunk, slot):
+        deep = out[item].shape[1] // 2
+        here = out[item].at[chunk, pl.ds(way * deep, deep)]
         return pltpu.make_async_remote_copy(
-            src_ref=source,
-            dst_ref=out[item].at[way, chunk],
+            src_ref=here,
+            dst_ref=here,
             send_sem=send_sem.at[way, item, slot],
             recv_sem=recv_sem.at[way, item, slot],
-            device_id={"replica": targets[way]},
+            device_id=targets[way],
             device_id_type=MESH,
         )
 
@@ -367,58 +440,400 @@
             return (place + size - 1 - slot) % size
         return (place + 1 + slot) % size
 
-    keep = []
     for item in range(count):
+
+        @pl.when(same)
+        def _(item=item):
+            for copy in copies(item, layer, 0, 0):
+                copy.wait()
+            if item < len(groups):
+                for copy in copies(item, layer, 1, 1, sibling):
+                    copy.wait_recv()
+
+        @pl.when(core != layer)
+        def _(item=item):
+            for copy in copies(item, layer, 0, 3, diagonal):
+                copy.wait_recv()
+            if item < len(groups):
+                for copy in copies(item, layer, 0, 2, across):
+                    copy.wait_recv()
+
         for way in range(2):
-            send(way, item, own[item].at[way], place, 0).start()
-            copy = pltpu.make_async_copy(
-                own[item].at[way], out[item].at[way, place], local_sem.at[way, item]
-            )
-            copy.start()
-            keep.append(copy)
+            send(way, item, place, 0).start()
 
     def step(slot, carry):
         for item in range(count):
             for way in range(2):
                 chunk = chunk_of(way, slot)
-                here = out[item].at[way, chunk]
-                send(way, item, here, chunk, slot).wait_recv()
-                send(way, item, here, chunk, slot + 1).start()
+                send(way, item, chunk, slot).wait_recv()
+                send(way, item, chunk, slot + 1).start()
         return carry
 
     lax.fori_loop(0, size - 2, step, 0)
     last = size - 2
     for item in range(count):
         for way in range(2):
-            chunk = chunk_of(way, last)
-            send(way, item, out[item].at[way, chunk], chunk, last).wait_recv()
-    for copy in keep:
-        copy.wait()
+            send(way, item, chunk_of(way, last), last).wait_recv()
+
+    @pl.when(same)
+    def _():
+        for item in range(len(groups)):
+            for copy in copies(item, 1 - layer, 0, 2, across):
+                copy.wait_send()
+
+    @pl.when(core != layer)
+    def _():
+        for item in range(count):
+            for copy in copies(item, 1 - layer, 0, 3, diagonal):
+                copy.wait_send()
+            if item < len(groups):
+                for copy in copies(item, layer, 1, 1, sibling):
+                    copy.wait_send()
 
     def finish(slot, carry):
         for item in range(count):
             for way in range(2):
-                send(way, item, own[item].at[way], place, slot).wait_send()
+                send(way, item, place, slot).wait_send()
         return carry
 
     lax.fori_loop(0, size - 1, finish, 0)
 
 
-def ring_gather(pieces, size):
+def ring_gather(pieces, groups, size):
+    spot = pl.BlockSpec(memory_space=pl.ANY)
+    shapes = [(size, item.shape[1], 2 * item.shape[2]) for item in pieces[: len(groups)]]
+    shapes += [(size, 2 * item.shape[1], item.shape[2]) for item in pieces[len(groups) :]]
     count = len(pieces)
-    spot = pl.BlockSpec(memory_space=pl.ANY)
     return pl.pallas_call(
-        functools.partial(gather_kernel, size, count),
-        out_shape=[
-            jax.ShapeDtypeStruct((2, size) + item.shape[1:], BF) for item in pieces
-        ],
-        in_specs=[spot] * count,
+        functools.partial(gather_kernel, size, groups),
+        out_shape=[jax.ShapeDtypeStruct(shape, BF) for shape in shapes],
+        in_specs=[pl.BlockSpec(memory_space=pltpu.VMEM)] * count,
         out_specs=[spot] * count,
-        scratch_shapes=[pltpu.SemaphoreType.DMA((2, count, size - 1))] * 2
-        + [pltpu.SemaphoreType.DMA((2, count))],
+        scratch_shapes=[
+            pltpu.SemaphoreType.DMA((count, 2, 3)),
+            pltpu.SemaphoreType.DMA((count, 4, 3)),
+        ]
+        + [pltpu.SemaphoreType.DMA((2, count, size - 1))] * 2,
         compiler_params=pltpu.CompilerParams(collective_id=1, has_side_effects=True),
         name="ring_gather",
     )(*pieces)
+
+
+def fetch_kernel(*refs):
+    tokens, cotangent, small, qkv, fc, out, proj = refs[:7]
+    outer, small_out, w_qkv, w_fc, w_out, w_proj = refs[7:13]
+    send_sem, recv_sem, extra_send, extra_recv, local_sem = refs[13:18]
+    buffers = refs[18:]
+    core, layer, sibling, across, diagonal = neighbours()
+    index = lax.axis_index("replica")
+    quarter = index % 4
+    low, high = index % 2, (index // 2) % 2
+    beside = {"replica": index + 1 - 2 * low}
+    above = {"replica": index + 2 - 4 * high}
+    beside_quarter = quarter + 1 - 2 * low
+    above_quarter = quarter + 2 - 4 * high
+    same = core == layer
+    far_quarter = 3 - quarter
+    greet((sibling, across, diagonal, beside, above))
+
+    depth = qkv.shape[0]
+    span = qkv.shape[1] // 6
+    wide = fc.shape[1] // 2
+    turn = proj.shape[0] // 2
+    cols = [
+        (qkv, w_qkv, lambda s, g=g: pl.multiple_of((2 * g + s) * span, span), g * span, span)
+        for g in range(3)
+    ]
+    cols.append((fc, w_fc, lambda s: pl.multiple_of(s * wide, wide), 0, wide))
+    rows = [(out, w_out, 0, out.shape[0]), (proj, w_proj, 0, turn), (proj, w_proj, turn, turn)]
+    order = [0, 1, 2, 4, 3, 5, 6]
+
+    def rows_of(item):
+        return depth if item < 4 else rows[item - 4][3]
+
+    def target(item, base, which, part=None):
+        deep = rows_of(item) // 4
+        start = base + which * deep
+        if part is not None:
+            deep = deep // 2
+            start = start + part * deep
+        place = pl.ds(pl.multiple_of(start, deep), deep)
+        if item < 4:
+            return cols[item][1].at[place, pl.ds(cols[item][3], cols[item][4])]
+        return rows[item - 4][1].at[place]
+
+    def base_of(item, shard):
+        return shard * depth if item < 4 else rows[item - 4][2]
+
+    def remote(stage, item, source, dest, device, lane=0):
+        return pltpu.make_async_remote_copy(
+            src_ref=source,
+            dst_ref=dest,
+            send_sem=send_sem.at[stage + lane, item],
+            recv_sem=recv_sem.at[stage, item],
+            device_id=device,
+            device_id_type=MESH,
+        )
+
+    def cross(item, receiver):
+        deep = rows_of(item) // 4
+        place = pl.multiple_of(base_of(item, 0) + quarter * deep, deep)
+        dest = target(item, base_of(item, layer), quarter)
+        if item < 4:
+            columns = cols[item][2](receiver)
+            source = cols[item][0].at[pl.ds(place, deep), pl.ds(columns, cols[item][4])]
+        else:
+            source = rows[item - 4][0].at[pl.ds(place, deep)]
+        return source, dest
+
+    def cross_same(item):
+        return remote(0, item, *cross(item, core), across, 5)
+
+    def cross_swap(item):
+        return remote(0, item, *cross(item, 1 - core), diagonal)
+
+    def pass_on(stage, item, which, device, part=None):
+        here = target(item, base_of(item, 1 - layer), which, part)
+        return remote(stage, item, here, here, device)
+
+    def to_sibling(item):
+        columns = cols[item][2](1 - core)
+        source = cols[item][0].at[:, pl.ds(columns, cols[item][4])]
+        start = pl.multiple_of(layer * depth, depth)
+        dest = cols[item][1].at[pl.ds(start, depth), pl.ds(cols[item][3], cols[item][4])]
+        return remote(6, item, source, dest, sibling)
+
+    def through(source, dest, number):
+        return (
+            pltpu.make_async_copy(source, buffers[number], local_sem.at[number]),
+            pltpu.make_async_copy(buffers[number], dest, local_sem.at[number]),
+        )
+
+    def keep_local(item):
+        if item < 4:
+            columns = cols[item][2](core)
+            source = cols[item][0].at[:, pl.ds(columns, cols[item][4])]
+            start = pl.multiple_of(layer * depth, depth)
+            dest = cols[item][1].at[pl.ds(start, depth), pl.ds(cols[item][3], cols[item][4])]
+        else:
+            source, dest, start, deep = rows[item - 4]
+            source, dest = source.at[pl.ds(start, deep)], dest.at[pl.ds(start, deep)]
+        return through(source, dest, item)
+
+    part = tokens.shape[1]
+    half = part // 2
+
+    def outer_rows(shard, which):
+        return pl.ds(pl.multiple_of(shard * part + which * half, half), half)
+
+    def outer_cross(block):
+        place = pl.ds(pl.multiple_of(core * half, half), half)
+
+        def copy(source):
+            return pltpu.make_async_remote_copy(
+                src_ref=source.at[block, place],
+                dst_ref=outer.at[block, outer_rows(layer, core)],
+                send_sem=extra_send.at[block],
+                recv_sem=extra_recv.at[block],
+                device_id=across,
+                device_id_type=MESH,
+            )
+
+        return copy
+
+    def outer_pass(block):
+        here = outer.at[block, outer_rows(1 - layer, core)]
+        return pltpu.make_async_remote_copy(
+            src_ref=here,
+            dst_ref=here,
+            send_sem=extra_send.at[2 + block],
+            recv_sem=extra_recv.at[2 + block],
+            device_id=sibling,
+            device_id_type=MESH,
+        )
+
+    def outer_local(source):
+        place = pl.ds(pl.multiple_of(layer * part, part), part)
+        return through(source, outer.at[:, place], 7)
+
+    def small_swap():
+        return pltpu.make_async_remote_copy(
+            src_ref=small,
+            dst_ref=small_out.at[1 - core],
+            send_sem=extra_send.at[4],
+            recv_sem=extra_recv.at[4],
+            device_id=diagonal,
+            device_id_type=MESH,
+        )
+
+    def small_pass():
+        return pltpu.make_async_remote_copy(
+            src_ref=small_out.at[core],
+            dst_ref=small_out.at[core],
+            send_sem=extra_send.at[5],
+            recv_sem=extra_recv.at[5],
+            device_id=sibling,
+            device_id_type=MESH,
+        )
+
+    def small_local():
+        return through(small, small_out.at[core], 8)
+
+    def start_outer(block):
+        @pl.when(layer == 0)
+        def _():
+            outer_cross(block)(cotangent).start()
+
+        @pl.when(layer == 1)
+        def _():
+            outer_cross(block)(tokens).start()
+
+    def crossings(item):
+        if item < 4:
+            cross_same(item).start()
+        cross_swap(item).start()
+
+    @pl.when(same)
+    def _():
+        small_local()[0].start()
+
+    @pl.when(core != layer)
+    def _():
+        small_swap().start()
+
+    start_outer(0)
+
+    @pl.when(core != layer)
+    def _():
+        crossings(order[0])
+        crossings(order[1])
+
+    @pl.when(layer == 0)
+    def _():
+        outer_local(tokens)[0].start()
+
+    @pl.when(layer == 1)
+    def _():
+        outer_local(cotangent)[0].start()
+
+    @pl.when(same)
+    def _():
+        for item in range(4):
+            to_sibling(item).start()
+        load, store = small_local()
+        load.wait()
+        store.start()
+        store.wait()
+
+    @pl.when(core != layer)
+    def _():
+        small_swap().wait_recv()
+
+    small_pass().start()
+    outer_local(tokens)[0].wait()
+    outer_local(tokens)[1].start()
+
+    @pl.when(same)
+    def _():
+        for item in range(7):
+            keep_local(item)[0].start()
+
+    def relay(sequence, ahead):
+        def onward(item):
+            pass_on(1, item, beside_quarter, beside).wait_recv()
+            pass_on(4, item, beside_quarter, above, 0).start()
+            pass_on(2, item, above_quarter, above).wait_recv()
+            pass_on(3, item, above_quarter, beside, 1).start()
+
+        for number, item in enumerate(sequence):
+            pass_on(0, item, quarter, beside).wait_recv()
+            if ahead and number + 2 < len(sequence):
+                crossings(sequence[number + 2])
+            pass_on(1, item, quarter, beside).start()
+            pass_on(2, item, quarter, above).start()
+            if number >= 1:
+                onward(sequence[number - 1])
+            if number == 0:
+                outer_cross(0)(tokens).wait_recv()
+                outer_pass(0).start()
+                start_outer(1)
+        onward(sequence[-1])
+        for item in sequence:
+            pass_on(3, item, far_quarter, beside, 1).wait_recv()
+            pass_on(4, item, far_quarter, above, 0).wait_recv()
+            for stage in (1, 2):
+                pass_on(stage, item, quarter, beside).wait_send()
+            for stage, which in ((3, 1), (4, 0)):
+                pass_on(stage, item, quarter, beside, which).wait_send()
+
+    @pl.when(same)
+    def _():
+        for item in range(7):
+            load, store = keep_local(item)
+            load.wait()
+            store.start()
+        relay([0, 1, 2, 3], False)
+        for item in range(4):
+            to_sibling(item).wait_send()
+        for item in range(7):
+            keep_local(item)[1].wait()
+
+    @pl.when(core != layer)
+    def _():
+        relay(order, True)
+        for item in range(4):
+            to_sibling(item).wait_recv()
+            cross_same(item).wait_send()
+        for item in range(7):
+            cross_swap(item).wait_send()
+        small_swap().wait_send()
+
+    outer_cross(1)(tokens).wait_recv()
+    outer_pass(1).start()
+    outer_local(tokens)[1].wait()
+    small_pass().wait()
+    for block in range(2):
+        outer_cross(block)(tokens).wait_send()
+        outer_pass(block).wait()
+
+
+def fetch_inputs(tokens, cotangent, small, qkv, fc, out, proj):
+    spot = pl.BlockSpec(memory_space=pl.ANY)
+    micro, part, width = tokens.shape
+    shapes = [
+        (micro, 2 * part, width),
+        (2,) + small.shape,
+        (2 * qkv.shape[0], qkv.shape[1] // 2),
+        (2 * fc.shape[0], fc.shape[1] // 2),
+        out.shape,
+        proj.shape,
+    ]
+    return pl.pallas_call(
+        fetch_kernel,
+        out_shape=[jax.ShapeDtypeStruct(shape, BF) for shape in shapes],
+        in_specs=[spot] * 7,
+        out_specs=[spot] * 6,
+        scratch_shapes=[
+            pltpu.SemaphoreType.DMA((7, 7)),
+            pltpu.SemaphoreType.DMA((7, 7)),
+            pltpu.SemaphoreType.DMA((6,)),
+            pltpu.SemaphoreType.DMA((6,)),
+            pltpu.SemaphoreType.DMA((9,)),
+        ]
+        + [pltpu.VMEM((qkv.shape[0], qkv.shape[1] // 6), BF)] * 3
+        + [
+            pltpu.VMEM((fc.shape[0], fc.shape[1] // 2), BF),
+            pltpu.VMEM(out.shape, BF),
+            pltpu.VMEM((proj.shape[0] // 2, width), BF),
+            pltpu.VMEM((proj.shape[0] // 2, width), BF),
+            pltpu.VMEM(tokens.shape, BF),
+            pltpu.VMEM(small.shape, BF),
+        ],
+        compiler_params=pltpu.CompilerParams(
+            collective_id=2, has_side_effects=True, vmem_limit_bytes=VMEM_LIMIT
+        ),
+        name="fetch_inputs",
+    )(tokens, cotangent, small, qkv, fc, out, proj)
 
 
 def shards(
@@ -441,7 +856,6 @@
     core = lax.axis_index("section")
     layer = lax.axis_index("shard")
     size = lax.axis_size("replica")
-    parity = lax.axis_index("replica") % 2
     own = core == layer
     first = layer == 0
     left = core == 0
@@ -470,70 +884,18 @@
             )
         ]
     ).reshape(-1, 128)
-    small = jnp.where(own, small, pair_permute(small, CROSS_SWAP))
-    small_other = core_swap(small[: 6 * half // 128])
+    outer, small_both, w_qkv, w_fc, w_out, w_proj = fetch_inputs(
+        tokens[0], cotangent[0], small, qkv_weight[0], fc_weight[0], out_weight[0], proj_weight[0]
+    )
+    flat = small_both.reshape(2, -1).astype(F32)
     full_small = jnp.concatenate(
-        [
-            jnp.where(left, small[: 6 * half // 128], small_other).reshape(6, half),
-            jnp.where(left, small_other, small[: 6 * half // 128]).reshape(6, half),
-        ],
-        axis=1,
-    ).astype(F32)
+        [flat[0, : 6 * half].reshape(6, half), flat[1, : 6 * half].reshape(6, half)], axis=1
+    )
     gain1, shift1, bias_o, gain2, shift2, bias_p = (full_small[i] for i in range(6))
-    flat = small.reshape(-1).astype(F32)
+    flat = jnp.where(left, flat[0], flat[1])
     bias_q = flat[6 * half : 7 * half]
     bias_v = flat[7 * half : 8 * half]
     bias_f = flat[8 * half :]
-
-    def fetch(index):
-        mine = jnp.where(first, tokens[0, index], cotangent[0, index])
-        give = jnp.where(first, cotangent[0, index], tokens[0, index])
-        give = lax.dynamic_slice_in_dim(give, core * (part // 2), part // 2, 0)
-        got = lax.ppermute(give, "shard", [(0, 1), (1, 0)])
-        other = ordered(left, got, core_swap(got), 0)
-        return ordered(first, mine, other, 0)
-
-    outer = [fetch(0)]
-
-    def crossed(value, axis, pairs):
-        length = value.shape[axis] // 2
-        piece = lax.dynamic_slice_in_dim(value, parity * length, length, axis)
-        pieces = [pair_permute(piece, each) for each in pairs]
-        got = pieces[0] if len(pieces) == 1 else jnp.where(own, pieces[0], pieces[1])
-        return ordered(parity == 0, got, replica_swap(got), axis)
-
-    def column_halves(weight, groups):
-        depth = weight.shape[0]
-        parts = weight.reshape(depth, groups, 2, -1)
-        mine = jnp.where(left, parts[:, :, 0], parts[:, :, 1]).reshape(depth, -1)
-        other = jnp.where(left, parts[:, :, 1], parts[:, :, 0]).reshape(depth, -1)
-        return mine, other
-
-    def fetch_columns(weight, groups):
-        mine, other = column_halves(weight, groups)
-        sibling = pair_permute(other, CORE_OUT)
-        length = mine.shape[0] // 2
-        piece_mine = lax.dynamic_slice_in_dim(mine, parity * length, length, 0)
-        piece_other = lax.dynamic_slice_in_dim(other, parity * length, length, 0)
-        got = jnp.where(
-            own, pair_permute(piece_mine, CROSS_SAME), pair_permute(piece_other, CROSS_SWAP)
-        )
-        far = ordered(parity == 0, got, replica_swap(got), 0)
-        near = jnp.where(own, mine, sibling)
-        return ordered(first, near, far, 0)
-
-    def fetch_rows(weight):
-        length = weight.shape[0] // 2
-        piece = lax.dynamic_slice_in_dim(weight, parity * length, length, 0)
-        got = pair_permute(piece, CROSS_SWAP)
-        far = ordered(parity == 0, got, replica_swap(got), 0)
-        return jnp.where(own, weight, far)
-
-    w_qkv = fetch_columns(qkv_weight[0], 3)
-    w_out = fetch_rows(out_weight[0])
-    w_fc = fetch_columns(fc_weight[0], 1)
-    w_proj = fetch_rows(proj_weight[0])
-    outer.append(fetch(1))
 
     def exchanged(partial):
         return partial + core_swap(partial.astype(BF)).astype(F32)
@@ -639,39 +1001,15 @@
     ]
     pieces[2] = jnp.swapaxes(pieces[2], 0, 1)
     pieces[3] = jnp.swapaxes(pieces[3], 0, 1)
-    g_qkv, g_fc, g_out, g_proj = ring_scatter(pieces)
-
-    def return_columns(piece, groups):
-        near = jnp.where(first, piece[0], piece[1])
-        far = jnp.where(first, piece[1], piece[0])
-        near_core = pair_permute(near, CORE_IN)
-        far_same = pair_permute(far, CROSS_BACK)
-        far_swap = pair_permute(far, CROSS_SWAP)
-        mine = jnp.where(own, near, far_same).reshape(chunk, groups, 1, -1)
-        other = jnp.where(own, near_core, far_swap).reshape(chunk, groups, 1, -1)
-        return ordered(left, mine, other, 2).reshape(2, chunk // 2, -1)
-
-    def return_rows(piece):
-        return jnp.where(own, piece, pair_permute(piece, CROSS_SWAP))
-
-    owned = [
-        return_columns(g_qkv, 3),
-        return_columns(g_fc, 1),
-        return_rows(g_out),
-        return_rows(g_proj),
-    ]
-    gathered = ring_gather(owned, size)
-
-    def finished(item):
-        full = jnp.swapaxes(item, 0, 1).astype(F32)
-        return full.reshape(1, -1, item.shape[-1])
-
-    qkv_grad, fc_grad, out_grad, proj_grad = (finished(item) for item in gathered)
-
-    sums = lax.all_gather(sums.astype(BF).reshape(-1, 128), "replica", axis=0)
-    sums = jnp.sum(sums.astype(F32), axis=0)
-    sums = jnp.where(own, sums, pair_permute(sums, CROSS_SWAP)).reshape(-1)
+    sums = sums.reshape(-1, 128)
+    sums = jnp.where(own, sums, pair_permute(sums, CROSS_SWAP))
+    *reduced, sums = ring_scatter(pieces, sums)
+    sums = jnp.sum(sums, axis=0).reshape(-1)
     vectors = [sums[i * half : (i + 1) * half][None] for i in range(8)] + [sums[8 * half :][None]]
+    qkv_grad, fc_grad, out_grad, proj_grad = (
+        item.astype(F32).reshape(1, -1, item.shape[-1])
+        for item in ring_gather(reduced, (3, 1), size)
+    )
 
     def placed(mine, arrived, pairs, far):
         near = lax.dynamic_slice_in_dim(mine, layer * part, part, 0)

time: 876 us -> 714 us (0.82)
  Pallas kernels: 311 us -> 399 us
  waiting for transfers between devices: 154 us -> 66.4 us
  starting transfers between devices: 85.1 us -> 23.7 us
  local copies, waits for them, and re-layouts: 98.3 us -> 39.4 us
  blocking collectives: 24.2 us -> 0 us
  other arithmetic: 95.9 us -> 77.7 us
    pallas_call x1 -> x2, Pallas kernels: 117 us -> 205 us  [the longest x1 130 us: ring_gather(): pl.pallas_call(functools.partial(gather_kernel, size, groups), out_shape=...]
    ppermute x6 -> x0, waiting for transfers between devices: 61.9 us -> none  [the longest x4 61.9 us: replica_swap(): return lax.ppermute(value, 'replica', [(i, i ^ 1) for i in range(size)])]
    ppermute x22 -> x5, starting transfers between devices: 57.8 us -> 8.05 us  [pair_permute(): return lax.ppermute(value, PAIR, pairs)]
    all_gather x1 -> x0, blocking collectives: 24.2 us -> none  [shards(): sums = lax.all_gather(sums.astype(BF).reshape(-1, 128), 'replica', axis=0)]
    ppermute x22 -> x5, waiting for transfers between devices: 28.3 us -> 5.7 us  [pair_permute(): return lax.ppermute(value, PAIR, pairs)]
    unnamed x322 -> x236, local copies, waits for them, and re-layouts: 49 us -> 27.9 us
    reshape x8 -> x0, local copies, waits for them, and re-layouts: 15.6 us -> none  [the longest x4 13.4 us: finished(): return full.reshape(1, -1, item.shape[-1])]
    select_n x15 -> x4, other arithmetic: 19 us -> 4.19 us  [ordered(): jnp.where(flag, first, second)]
  transfers between devices with their start and end apart: 51 -> 25, of which waited for: 23 -> 14; matrix products, arithmetic and copies ran while one was open for 17% -> 12% of each run, Pallas kernels for 16% -> 38%
where the time goes in v2:
time: 714 us; the launch traced here: 707 us
  Pallas kernels  399 us (56%)
  matrix products  97.7 us (14%)
  other arithmetic  77.7 us (11%)
  waiting for transfers between devices  66.4 us (9%)
  local copies, waits for them, and re-layouts  39.4 us (6%)
  starting transfers between devices  23.7 us (3%)
    pallas_call x1, Pallas kernels, ring_gather(): pl.pallas_call(functools.partial(gather_kernel, size, groups), out_shape=...  130 us
    pallas_call x1, Pallas kernels, ring_scatter(): pl.pallas_call(functools.partial(scatter_kernel, size, count), out_shape=...  128 us
    pallas_call x1, Pallas kernels, fetch_inputs(): pl.pallas_call(fetch_kernel, out_shape=[jax.ShapeDtypeStruct(shape, BF) f...  74.6 us
    dot_general x12, matrix products, cols_product(): lax.dot_general(left, right, COLS_CONTRACT, preferred_element_type=F32)  43 us
    ppermute x4, waiting for transfers between devices, passed(): got = lax.ppermute(give, 'shard', pairs)  41 us
    pallas_call x3, Pallas kernels, attend_back(): pl.pallas_call(attend_back_kernel, grid_spec=pltpu.PrefetchScalarGridSpec...  33.7 us
    pallas_call x3, Pallas kernels, attend(): pl.pallas_call(attend_kernel, grid_spec=pltpu.PrefetchScalarGridSpec(num_...  32.9 us
    unnamed x236, local copies, waits for them, and re-layouts  27.9 us
  transfers between devices with their start and end apart: 25, of which 14 were waited for; matrix products, arithmetic and copies ran while one was open for 12% of the time, Pallas kernels for 38%

profile of v2, /device:TPU:1, one launch (start us, length us, event | category | flops | bytes accessed | tf_op | source)
XLA Modules:
  0.0 706.7 jit_solution(4213331349193839009)
XLA Ops:
  9.3 74.6 %fetch_inputs.1 = (bf16[2,512,1024]{2,1,0:T(8,128)(2,1)}, bf16[2,48,128]{2,1,0:T(8,128)(2,1)}, bf16[1024,1536]{1,0:T(8,128)(2,1)}, bf16[1024,2048]{1,0:T(8,128)(...) custom-call(bf16[2,256,1024]{2,1,0:T(8,128)(2,1)} %bitcast.184, bf16[2,256,1024]{2,1,0:T(8,128)(2,1)} %bitcast.185, ...), custom_call_target="tpu_custom_call" | custom-call | tf_op jit(solution)/shard_map/fetch_inputs/pallas_call | solution.py:811
  84.0 1.7 convert_reduce_fusion.5
  85.7 1.7 fusion.79
  88.3 3.8 fusion.164
  95.4 8.3 %attend.3 = (bf16[512,512]{1,0:T(8,128)(2,1)}, f32[4,8,512]{2,1,0:T(8,128)}) custom-call(s32[1]{0:T(128)} %constant.57.clone.1.block_ref, bf16[512,512]{1,0:T(8,128)(2,1)} %get-tuple-element.143.q_ref, bf16[1024,512]{1,0:T(8,128)(2,1)} %dynamic_update_slice.18.k_ref, bf16[1024,512]{1,0:T(8,128)(2,1)} %dynamic_update_slice.19.v_ref), custom_call_target="tpu_custom_call" | custom-call | flops 1073741824 | bytes 2097152 | tf_op jit(solution)/shard_map/attend/pallas_call | solution.py:116
  103.7 1.8 fusion.185
  105.9 2.3 collective-permute-done
  109.1 2.0 copy-done.87
  111.1 2.5 fusion.166
  113.6 4.5 fusion.186
  118.5 2.5 collective-permute-done.1
  122.0 3.1 add_convert_fusion.4
  125.1 4.1 collective-permute-start.2
  129.2 10.4 %collective-permute-done.2 = bf16[256,1024]{1,0:T(8,128)(2,1)} collective-permute-done((bf16[256,1024]{1,0:T(8,128)(2,1)S(1)}, bf16[256,1024]{1,0:T(8,128)(2,1)}, u32[]{:S(2)}, u32[]{:S(2)}) %collective-permute-start.2) | collective-permute-done | bytes 524320 | tf_op jit(solution)/shard_map/ppermute | solution.py:905
  140.5 1.9 collective-permute-done.3
  146.4 1.8 fusion.197
  150.7 12.4 %attend.4 = (bf16[512,512]{1,0:T(8,128)(2,1)}, f32[4,8,512]{2,1,0:T(8,128)}) custom-call(s32[1]{0:T(128)} %bitcast.19.block_ref, bf16[512,512]{1,0:T(8,128)(2,1)} %fusion.120.q_ref, bf16[1024,512]{1,0:T(8,128)(2,1)} %copy-done.74, bf16[1024,512]{1,0:T(8,128)(2,1)} %copy-done.70), custom_call_target="tpu_custom_call" | custom-call | flops 1073741824 | bytes 2097152 | tf_op jit(solution)/shard_map/attend/pallas_call | solution.py:116
  163.0 1.8 fusion.187
  165.2 2.3 collective-permute-done.4
  168.9 2.2 copy-done.88
  171.0 5.2 multiply_convert_fusion.4
  176.3 2.3 fusion.188
  179.1 2.3 collective-permute-done.5
  181.4 1.7 broadcast_select_fusion.8
  183.2 1.7 collective-permute-start.7
  184.9 10.8 %collective-permute-done.7 = bf16[256,1024]{1,0:T(8,128)(2,1)S(1)} collective-permute-done((bf16[256,1024]{1,0:T(8,128)(2,1)S(1)}, bf16[256,1024]{1,0:T(8,128)(2,1)S(1)}, u32[]{:S(2)}, u32[]{:S(2)}) %collective-permute-start.7) | collective-permute-done | bytes 524320 | tf_op jit(solution)/shard_map/ppermute | solution.py:905
  200.5 1.9 fusion.156
  204.1 12.2 %attend.5 = (bf16[512,512]{1,0:T(8,128)(2,1)}, f32[4,8,512]{2,1,0:T(8,128)}) custom-call(s32[1]{0:T(128)} %constant.69.clone.1.block_ref, bf16[512,512]{1,0:T(8,128)(2,1)} %fusion.118.q_ref, bf16[1024,512]{1,0:T(8,128)(2,1)} %copy-done.76, bf16[1024,512]{1,0:T(8,128)(2,1)} %copy-done.72), custom_call_target="tpu_custom_call" | custom-call | flops 1073741824 | bytes 2097152 | tf_op jit(solution)/shard_map/attend/pallas_call | solution.py:116
  216.3 1.8 fusion.189
  218.5 2.3 collective-permute-done.9
  221.7 2.0 copy-done.89
  225.0 6.0 broadcast_select_fusion
  231.0 5.0 convert_reduce_fusion.2
  236.1 2.4 fusion.191
  238.9 2.3 collective-permute-done.12
  245.9 12.3 %attend_back.3 = (bf16[512,512]{1,0:T(8,128)(2,1)}, bf16[512,512]{1,0:T(8,128)(2,1)}, bf16[512,512]{1,0:T(8,128)(2,1)}, f32[512,512]{1,0:T(8,128)}, f32[512,512]{1,0:T(8,128)}) custom-call(s32[1]{0:T(128)} %constant.69.clone.1.block_ref, bf16[512,512]{1,0:T(8,128)(2,1)} %fusion.118.q_ref, bf16[1024,512]{1,0:T(8,128)(2,1)} %copy-done.76, ...), custom_call_target="tpu_custom_call" | custom-call | flops 2684354560 | bytes 4194304 | tf_op jit(solution)/shard_map/attend_back/pallas_call | solution.py:222
  260.5 4.3 fusion.192
  265.3 2.3 collective-permute-done.13
  271.9 14.1 %collective-permute-done.14 = bf16[256,1024]{1,0:T(8,128)(2,1)} collective-permute-done((bf16[256,1024]{1,0:T(8,128)(2,1)S(1)}, bf16[256,1024]{1,0:T(8,128)(2,1)}, u32[]{:S(2)}, u32[]{:S(2)}) %collective-permute-start.14) | collective-permute-done | bytes 524320 | tf_op jit(solution)/shard_map/ppermute | solution.py:905
  292.5 6.8 convert_reduce_fusion.1
  299.3 2.4 fusion.193
  302.9 3.8 fusion.190
  310.8 12.7 %attend_back.4 = (bf16[512,512]{1,0:T(8,128)(2,1)}, bf16[512,512]{1,0:T(8,128)(2,1)}, bf16[512,512]{1,0:T(8,128)(2,1)}, f32[512,512]{1,0:T(8,128)}, f32[512,512]{1,0:T(8,128)}) custom-call(s32[1]{0:T(128)} %bitcast.19.block_ref, bf16[512,512]{1,0:T(8,128)(2,1)} %fusion.120.q_ref, bf16[1024,512]{1,0:T(8,128)(2,1)} %copy-done.76, ...), custom_call_target="tpu_custom_call" | custom-call | flops 2684354560 | bytes 4194304 | tf_op jit(solution)/shard_map/attend_back/pallas_call | solution.py:222
  325.9 4.3 fusion.194
  331.5 3.3 broadcast_select_fusion.5
  340.6 5.7 collective-permute-done.11
  350.5 5.8 collective-permute-done.18
  356.6 2.8 fusion.137
  362.2 7.1 %broadcast_select_fusion.1 = (bf16[512,2048]{1,0:T(8,128)(2,1)S(1)}, bf16[512,2048]{1,0:T(8,128)(2,1)S(1)}) fusion(bf16[512,2048]{1,0:T(8,128)(2,1)S(1)} %copy-done.102, pred[]{:T(512)S(6)} %eq.16, f32[512,2048]{1,0:T(8,128)} %copy-done.99, f32[2048]{0:T(1024)S(1)} %bitcast.254, bf16[512,1024]{1,0:T(8,128)(2,1)S(1)} %get-tuple-element.111, ...), kind=kOutput, calls=%fused_computation.167 | convolution fusion | flops 2171600896 | bytes 15736833 | tf_op jit(solution)/shard_map/dot_general | solution.py:31
  369.4 2.4 fusion.195
  372.3 6.2 fusion.29
  382.5 8.6 %attend_back.5 = (bf16[512,512]{1,0:T(8,128)(2,1)}, bf16[512,512]{1,0:T(8,128)(2,1)}, bf16[512,512]{1,0:T(8,128)(2,1)}, f32[512,512]{1,0:T(8,128)}, f32[512,512]{1,0:T(8,128)}) custom-call(s32[1]{0:T(128)} %constant.57.clone.1.block_ref, bf16[512,512]{1,0:T(8,128)(2,1)} %get-tuple-element.143.q_ref, bf16[1024,512]{1,0:T(8,128)(2,1)} %copy-done.76, ...), custom_call_target="tpu_custom_call" | custom-call | flops 2684354560 | bytes 4194304 | tf_op jit(solution)/shard_map/attend_back/pallas_call | solution.py:222
  393.4 3.7 fusion.196
  402.4 2.2 collective-permute-start.24
  404.6 5.4 broadcast_select_fusion.6
  412.4 5.2 fusion.26
  417.7 5.0 convolution_convert_fusion
  423.9 2.5 copy.36
  428.1 127.6 %ring_scatter.1 = (bf16[2,64,1536]{2,1,0:T(8,128)(2,1)}, bf16[2,64,2048]{2,1,0:T(8,128)(2,1)}, bf16[2,32,1024]{2,1,0:T(8,128)(2,1)}, bf16[2,128,1024]{2,1,0:T(8,128)(2,1)}, f32[8,48,128]{2,1,0:T(8,128)}) custom-call(bf16[2,8,64,1536]{3,2,1,0:T(8,128)(2,1)} %bitcast.179, bf16[2,8,64,2048]{3,2,1,0:T(8,128)(2,1)} %bitcast.174, ...), custom_call_target="tpu_custom_call" | custom-call | tf_op jit(solution)/shard_map/ring_scatter/pallas_call | solution.py:353
  557.3 130.4 %ring_gather.1 = (bf16[8,64,3072]{2,1,0:T(8,128)(2,1)}, bf16[8,64,4096]{2,1,0:T(8,128)(2,1)}, bf16[8,64,1024]{2,1,0:T(8,128)(2,1)}, bf16[8,256,1024]{2,1,0:T(8,128)(2,1)}) custom-call(bf16[2,64,1536]{2,1,0:T(8,128)(2,1)} %get-tuple-element.75.refs_0_, bf16[2,64,2048]{2,1,0:T(8,128)(2,1)} %get-tuple-element.76.refs_1_, ...), custom_call_target="tpu_custom_call" | custom-call | tf_op jit(solution)/shard_map/ring_gather/pallas_call | solution.py:507
  687.7 5.5 bitcast_convert_fusion.2
  693.2 4.5 bitcast_convert_fusion.1
  697.7 4.4 bitcast_convert_fusion
  702.8 1.6 bitcast_convert_fusion.3
  (392 shorter events, 95.9 us)
Async XLA Ops:
  85.6 6.5 copy-start.82
  95.4 8.3 %copy-start.11 = (bf16[512,1024]{1,0:T(8,128)(2,1)S(1)}, bf16[512,1024]{1,0:T(8,128)(2,1)}, u32[]{:S(2)}) copy-start(bf16[512,1024]{1,0:T(8,128)(2,1)} %get-tuple-element.53) | copy-start | bytes 3145732
  105.4 2.7 collective-permute-start
  108.8 4.8 copy-start.1
  118.1 2.9 collective-permute-start.1
  125.1 18.6 %copy-start.23 = (bf16[512,1024]{1,0:T(8,128)(2,1)}, bf16[512,1024]{1,0:T(8,128)(2,1)S(1)}, u32[]{:S(2)}) copy-start(bf16[512,1024]{1,0:T(8,128)(2,1)S(1)} %add_convert_fusion.4) | copy-start | bytes 3145732
  125.1 14.4 %collective-permute-start.2 = (bf16[256,1024]{1,0:T(8,128)(2,1)S(1)}, bf16[256,1024]{1,0:T(8,128)(2,1)}, u32[]{:S(2)}, u32[]{:S(2)}) collective-permute-start(bf16[256,1024]{1,0:T(8,128)(2,1)S(1)} %constant_dynamic-slice_fusion.10), channel_id=1, source_target_pairs={{0,8},{1,9},{2,10},{3,11},{4,12},{5,13},{6,14},{7,15},{16,24},{17,... | collective-permute-start | bytes 1572872 | tf_op jit(solution)/shard_map/ppermute | solution.py:905
  139.6 2.8 collective-permute-start.3
  144.1 23.4 %copy-start.6 = (bf16[512,1024]{1,0:T(8,128)(2,1)}, bf16[512,1024]{1,0:T(8,128)(2,1)S(1)}, u32[]{:S(2)}) copy-start(bf16[512,1024]{1,0:T(8,128)(2,1)S(1)} %get-tuple-element.135) | copy-start | bytes 3145732
  149.4 13.7 %copy-start.12 = (bf16[512,1024]{1,0:T(8,128)(2,1)S(1)}, bf16[512,1024]{1,0:T(8,128)(2,1)}, u32[]{:S(2)}) copy-start(bf16[512,1024]{1,0:T(8,128)(2,1)} %get-tuple-element.53) | copy-start | bytes 3145732
  164.8 2.7 collective-permute-start.4
  168.1 13.3 %copy-start.4 = (f32[512,1024]{1,0:T(8,128)}, f32[512,1024]{1,0:T(8,128)S(1)}, u32[]{:S(2)}) copy-start(f32[512,1024]{1,0:T(8,128)S(1)} %get-tuple-element.133) | copy-start | bytes 6291460
  171.0 5.3 copy-start.67
  171.0 5.3 copy-start.93
  176.3 5.1 copy-start.24
  178.6 2.7 collective-permute-start.5
  183.1 15.1 %copy-start.21 = (bf16[512,1024]{1,0:T(8,128)(2,1)}, bf16[512,1024]{1,0:T(8,128)(2,1)S(1)}, u32[]{:S(2)}) copy-start(bf16[512,1024]{1,0:T(8,128)(2,1)S(1)} %get-tuple-element.127) | copy-start | bytes 3145732
  183.2 12.5 %collective-permute-start.7 = (bf16[256,1024]{1,0:T(8,128)(2,1)S(1)}, bf16[256,1024]{1,0:T(8,128)(2,1)S(1)}, u32[]{:S(2)}, u32[]{:S(2)}) collective-permute-start(bf16[256,1024]{1,0:T(8,128)(2,1)S(1)} %constant_dynamic-slice_fusion.8), channel_id=1, source_target_pairs={{0,8},{1,9},{2,10},{3,11},{4,12},{5,13},{6,14},{7,15},{16,24},{17,... | collective-permute-start | bytes 1572872 | tf_op jit(solution)/shard_map/ppermute | solution.py:905
  195.7 2.4 collective-permute-start.8
  218.1 2.7 collective-permute-start.9
  221.3 19.9 %copy-start.9 = (f32[512,1024]{1,0:T(8,128)}, f32[512,1024]{1,0:T(8,128)S(1)}, u32[]{:S(2)}) copy-start(f32[512,1024]{1,0:T(8,128)S(1)} %get-tuple-element.129) | copy-start | bytes 6291460
  225.0 6.0 copy-start.94
  231.0 5.1 copy-start.105
  238.5 2.7 collective-permute-start.12
  243.3 25.4 %copy-start.8 = (f32[512,1024]{1,0:T(8,128)}, f32[512,1024]{1,0:T(8,128)S(1)}, u32[]{:S(2)}) copy-start(f32[512,1024]{1,0:T(8,128)S(1)} %get-tuple-element.120) | copy-start | bytes 6291460
  264.8 2.7 collective-permute-start.13
  270.6 15.4 %collective-permute-start.14 = (bf16[256,1024]{1,0:T(8,128)(2,1)S(1)}, bf16[256,1024]{1,0:T(8,128)(2,1)}, u32[]{:S(2)}, u32[]{:S(2)}) collective-permute-start(bf16[256,1024]{1,0:T(8,128)(2,1)S(1)} %constant_dynamic-slice_fusion.5), channel_id=1, source_target_pairs={{8,0},{9,1},{10,2},{11,3},{12,4},{13,5},{14,6},{15,7},{24,16},{25,... | collective-permute-start | bytes 1572872 | tf_op jit(solution)/shard_map/ppermute | solution.py:905
  286.0 3.7 collective-permute-start.15
  288.1 13.7 %collective-permute-start.6 = (bf16[256,1024]{1,0:T(8,128)(2,1)S(1)}, bf16[256,1024]{1,0:T(8,128)(2,1)S(1)}, u32[]{:S(2)}, u32[]{:S(2)}) collective-permute-start(bf16[256,1024]{1,0:T(8,128)(2,1)S(1)} %constant_dynamic-slice_fusion.9), channel_id=1, source_target_pairs={{24,16},{25,17},{26,18},{27,19},{28,20},{29,21},{30,22},{31,23}} | collective-permute-start | bytes 1572872 | tf_op jit(solution)/shard_map/ppermute | solution.py:869
  292.4 15.6 %copy-start.41 = (bf16[512,1024]{1,0:T(8,128)(2,1)}, bf16[512,1024]{1,0:T(8,128)(2,1)S(1)}, u32[]{:S(2)}) copy-start(bf16[512,1024]{1,0:T(8,128)(2,1)S(1)} %get-tuple-element.115) | copy-start | bytes 3145732
  292.5 6.8 copy-start.90
  301.7 5.2 collective-permute-start.16
  306.7 24.8 %collective-permute-start.10 = (bf16[512,1024]{1,0:T(8,128)(2,1)}, bf16[512,1024]{1,0:T(8,128)(2,1)}, u32[]{:S(2)}, u32[]{:S(2)}) collective-permute-start(bf16[512,1024]{1,0:T(8,128)(2,1)} %get-tuple-element.188), channel_id=1, source_target_pairs={{0,16},{16,0},{1,17},{17,1},{2,18},{18,2},{3,19},{19,3},{4,20},{20... | collective-permute-start | bytes 3145736 | tf_op jit(solution)/shard_map/ppermute | solution.py:35
  325.9 5.6 copy-start.2
  325.9 5.6 copy-start.10
  330.2 6.2 collective-permute-start.17
  334.9 11.5 %collective-permute-start.11 = (bf16[256,1024]{1,0:T(8,128)(2,1)S(1)}, bf16[256,1024]{1,0:T(8,128)(2,1)S(1)}, u32[]{:S(2)}, u32[]{:S(2)}) collective-permute-start(bf16[256,1024]{1,0:T(8,128)(2,1)S(1)} %constant_dynamic-slice_fusion.6), channel_id=1, source_target_pairs={{24,16},{25,17},{26,18},{27,19},{28,20},{29,21},{30,22},{31,23}} | collective-permute-start | bytes 1572872 | tf_op jit(solution)/shard_map/ppermute | solution.py:869
  337.7 8.7 %copy-start.26 = (bf16[256,1024]{1,0:T(8,128)(2,1)S(1)}, bf16[256,1024]{1,0:T(8,128)(2,1)}, u32[]{:S(2)}) copy-start(bf16[256,1024]{1,0:T(8,128)(2,1)} %copy-done.25) | copy-start | bytes 1572868
  337.7 8.7 %copy-start.28 = (bf16[256,1024]{1,0:T(8,128)(2,1)S(1)}, bf16[256,1024]{1,0:T(8,128)(2,1)}, u32[]{:S(2)}) copy-start(bf16[256,1024]{1,0:T(8,128)(2,1)} %copy-done.27) | copy-start | bytes 1572868
  339.1 7.9 %copy-start.18 = (bf16[512,1024]{1,0:T(8,128)(2,1)}, bf16[512,1024]{1,0:T(8,128)(2,1)S(1)}, u32[]{:S(2)}) copy-start(bf16[512,1024]{1,0:T(8,128)(2,1)S(1)} %get-tuple-element.123) | copy-start | bytes 3145732
  339.2 7.9 %copy-start.46 = (bf16[512,1024]{1,0:T(8,128)(2,1)}, bf16[512,1024]{1,0:T(8,128)(2,1)S(1)}, u32[]{:S(2)}) copy-start(bf16[512,1024]{1,0:T(8,128)(2,1)S(1)} %get-tuple-element.122) | copy-start | bytes 3145732
  339.2 17.1 %collective-permute-start.18 = (bf16[256,1024]{1,0:T(8,128)(2,1)S(1)}, bf16[256,1024]{1,0:T(8,128)(2,1)}, u32[]{:S(2)}, u32[]{:S(2)}) collective-permute-start(bf16[256,1024]{1,0:T(8,128)(2,1)S(1)} %constant_dynamic-slice_fusion.4), channel_id=1, source_target_pairs={{8,0},{9,1},{10,2},{11,3},{12,4},{13,5},{14,6},{15,7},{24,16},{25,... | collective-permute-start | bytes 1572872 | tf_op jit(solution)/shard_map/ppermute | solution.py:905
  347.1 9.2 %copy-start.56 = (bf16[512,512]{1,0:T(8,128)(2,1)S(1)}, bf16[512,512]{1,0:T(8,128)(2,1)}, u32[]{:S(2)}) copy-start(bf16[512,512]{1,0:T(8,128)(2,1)} %get-tuple-element.65) | copy-start | bytes 1572868
  348.0 8.6 %collective-permute-start.23 = (bf16[256,1024]{1,0:T(8,128)(2,1)}, bf16[256,1024]{1,0:T(8,128)(2,1)}, u32[]{:S(2)}, u32[]{:S(2)}) collective-permute-start(bf16[256,1024]{1,0:T(8,128)(2,1)} %constant_dynamic-slice_fusion), channel_id=1, source_target_pairs={{0,8},{1,9},{2,10},{3,11},{4,12},{5,13},{6,14},{7,15}} | collective-permute-start | bytes 1572872 | tf_op jit(solution)/shard_map/ppermute | solution.py:869
  356.3 3.1 collective-permute-start.19
  356.6 5.5 copy-start.102
  362.1 17.6 %copy-start.16 = (bf16[512,1024]{1,0:T(8,128)(2,1)}, bf16[512,1024]{1,0:T(8,128)(2,1)S(1)}, u32[]{:S(2)}) copy-start(bf16[512,1024]{1,0:T(8,128)(2,1)S(1)} %get-tuple-element.111) | copy-start | bytes 3145732
  362.2 7.1 %copy-start.91 = (bf16[1024,2048]{1,0:T(8,128)(2,1)S(1)}, bf16[1024,2048]{1,0:T(8,128)(2,1)}, u32[]{:S(2)}) copy-start(bf16[1024,2048]{1,0:T(8,128)(2,1)} %get-tuple-element.54) | copy-start | bytes 12582916
  371.7 6.8 collective-permute-start.20
  372.3 6.2 copy-start.3
  397.1 3.7 collective-permute-start.21
  402.4 10.0 %copy-start.42 = (bf16[512,1024]{1,0:T(8,128)(2,1)S(1)}, bf16[512,1024]{1,0:T(8,128)(2,1)}, u32[]{:S(2)}) copy-start(bf16[512,1024]{1,0:T(8,128)(2,1)} %copy-done.41) | copy-start | bytes 3145732
  402.4 10.0 %copy-start.108 = (bf16[512,2048]{1,0:T(8,128)(2,1)S(1)}, bf16[512,2048]{1,0:T(8,128)(2,1)}, u32[]{:S(2)}) copy-start(bf16[512,2048]{1,0:T(8,128)(2,1)} %copy-done.107) | copy-start | bytes 6291460
  402.4 10.0 %copy-start.109 = (bf16[512,2048]{1,0:T(8,128)(2,1)S(1)}, bf16[512,2048]{1,0:T(8,128)(2,1)}, u32[]{:S(2)}) copy-start(bf16[512,2048]{1,0:T(8,128)(2,1)} %get-tuple-element.204) | copy-start | bytes 6291460
  402.4 25.1 %collective-permute-start.24 = (f32[48,128]{1,0:T(8,128)S(1)}, f32[48,128]{1,0:T(8,128)S(1)}, u32[]{:S(2)}, u32[]{:S(2)}) collective-permute-start(f32[48,128]{1,0:T(8,128)S(1)} %fusion.148), channel_id=1, source_target_pairs={{8,16},{16,8},{9,17},{17,9},{10,18},{18,10},{11,19},{19,11},{12,20... | collective-permute-start | bytes 73736 | tf_op jit(solution)/shard_map/ppermute | solution.py:869
  410.9 293.4 %collective-permute-start.22 = (bf16[256,1024]{1,0:T(8,128)(2,1)}, bf16[256,1024]{1,0:T(8,128)(2,1)}, u32[]{:S(2)}, u32[]{:S(2)}) collective-permute-start(bf16[256,1024]{1,0:T(8,128)(2,1)} %constant_dynamic-slice_fusion.2), channel_id=1, source_target_pairs={{0,8},{1,9},{2,10},{3,11},{4,12},{5,13},{6,14},{7,15}} | collective-permute-start | bytes 1572872 | tf_op jit(solution)/shard_map/ppermute | solution.py:869
  412.4 5.2 copy-start.60
  412.4 5.2 copy-start.66
  412.4 5.2 copy-start.81
  417.6 5.0 copy-start.62
  417.6 5.0 copy-start.78
  417.6 5.0 copy-start.79
  687.7 5.6 copy-start.40
  697.7 5.1 copy-start.64
  (71 other events, 166.0 us)

commit v3 on v2

--- a/solution.py
+++ b/solution.py
@@ -31,16 +31,6 @@
     return lax.dot_general(left, right, COLS_CONTRACT, preferred_element_type=F32)
 
 
-def core_swap(value):
-    return lax.ppermute(value, "section", [(0, 1), (1, 0)])
-
-
-def ordered(flag, first, second, axis):
-    return jnp.concatenate(
-        [jnp.where(flag, first, second), jnp.where(flag, second, first)], axis=axis
-    )
-
-
 def norm_parts(inputs):
     mean = jnp.mean(inputs, axis=-1, keepdims=True)
     centered = inputs - mean
@@ -81,169 +71,6 @@
     if length == QTILE:
         return tail
     return jnp.concatenate([scores[: length - QTILE], tail], axis=0)
-
-
-def attend_kernel(block_ref, q_ref, k_ref, v_ref, out_ref, lse_ref):
-    block = block_ref[0]
-    rows = q_ref.shape[0]
-    for index in range(k_ref.shape[0] // rows):
-
-        @pl.when(block == index)
-        def _(index=index):
-            for tile in range(rows // QTILE):
-                span = pl.ds(tile * QTILE, QTILE)
-                length = index * rows + (tile + 1) * QTILE
-                keys = k_ref[:length, :]
-                values = v_ref[:length, :]
-                mixed = []
-                for head, part in enumerate(head_parts(q_ref[span, :])):
-                    scores = masked_scores(keys, part * BF(HEAD_DIM**-0.5), length)
-                    top = jnp.max(scores, axis=0, keepdims=True)
-                    probs = jnp.exp(scores - top)
-                    total = jnp.sum(probs, axis=0, keepdims=True)
-                    lse_ref[0, pl.ds(head, 1), span] = top + jnp.log(total)
-                    piece = rows_product(values, probs.astype(BF))
-                    piece = piece[head * HEAD_DIM : (head + 1) * HEAD_DIM]
-                    mixed.append(piece * (1.0 / total))
-                mixed = jnp.concatenate(mixed, axis=0)
-                out_ref[span, :] = jnp.transpose(mixed).astype(BF)
-
-
-def attend(block, query, keys, values):
-    rows, width = query.shape
-    pairs = width // 128
-    total = keys.shape[0]
-    return pl.pallas_call(
-        attend_kernel,
-        grid_spec=pltpu.PrefetchScalarGridSpec(
-            num_scalar_prefetch=1,
-            grid=(pairs,),
-            in_specs=[
-                pl.BlockSpec((rows, 128), lambda i, b: (0, i)),
-                pl.BlockSpec((total, 128), lambda i, b: (0, i)),
-                pl.BlockSpec((total, 128), lambda i, b: (0, i)),
-            ],
-            out_specs=[
-                pl.BlockSpec((rows, 128), lambda i, b: (0, i)),
-                pl.BlockSpec((1, 8, rows), lambda i, b: (i, 0, 0)),
-            ],
-        ),
-        out_shape=[
-            jax.ShapeDtypeStruct((rows, width), BF),
-            jax.ShapeDtypeStruct((pairs, 8, rows), F32),
-        ],
-        compiler_params=pltpu.CompilerParams(vmem_limit_bytes=VMEM_LIMIT),
-        cost_estimate=pl.CostEstimate(
-            flops=4 * rows * total * width, bytes_accessed=4 * total * width, transcendentals=0
-        ),
-        name="attend",
-    )(block, query, keys, values)
-
-
-def attend_back_kernel(
-    block_ref,
-    q_ref,
-    k_ref,
-    v_ref,
-    o_ref,
-    do_ref,
-    lse_ref,
-    pend_k_ref,
-    pend_v_ref,
-    dq_ref,
-    dk_ref,
-    dv_ref,
-    new_k_ref,
-    new_v_ref,
-    sum_k,
-    sum_v,
-):
-    block = block_ref[0]
-    rows = q_ref.shape[0]
-    scale = HEAD_DIM**-0.5
-    for index in range(k_ref.shape[0] // rows):
-
-        @pl.when(block == index)
-        def _(index=index):
-            end = (index + 1) * rows
-            if index == 0:
-                sum_k[:rows, :] = pend_k_ref[...]
-                sum_v[:rows, :] = pend_v_ref[...]
-            else:
-                sum_k[:end, :] = jnp.zeros((end, 128), F32)
-                sum_v[:end, :] = jnp.zeros((end, 128), F32)
-            for tile in range(rows // QTILE):
-                span = pl.ds(tile * QTILE, QTILE)
-                length = index * rows + (tile + 1) * QTILE
-                keys = k_ref[:length, :]
-                values = v_ref[:length, :]
-                grads = do_ref[span, :]
-                products = jnp.transpose(grads.astype(F32) * o_ref[span, :].astype(F32))
-                queries = head_parts(q_ref[span, :])
-                grads = head_parts(grads)
-                d_query = []
-                d_keys = d_values = None
-                for head in range(2):
-                    take = slice(head * HEAD_DIM, (head + 1) * HEAD_DIM)
-                    query = queries[head] * BF(scale)
-                    scores = masked_scores(keys, query, length)
-                    weights = jnp.exp(scores - lse_ref[0, pl.ds(head, 1), span])
-                    d_probs = cols_product(values, grads[head])
-                    delta = jnp.sum(products[take], axis=0, keepdims=True)
-                    d_scores = (weights * (d_probs - delta)).astype(BF)
-                    d_value = jnp.dot(weights.astype(BF), grads[head], preferred_element_type=F32)
-                    d_key = jnp.dot(d_scores, query, preferred_element_type=F32)
-                    d_values = d_value if head == 0 else d_values + d_value
-                    d_keys = d_key if head == 0 else d_keys + d_key
-                    d_query.append(rows_product(keys, d_scores)[take])
-                sum_k[:length, :] += d_keys
-                sum_v[:length, :] += d_values
-                d_query = jnp.concatenate(d_query, axis=0) * scale
-                dq_ref[span, :] = jnp.transpose(d_query).astype(BF)
-            dk_ref[...] = sum_k[index * rows : end, :].astype(BF)
-            dv_ref[...] = sum_v[index * rows : end, :].astype(BF)
-            if index == 0:
-                new_k_ref[...] = pend_k_ref[...]
-                new_v_ref[...] = pend_v_ref[...]
-            else:
-                new_k_ref[...] = sum_k[:rows, :]
-                new_v_ref[...] = sum_v[:rows, :]
-
-
-def attend_back(block, query, keys, values, mixed, d_mixed, lse, pending):
-    rows, width = query.shape
-    pairs = width // 128
-    total = keys.shape[0]
-    assert total == 2 * rows
-    small = pl.BlockSpec((rows, 128), lambda i, b: (0, i))
-    large = pl.BlockSpec((total, 128), lambda i, b: (0, i))
-    low = jax.ShapeDtypeStruct((rows, width), BF)
-    wide = jax.ShapeDtypeStruct((rows, width), F32)
-    return pl.pallas_call(
-        attend_back_kernel,
-        grid_spec=pltpu.PrefetchScalarGridSpec(
-            num_scalar_prefetch=1,
-            grid=(pairs,),
-            in_specs=[
-                small,
-                large,
-                large,
-                small,
-                small,
-                pl.BlockSpec((1, 8, rows), lambda i, b: (i, 0, 0)),
-                small,
-                small,
-            ],
-            out_specs=[small] * 5,
-            scratch_shapes=[pltpu.VMEM((total, 128), F32), pltpu.VMEM((total, 128), F32)],
-        ),
-        out_shape=[low, low, low, wide, wide],
-        compiler_params=pltpu.CompilerParams(vmem_limit_bytes=VMEM_LIMIT),
-        cost_estimate=pl.CostEstimate(
-            flops=10 * rows * total * width, bytes_accessed=8 * total * width, transcendentals=0
-        ),
-        name="attend_back",
-    )(block, query, keys, values, mixed, d_mixed, lse, *pending)
 
 
 def ring_place(size):
@@ -836,6 +663,573 @@
     )(tokens, cotangent, small, qkv, fc, out, proj)
 
 
+TILES = 2
+
+
+class Loads:
+    def __init__(self, sem):
+        self.sem, self.count, self.made = sem, 0, {}
+
+    def start(self, name, source, buffer):
+        copy = pltpu.make_async_copy(source, buffer, self.sem.at[self.count])
+        self.count += 1
+        copy.start()
+        self.made[name] = copy
+
+    def wait(self, *names):
+        for name in names:
+            self.made.pop(name).wait()
+
+
+def chosen_load(first_ref, other_ref, buffer, sem):
+    layer = lax.axis_index("shard")
+
+    @pl.when(layer == 0)
+    def _():
+        pltpu.make_async_copy(first_ref, buffer, sem).start()
+
+    @pl.when(layer != 0)
+    def _():
+        pltpu.make_async_copy(other_ref, buffer, sem).start()
+
+    return pltpu.make_async_copy(first_ref, buffer, sem)
+
+
+def greet_step(sender, passing):
+    core, layer, sibling, across, _ = neighbours()
+    barrier = pltpu.get_barrier_semaphore()
+    pl.semaphore_signal(barrier, inc=1, device_id=sibling, device_id_type=MESH)
+    if not passing:
+        pl.semaphore_wait(barrier, 1)
+        return
+
+    @pl.when(layer != sender)
+    def _():
+        pl.semaphore_signal(barrier, inc=1, device_id=across, device_id_type=MESH)
+        pl.semaphore_wait(barrier, 1)
+
+    @pl.when(layer == sender)
+    def _():
+        pl.semaphore_wait(barrier, 2)
+
+
+class Exchange:
+    def __init__(self, send_buf, recv_buf, send_sem, recv_sem):
+        self.refs = (send_buf, recv_buf, send_sem, recv_sem)
+
+    def copy(self, slot):
+        send_buf, recv_buf, send_sem, recv_sem = self.refs
+        return pltpu.make_async_remote_copy(
+            src_ref=send_buf.at[slot],
+            dst_ref=recv_buf.at[slot],
+            send_sem=send_sem.at[slot],
+            recv_sem=recv_sem.at[slot],
+            device_id={"section": 1 - lax.axis_index("section")},
+            device_id_type=MESH,
+        )
+
+    def give(self, slot, partial):
+        self.refs[0][slot] = partial.astype(BF)
+        self.copy(slot).start()
+
+    def take(self, slot):
+        self.copy(slot).wait_recv()
+        return self.refs[1][slot].astype(F32)
+
+    def finish(self, count):
+        for slot in range(count):
+            self.copy(slot).wait_send()
+
+
+class Across:
+    def __init__(self, sender, source, dest, sems):
+        self.sender, self.source, self.dest, self.sems = sender, source, dest, sems
+        self.core, self.layer, self.sibling, self.across, _ = neighbours()
+
+    def copy(self, tile, stage):
+        rows = self.dest.shape[0] // (2 * TILES)
+        place = pl.ds(pl.multiple_of((2 * tile + self.core) * rows, rows), rows)
+        source = self.source if stage == 0 else self.dest
+        return pltpu.make_async_remote_copy(
+            src_ref=source.at[place],
+            dst_ref=self.dest.at[place],
+            send_sem=self.sems.at[stage, tile],
+            recv_sem=self.sems.at[2 + stage, tile],
+            device_id=self.across if stage == 0 else self.sibling,
+            device_id_type=MESH,
+        )
+
+    def send(self, tile):
+        @pl.when(self.layer == self.sender)
+        def _():
+            self.copy(tile, 0).start()
+
+    def finish(self):
+        @pl.when(self.layer == self.sender)
+        def _():
+            for tile in range(TILES):
+                self.copy(tile, 0).wait_send()
+
+        @pl.when(self.layer != self.sender)
+        def _():
+            for tile in range(TILES):
+                self.copy(tile, 0).wait_recv()
+                self.copy(tile, 1).start()
+            for tile in range(TILES):
+                self.copy(tile, 1).wait()
+
+
+def by_past(mode, body):
+    if mode is not None:
+        body(mode)
+        return
+    layer = lax.axis_index("shard")
+
+    @pl.when(layer == 0)
+    def _():
+        body(True)
+
+    @pl.when(layer != 0)
+    def _():
+        body(False)
+
+
+FORWARD_LOADS = 7
+
+
+def forward_kernel(mode, passing, *refs):
+    x_first, x_other, params, w_qkv, w_out, w_fc, w_proj, k_past, v_past = refs[:9]
+    refs = refs[9:]
+    (normed1, query, keys, values, mixed, lse, scaled2, inverse2, normed2, slope, act, out, passed) = refs[:13]
+    refs = refs[13:]
+    (x_v, wq_v, wo_v, wf_v, wp_v, k_v, v_v, hid_v, part_v, send_v, recv_v) = refs[:11]
+    refs = refs[11:]
+    (n1_v, q_v, m_v, lse_v, s2_v, i2_v, n2_v, sl_v, a_v, o_v) = refs[:10]
+    load_sem, store_sem, send_sem, recv_sem, across_sem = refs[10:]
+    rows, width = x_v.shape
+    half = q_v.shape[1]
+    tile_rows = rows // TILES
+    wide = a_v.shape[1]
+
+    loads = Loads(load_sem)
+    load_x = chosen_load(x_first, x_other, x_v, load_sem.at[FORWARD_LOADS])
+    loads.start("qkv", w_qkv, wq_v)
+    if mode is not False:
+        loads.start("k", k_past, k_v.at[pl.ds(0, rows)])
+        loads.start("v", v_past, v_v.at[pl.ds(0, rows)])
+    loads.start("out", w_out, wo_v)
+    loads.start("fc", w_fc, wf_v)
+    loads.start("proj", w_proj, wp_v)
+    greet_step(0, passing)
+    exchange = Exchange(send_v, recv_v, send_sem, recv_sem)
+    across = Across(0, o_v, passed, across_sem)
+    stores = []
+
+    def store(buffer, dest):
+        copy = pltpu.make_async_copy(buffer, dest, store_sem.at[len(stores)])
+        copy.start()
+        stores.append(copy)
+
+    def vector(row, start=0, size=None):
+        return params[row : row + 1, start : start + (size or width)]
+
+    load_x.wait()
+    for tile in range(TILES):
+        span = pl.ds(tile * tile_rows, tile_rows)
+        scaled, _ = norm_parts(x_v[span, :].astype(F32))
+        n1_v[span, :] = (scaled * vector(0) + vector(1)).astype(BF)
+    store(n1_v, normed1)
+    loads.wait("qkv")
+    own_rows = pl.ds(rows, rows)
+    for tile in range(TILES):
+        span = pl.ds(tile * tile_rows, tile_rows)
+        later = pl.ds(rows + tile * tile_rows, tile_rows)
+        normed = n1_v[span, :]
+        piece = jnp.dot(normed, wq_v[:, :half], preferred_element_type=F32)
+        q_v[span, :] = (piece + vector(6, 0, half)).astype(BF)
+        piece = jnp.dot(normed, wq_v[:, half : 2 * half], preferred_element_type=F32)
+        k_v[later, :] = piece.astype(BF)
+        piece = jnp.dot(normed, wq_v[:, 2 * half :], preferred_element_type=F32)
+        v_v[later, :] = (piece + vector(6, half, half)).astype(BF)
+    store(q_v, query)
+    store(k_v.at[own_rows], keys)
+    store(v_v.at[own_rows], values)
+    if mode is not False:
+        loads.wait("k", "v")
+    loads.wait("out")
+
+    def attention(past):
+        first_key = 0 if past else rows
+        for tile in range(TILES):
+            span = pl.ds(tile * tile_rows, tile_rows)
+            length = (rows if past else 0) + (tile + 1) * tile_rows
+            reach = pl.ds(first_key, length)
+
+            def pair(number, carry):
+                lanes = pl.ds(pl.multiple_of(number * 128, 128), 128)
+                key, value = k_v[reach, lanes], v_v[reach, lanes]
+                pieces = []
+                for head, part in enumerate(head_parts(q_v[span, lanes])):
+                    scores = masked_scores(key, part * BF(HEAD_DIM**-0.5), length)
+                    top = jnp.max(scores, axis=0, keepdims=True)
+                    probs = jnp.exp(scores - top)
+                    total = jnp.sum(probs, axis=0, keepdims=True)
+                    lse_v[number, pl.ds(head, 1), span] = top + jnp.log(total)
+                    piece = rows_product(value, probs.astype(BF))
+                    piece = piece[head * HEAD_DIM : (head + 1) * HEAD_DIM]
+                    pieces.append(piece * (1.0 / total))
+                m_v[span, lanes] = jnp.transpose(jnp.concatenate(pieces, axis=0)).astype(BF)
+                return carry
+
+            lax.fori_loop(0, half // 128, pair, 0)
+            partial = jnp.dot(m_v[span, :], wo_v[...], preferred_element_type=F32)
+            part_v[tile] = partial
+            exchange.give(tile, partial)
+
+    by_past(mode, attention)
+    store(m_v, mixed)
+    store(lse_v, lse)
+    loads.wait("fc", "proj")
+    for tile in range(TILES):
+        span = pl.ds(tile * tile_rows, tile_rows)
+        hidden = x_v[span, :].astype(F32) + (part_v[tile] + exchange.take(tile)) + vector(2)
+        hid_v[span, :] = hidden
+        scaled, inverse = norm_parts(hidden)
+        s2_v[span, :] = scaled.astype(BF)
+        i2_v[span, :] = jnp.broadcast_to(inverse, (tile_rows, 128))
+        normed = (scaled * vector(3) + vector(4)).astype(BF)
+        n2_v[span, :] = normed
+        chunk = width // 2
+        for part in range(wide // chunk):
+            columns = pl.ds(part * chunk, chunk)
+            pre = jnp.dot(normed, wf_v[:, columns], preferred_element_type=F32)
+            bias = vector(7 + part * chunk // width, part * chunk % width, chunk)
+            activated, inclined = gelu_pair(pre + bias)
+            a_v[span, columns] = activated.astype(BF)
+            sl_v[span, columns] = inclined.astype(BF)
+        partial = jnp.dot(a_v[span, :], wp_v[...], preferred_element_type=F32)
+        part_v[TILES + tile] = partial
+        exchange.give(TILES + tile, partial)
+    store(s2_v, scaled2)
+    store(i2_v, inverse2)
+    store(n2_v, normed2)
+    store(sl_v, slope)
+    store(a_v, act)
+    for tile in range(TILES):
+        span = pl.ds(tile * tile_rows, tile_rows)
+        total = part_v[TILES + tile] + exchange.take(TILES + tile)
+        o_v[span, :] = (hid_v[span, :] + total + vector(5)).astype(BF)
+        if passing:
+            across.send(tile)
+    store(o_v, out)
+    for copy in stores:
+        copy.wait()
+    exchange.finish(2 * TILES)
+    if passing:
+        across.finish()
+
+
+def step_sems(loads, stores):
+    return [
+        pltpu.SemaphoreType.DMA((loads,)),
+        pltpu.SemaphoreType.DMA((stores,)),
+        pltpu.SemaphoreType.DMA((2 * TILES,)),
+        pltpu.SemaphoreType.DMA((2 * TILES,)),
+        pltpu.SemaphoreType.DMA((4, TILES)),
+    ]
+
+
+def forward_step(mode, passing, x_first, x_other, params, weights, past):
+    rows, width = x_first.shape
+    half = width // 2
+    wide = weights[2].shape[1]
+    pairs = half // 128
+    tile_rows = rows // TILES
+    spot = pl.BlockSpec(memory_space=pl.ANY)
+    low = lambda columns: ((rows, columns), BF)
+    outs = [
+        low(width),
+        low(half),
+        low(half),
+        low(half),
+        low(half),
+        ((pairs, 8, rows), F32),
+        low(width),
+        ((rows, 128), F32),
+        low(width),
+        low(wide),
+        low(wide),
+        low(width),
+        low(width),
+    ]
+    scratch = [
+        low(width),
+        *((item.shape, BF) for item in weights),
+        ((2 * rows, half), BF),
+        ((2 * rows, half), BF),
+        ((rows, width), F32),
+        ((2 * TILES, tile_rows, width), F32),
+        ((2 * TILES, tile_rows, width), BF),
+        ((2 * TILES, tile_rows, width), BF),
+        low(width),
+        low(half),
+        low(half),
+        ((pairs, 8, rows), F32),
+        low(width),
+        ((rows, 128), F32),
+        low(width),
+        low(wide),
+        low(wide),
+        low(width),
+    ]
+    number = {(False, True): 3, (None, True): 4, (True, False): 5}[(mode, passing)]
+    return pl.pallas_call(
+        functools.partial(forward_kernel, mode, passing),
+        out_shape=[jax.ShapeDtypeStruct(*item) for item in outs],
+        in_specs=[spot] * 2 + [pl.BlockSpec(memory_space=pltpu.VMEM)] + [spot] * 6,
+        out_specs=[spot] * len(outs),
+        scratch_shapes=[pltpu.VMEM(*item) for item in scratch]
+        + step_sems(FORWARD_LOADS + 1, len(outs)),
+        compiler_params=pltpu.CompilerParams(
+            collective_id=number, has_side_effects=True, vmem_limit_bytes=VMEM_LIMIT
+        ),
+        name="forward_step",
+    )(x_first, x_other, params, *weights, *past)
+
+
+BACKWARD_LOADS = 16
+
+
+def backward_kernel(mode, passing, *refs):
+    (g_first, g_other, x_first, x_other, params, w_qkv, w_out, w_fc, w_proj) = refs[:9]
+    (query, keys, values, k_past, v_past, mixed, lse, scaled2, inverse2, slope, pend_k, pend_v) = refs[9:21]
+    refs = refs[21:]
+    (d_qkv, d_branch, d_pre, out, next_k, next_v, sums, passed) = refs[:8]
+    refs = refs[8:]
+    (g_v, x_v, wq_v, wo_v, wf_v, wp_v, q_v, k_v, v_v, m_v, lse_v, s2_v, i2_v, sl_v) = refs[:14]
+    refs = refs[14:]
+    (dk_v, dv_v, hid_v, part_v, send_v, recv_v, dqkv_v, db_v, dp_v, dm_v, o_v, sum_v) = refs[:12]
+    load_sem, store_sem, send_sem, recv_sem, across_sem = refs[12:]
+    rows, width = x_v.shape
+    half = q_v.shape[1]
+    wide = dp_v.shape[1]
+    tile_rows = rows // TILES
+    own_rows, past_rows = pl.ds(rows, rows), pl.ds(0, rows)
+    scale = HEAD_DIM**-0.5
+
+    loads = Loads(load_sem)
+    load_g = chosen_load(g_first, g_other, g_v, load_sem.at[BACKWARD_LOADS])
+    loads.start("proj", w_proj, wp_v)
+    loads.start("slope", slope, sl_v)
+    loads.start("fc", w_fc, wf_v)
+    loads.start("scaled2", scaled2, s2_v)
+    loads.start("inverse2", inverse2, i2_v)
+    loads.start("out", w_out, wo_v)
+    loads.start("q", query, q_v)
+    loads.start("k", keys, k_v.at[own_rows])
+    loads.start("v", values, v_v.at[own_rows])
+    if mode is not False:
+        loads.start("k_past", k_past, k_v.at[past_rows])
+        loads.start("v_past", v_past, v_v.at[past_rows])
+    loads.start("mixed", mixed, m_v)
+    loads.start("lse", lse, lse_v)
+    if mode is not True:
+        loads.start("pend_k", pend_k, dk_v.at[own_rows])
+        loads.start("pend_v", pend_v, dv_v.at[own_rows])
+    loads.start("qkv", w_qkv, wq_v)
+    load_x = chosen_load(x_first, x_other, x_v, load_sem.at[BACKWARD_LOADS + 1])
+    greet_step(1, passing)
+    exchange = Exchange(send_v, recv_v, send_sem, recv_sem)
+    across = Across(1, o_v, passed, across_sem)
+    stores = []
+
+    def store(buffer, dest):
+        copy = pltpu.make_async_copy(buffer, dest, store_sem.at[len(stores)])
+        copy.start()
+        stores.append(copy)
+
+    def vector(row, start=0, size=None):
+        return params[row : row + 1, start : start + (size or width)]
+
+    sum_v[...] = jnp.zeros_like(sum_v)
+
+    def tally(row, piece, start=0):
+        place = (slice(row, row + 1), slice(start, start + piece.shape[1]))
+        sum_v[place] += jnp.sum(piece, axis=0, keepdims=True)
+
+    load_g.wait()
+    loads.wait("proj", "slope", "fc")
+    chunk = width // 2
+    for tile in range(TILES):
+        span = pl.ds(tile * tile_rows, tile_rows)
+        grad = g_v[span, :]
+        for part in range(wide // chunk):
+            columns = pl.ds(part * chunk, chunk)
+            d_act = cols_product(grad, wp_v[columns, :])
+            piece = (d_act * sl_v[span, columns].astype(F32)).astype(BF)
+            dp_v[span, columns] = piece
+            tally(7 + part * chunk // width, piece.astype(F32), part * chunk % width)
+        partial = cols_product(dp_v[span, :], wf_v[...])
+        part_v[tile] = partial
+        exchange.give(tile, partial)
+        tally(5, grad.astype(F32))
+    store(dp_v, d_pre)
+    loads.wait("scaled2", "inverse2", "out")
+    for tile in range(TILES):
+        span = pl.ds(tile * tile_rows, tile_rows)
+        d_normed = part_v[tile] + exchange.take(tile)
+        scaled = s2_v[span, :].astype(F32)
+        tally(3, d_normed * scaled)
+        tally(4, d_normed)
+        d_hidden = g_v[span, :].astype(F32) + norm_backward(
+            d_normed, scaled, i2_v[span, 0:1], vector(3)
+        )
+        hid_v[span, :] = d_hidden
+        branch = d_hidden.astype(BF)
+        db_v[span, :] = branch
+        tally(2, branch.astype(F32))
+        dm_v[span, :] = cols_product(branch, wo_v[...]).astype(BF)
+    store(db_v, d_branch)
+    loads.wait("q", "k", "v", "mixed", "lse")
+    if mode is not False:
+        loads.wait("k_past", "v_past")
+    if mode is not True:
+        loads.wait("pend_k", "pend_v")
+
+    def attention(past):
+        first_key = 0 if past else rows
+        if past:
+            dk_v[...] = jnp.zeros_like(dk_v)
+            dv_v[...] = jnp.zeros_like(dv_v)
+        for tile in range(TILES):
+            span = pl.ds(tile * tile_rows, tile_rows)
+            length = (rows if past else 0) + (tile + 1) * tile_rows
+            reach = pl.ds(first_key, length)
+
+            def pair(number, carry):
+                lanes = pl.ds(pl.multiple_of(number * 128, 128), 128)
+                key, value = k_v[reach, lanes], v_v[reach, lanes]
+                grads = dm_v[span, lanes]
+                products = jnp.transpose(grads.astype(F32) * m_v[span, lanes].astype(F32))
+                queries, grads = head_parts(q_v[span, lanes]), head_parts(grads)
+                d_query = []
+                d_key = d_value = None
+                for head in range(2):
+                    take = slice(head * HEAD_DIM, (head + 1) * HEAD_DIM)
+                    scaled_query = queries[head] * BF(scale)
+                    scores = masked_scores(key, scaled_query, length)
+                    weights = jnp.exp(scores - lse_v[number, pl.ds(head, 1), span])
+                    d_probs = cols_product(value, grads[head])
+                    delta = jnp.sum(products[take], axis=0, keepdims=True)
+                    d_scores = (weights * (d_probs - delta)).astype(BF)
+                    one = jnp.dot(weights.astype(BF), grads[head], preferred_element_type=F32)
+                    two = jnp.dot(d_scores, scaled_query, preferred_element_type=F32)
+                    d_value = one if head == 0 else d_value + one
+                    d_key = two if head == 0 else d_key + two
+                    d_query.append(rows_product(key, d_scores)[take])
+                dk_v[reach, lanes] += d_key
+                dv_v[reach, lanes] += d_value
+                d_query = jnp.transpose(jnp.concatenate(d_query, axis=0) * scale)
+                dqkv_v[span, lanes] = d_query.astype(BF)
+                return carry
+
+            lax.fori_loop(0, half // 128, pair, 0)
+
+    by_past(mode, attention)
+    if mode is not False:
+        store(dk_v.at[past_rows], next_k)
+        store(dv_v.at[past_rows], next_v)
+    loads.wait("qkv")
+    load_x.wait()
+    for tile in range(TILES):
+        span = pl.ds(tile * tile_rows, tile_rows)
+        later = pl.ds(rows + tile * tile_rows, tile_rows)
+        dqkv_v[span, half : 2 * half] = dk_v[later, :].astype(BF)
+        dqkv_v[span, 2 * half :] = dv_v[later, :].astype(BF)
+        piece = dqkv_v[span, :]
+        partial = cols_product(piece, wq_v[...])
+        part_v[TILES + tile] = partial
+        exchange.give(TILES + tile, partial)
+        tally(6, piece[:, :half].astype(F32))
+        tally(6, piece[:, 2 * half :].astype(F32), half)
+    store(dqkv_v, d_qkv)
+    for tile in range(TILES):
+        span = pl.ds(tile * tile_rows, tile_rows)
+        scaled, inverse = norm_parts(x_v[span, :].astype(F32))
+        d_normed = part_v[TILES + tile] + exchange.take(TILES + tile)
+        tally(0, d_normed * scaled)
+        tally(1, d_normed)
+        d_inputs = hid_v[span, :] + norm_backward(d_normed, scaled, inverse, vector(0))
+        o_v[span, :] = d_inputs.astype(BF)
+        if passing:
+            across.send(tile)
+    store(o_v, out)
+    store(sum_v, sums)
+    for copy in stores:
+        copy.wait()
+    exchange.finish(2 * TILES)
+    if passing:
+        across.finish()
+
+
+def backward_step(mode, passing, grads, inputs, params, weights, kept, pending):
+    rows, width = inputs[0].shape
+    half = width // 2
+    wide = weights[2].shape[1]
+    pairs = half // 128
+    tile_rows = rows // TILES
+    spot = pl.BlockSpec(memory_space=pl.ANY)
+    low = lambda columns: ((rows, columns), BF)
+    outs = [
+        low(3 * half),
+        low(width),
+        low(wide),
+        low(width),
+        ((rows, half), F32),
+        ((rows, half), F32),
+        ((16, width), F32),
+        low(width),
+    ]
+    scratch = [
+        low(width),
+        low(width),
+        *((item.shape, BF) for item in weights),
+        low(half),
+        ((2 * rows, half), BF),
+        ((2 * rows, half), BF),
+        low(half),
+        ((pairs, 8, rows), F32),
+        low(width),
+        ((rows, 128), F32),
+        low(wide),
+        ((2 * rows, half), F32),
+        ((2 * rows, half), F32),
+        ((rows, width), F32),
+        ((2 * TILES, tile_rows, width), F32),
+        ((2 * TILES, tile_rows, width), BF),
+        ((2 * TILES, tile_rows, width), BF),
+        low(3 * half),
+        low(width),
+        low(wide),
+        low(half),
+        low(width),
+        ((16, width), F32),
+    ]
+    number = {(True, True): 6, (None, True): 7, (False, False): 8}[(mode, passing)]
+    return pl.pallas_call(
+        functools.partial(backward_kernel, mode, passing),
+        out_shape=[jax.ShapeDtypeStruct(*item) for item in outs],
+        in_specs=[spot] * 4 + [pl.BlockSpec(memory_space=pltpu.VMEM)] + [spot] * 16,
+        out_specs=[spot] * len(outs),
+        scratch_shapes=[pltpu.VMEM(*item) for item in scratch]
+        + step_sems(BACKWARD_LOADS + 2, len(outs)),
+        compiler_params=pltpu.CompilerParams(
+            collective_id=number, has_side_effects=True, vmem_limit_bytes=VMEM_LIMIT
+        ),
+        name="backward_step",
+    )(*grads, *inputs, params, *weights, *kept, *pending)
+
+
 def shards(
     tokens,
     cotangent,
@@ -888,106 +1282,67 @@
         tokens[0], cotangent[0], small, qkv_weight[0], fc_weight[0], out_weight[0], proj_weight[0]
     )
     flat = small_both.reshape(2, -1).astype(F32)
-    full_small = jnp.concatenate(
-        [flat[0, : 6 * half].reshape(6, half), flat[1, : 6 * half].reshape(6, half)], axis=1
+    mine = jnp.where(left, flat[0], flat[1])
+    params = jnp.concatenate(
+        [
+            flat[0, : 6 * half].reshape(6, half),
+            flat[1, : 6 * half].reshape(6, half),
+        ],
+        axis=1,
     )
-    gain1, shift1, bias_o, gain2, shift2, bias_p = (full_small[i] for i in range(6))
-    flat = jnp.where(left, flat[0], flat[1])
-    bias_q = flat[6 * half : 7 * half]
-    bias_v = flat[7 * half : 8 * half]
-    bias_f = flat[8 * half :]
-
-    def exchanged(partial):
-        return partial + core_swap(partial.astype(BF)).astype(F32)
-
-    def passed(value, pairs):
-        give = lax.dynamic_slice_in_dim(value, core * part, part, 0)
-        got = lax.ppermute(give, "shard", pairs)
-        return ordered(left, got, core_swap(got), 0)
-
-    keys_all = jnp.zeros((micro * rows, half), BF)
-    values_all = jnp.zeros((micro * rows, half), BF)
-    received = [jnp.zeros((rows, width), BF)]
-    kept_list, outputs = [], []
+    params = jnp.concatenate(
+        [params, mine[6 * half :].reshape(-1, width), jnp.zeros((7, width), F32)], axis=0
+    )
+    weights = (w_qkv, w_out, w_fc, w_proj)
+
+    empty = jnp.zeros((rows, half), BF)
+    received, kept_list, outputs, past = [outer[0]], [], [], (empty, empty)
     for step in range(micro + 1):
-        index = jnp.where(first, min(step, micro - 1), max(step - 1, 0)).astype(jnp.int32)
-        inputs = jnp.where(first, outer[min(step, micro - 1)], received[step])
-        scaled1, inverse1 = norm_parts(inputs.astype(F32))
-        normed1 = (scaled1 * gain1 + shift1).astype(BF)
-        qkv = jnp.dot(normed1, w_qkv, preferred_element_type=F32)
-        query = (qkv[:, :half] + bias_q).astype(BF)
-        keys = qkv[:, half : 2 * half].astype(BF)
-        values = (qkv[:, 2 * half :] + bias_v).astype(BF)
-        keys_all = lax.dynamic_update_slice_in_dim(keys_all, keys, index * rows, 0)
-        values_all = lax.dynamic_update_slice_in_dim(values_all, values, index * rows, 0)
-        mixed, lse = attend(index[None], query, keys_all, values_all)
-        partial = jnp.dot(mixed, w_out, preferred_element_type=F32)
-        hidden = inputs.astype(F32) + exchanged(partial) + bias_o
-        scaled2, inverse2 = norm_parts(hidden)
-        normed2 = (scaled2 * gain2 + shift2).astype(BF)
-        pre = jnp.dot(normed2, w_fc, preferred_element_type=F32) + bias_f
-        activated, slope = gelu_pair(pre)
-        act = activated.astype(BF)
-        partial = jnp.dot(act, w_proj, preferred_element_type=F32)
-        output = (hidden + exchanged(partial) + bias_p).astype(BF)
+        mode = (False, None, True)[step]
+        normed1, query, keys, values, mixed, lse, scaled2, inverse2, normed2, slope, act, output, got = (
+            forward_step(
+                mode,
+                step < micro,
+                outer[min(step, micro - 1)],
+                received[step],
+                params,
+                weights,
+                past,
+            )
+        )
         outputs.append(output)
-        kept_list.append(
-            (inputs, normed1, query, lse, mixed, scaled2.astype(BF), inverse2, normed2,
-             slope.astype(BF), act)
-        )
-        if step < micro:
-            received.append(passed(output, [(0, 1)]))
+        kept = (query, keys, values, *past, mixed, lse, scaled2, inverse2, slope)
+        kept_list.append((kept, normed1, normed2, act))
+        past = (keys, values)
+        received.append(got)
 
     pending = (jnp.zeros((rows, half), F32), jnp.zeros((rows, half), F32))
-    grad_received = [jnp.zeros((rows, width), BF)]
+    grad_received = [outer[0]]
     terms_list, results, sums = [], [], None
     for step in range(micro + 1):
-        index = jnp.where(first, min(micro - step, micro - 1), max(micro - 1 - step, 0)).astype(
-            jnp.int32
+        mode = (True, None, False)[step]
+        active = jnp.where(first, step >= 1, step < micro)
+        last = micro - step
+        kept, normed1, normed2, act = kept_list[last]
+        grads = (grad_received[step], outer[max(micro - 1 - step, 0)])
+        d_qkv, d_branch, d_pre, result, *pending, vector, got = backward_step(
+            mode,
+            step < micro,
+            grads,
+            (outer[min(last, micro - 1)], received[last]),
+            params,
+            weights,
+            kept,
+            pending,
         )
-        active = jnp.where(first, 1.0 if step >= 1 else 0.0, 1.0 if step < micro else 0.0)
-        grad = jnp.where(first, grad_received[step], outer[max(micro - 1 - step, 0)])
-        inputs, normed1, query, lse, mixed, scaled2, inverse2, normed2, slope, act = kept_list[
-            micro - step
-        ]
-        d_pre = (cols_product(grad, w_proj) * slope.astype(F32)).astype(BF)
-        d_normed2 = exchanged(cols_product(d_pre, w_fc))
-        scaled2 = scaled2.astype(F32)
-        d_hidden = grad.astype(F32) + norm_backward(d_normed2, scaled2, inverse2, gain2)
-        d_branch = d_hidden.astype(BF)
-        d_mixed = cols_product(d_branch, w_out).astype(BF)
-        d_query, d_keys, d_values, *pending = attend_back(
-            index[None], query, keys_all, values_all, mixed, d_mixed, lse, pending
-        )
-        d_qkv = jnp.concatenate([d_query, d_keys, d_values], axis=1)
-        d_normed1 = exchanged(cols_product(d_qkv, w_qkv))
-        scaled1, inverse1 = norm_parts(inputs.astype(F32))
-        d_inputs = d_hidden + norm_backward(d_normed1, scaled1, inverse1, gain1)
-        result = d_inputs.astype(BF)
         results.append(result)
-        if step < micro:
-            grad_received.append(passed(result, [(1, 0)]))
-        full = jnp.stack(
-            [
-                jnp.sum(d_normed1 * scaled1, axis=0),
-                jnp.sum(d_normed1, axis=0),
-                jnp.sum(d_branch.astype(F32), axis=0),
-                jnp.sum(d_normed2 * scaled2, axis=0),
-                jnp.sum(d_normed2, axis=0),
-                jnp.sum(grad.astype(F32), axis=0),
-            ]
-        )
-        full = lax.dynamic_slice_in_dim(full, core * half, half, 1)
-        vector = jnp.concatenate(
-            [
-                full.reshape(-1),
-                jnp.sum(d_query.astype(F32), axis=0),
-                jnp.sum(d_values.astype(F32), axis=0),
-                jnp.sum(d_pre.astype(F32), axis=0),
-            ]
-        )
-        sums = active * vector if sums is None else sums + active * vector
-        terms_list.append((normed1, d_qkv, mixed, d_branch, normed2, d_pre, act, grad))
+        grad_received.append(got)
+        vector = jnp.where(active, vector, 0.0)
+        sums = vector if sums is None else sums + vector
+        grad = jnp.where(first, *grads)
+        terms_list.append((normed1, d_qkv, kept[5], d_branch, normed2, d_pre, act, grad))
+    full = lax.dynamic_slice_in_dim(sums[:6], core * half, half, 1)
+    sums = jnp.concatenate([full.reshape(-1), sums[6:9].reshape(-1)])
 
     late = [jnp.where(first, a, b) for a, b in zip(terms_list[2], terms_list[0])]
     both = [jnp.concatenate([a, b], axis=0) for a, b in zip(terms_list[1], late)]

time: 714 us -> 638 us (0.89)
  Pallas kernels: 399 us -> 542 us
  matrix products: 97.7 us -> 20 us
  waiting for transfers between devices: 66.4 us -> 0.01 us
  other arithmetic: 77.7 us -> 35.1 us
  starting transfers between devices: 23.7 us -> 7.51 us
  local copies, waits for them, and re-layouts: 39.4 us -> 27.7 us
    pallas_call x6, Pallas kernels: 66.5 us -> 210 us  [the longest x3 109 us: backward_step(): pl.pallas_call(functools.partial(backward_kernel, mode, passing), out_sha...]
    dot_general x24 -> x0, matrix products: 80.1 us -> none  [the longest x12 43 us: cols_product(): lax.dot_general(left, right, COLS_CONTRACT, preferred_element_type=F32)]
    ppermute x20 -> x0, waiting for transfers between devices: 60.7 us -> none  [the longest x4 41 us: passed(): got = lax.ppermute(give, 'shard', pairs)]
    reduce_sum x30 -> x0, other arithmetic: 19.2 us -> none  [the longest x6 4.09 us: norm_parts(): mean = jnp.mean(inputs, axis=-1, keepdims=True)]
    unnamed x236 -> x92, local copies, waits for them, and re-layouts: 27.9 us -> 10.8 us
    ppermute x20 -> x0, starting transfers between devices: 15.6 us -> none  [the longest x4 8.38 us: passed(): got = lax.ppermute(give, 'shard', pairs)]
    select_n x4 -> x7, other arithmetic: 10.9 us -> 0.98 us  [shards(): jnp.where(first, a, b)]
    convert_element_type x8 -> x0, other arithmetic: 8.69 us -> none  [the longest x1 3.09 us: shards(): output = (hidden + exchanged(partial) + bias_p).astype(BF)]
  transfers between devices with their start and end apart: 25 -> 5, of which waited for: 14 -> 0; matrix products, arithmetic and copies ran while one was open for 12% -> 9% of each run, Pallas kernels for 38% -> 58%
where the time goes in v3:
time: 638 us; the launch traced here: 634 us
  Pallas kernels  542 us (85%)
  other arithmetic  35.1 us (6%)
  local copies, waits for them, and re-layouts  27.7 us (4%)
  matrix products  20 us (3%)
  starting transfers between devices  7.51 us (1%)
    pallas_call x1, Pallas kernels, ring_gather(): pl.pallas_call(functools.partial(gather_kernel, size, groups), out_shape=...  131 us
    pallas_call x1, Pallas kernels, ring_scatter(): pl.pallas_call(functools.partial(scatter_kernel, size, count), out_shape=...  127 us
    pallas_call x3, Pallas kernels, backward_step(): pl.pallas_call(functools.partial(backward_kernel, mode, passing), out_sha...  109 us
    pallas_call x3, Pallas kernels, forward_step(): pl.pallas_call(functools.partial(forward_kernel, mode, passing), out_shap...  101 us
    pallas_call x1, Pallas kernels, fetch_inputs(): pl.pallas_call(fetch_kernel, out_shape=[jax.ShapeDtypeStruct(shape, BF) f...  74.6 us
    dot_general x4, matrix products, rows_product(): lax.dot_general(left, right, ROWS_CONTRACT, preferred_element_type=F32)  20 us
    reshape x4, other arithmetic, shards(): item.astype(F32).reshape(1, -1, item.shape[-1])  16 us
  transfers between devices with their start and end apart: 5, of which 0 were waited for; matrix products, arithmetic and copies ran while one was open for 9% of the time, Pallas kernels for 58%

profile of v3, /device:TPU:1, one launch (start us, length us, event | category | flops | bytes accessed | tf_op | source)
XLA Modules:
  0.0 634.0 jit_solution(5727350826367650384)
XLA Ops:
  0.7 0.7 reduce
  1.4 0.7 reduce.1
  2.1 0.7 reduce.6
  2.8 0.7 reduce.7
  3.5 0.7 reduce.2
  4.2 0.7 reduce.3
  4.9 0.7 reduce.4
  5.6 0.7 reduce.5
  6.3 0.7 reduce.8
  8.7 0.6 copy-done.34
  9.3 74.6 %fetch_inputs.1 = (bf16[2,512,1024]{2,1,0:T(8,128)(2,1)}, bf16[2,48,128]{2,1,0:T(8,128)(2,1)}, bf16[1024,1536]{1,0:T(8,128)(2,1)}, bf16[1024,2048]{1,0:T(8,128)(...) custom-call(bf16[2,256,1024]{2,1,0:T(8,128)(2,1)} %bitcast.83, bf16[2,256,1024]{2,1,0:T(8,128)(2,1)} %bitcast.84, ...), custom_call_target="tpu_custom_call" | custom-call | tf_op jit(solution)/shard_map/fetch_inputs/pallas_call | solution.py:638
  84.0 0.7 convert_bitcast_fusion
  84.9 3.0 slice_bitcast_fusion.1
  88.0 0.7 maximum_maximum_fusion.refs_2_.refs_4_
  88.7 0.8 broadcast_in_dim.46.refs_7_.refs_8_.refs_12_.refs_13_
  89.5 32.1 %forward_step.3 = (bf16[512,1024]{1,0:T(8,128)(2,1)}, bf16[512,512]{1,0:T(8,128)(2,1)}, bf16[512,512]{1,0:T(8,128)(2,1)}, bf16[512,512]{1,0:T(8,128)(2,1)}, bf16...) custom-call(bf16[512,1024]{1,0:T(8,128)(2,1)} %get-tuple-element.167, ...), custom_call_target="tpu_custom_call" | custom-call | tf_op jit(solution)/shard_map/forward_step/pallas_call | solution.py:986
  121.6 39.9 %forward_step.4 = (bf16[512,1024]{1,0:T(8,128)(2,1)}, bf16[512,512]{1,0:T(8,128)(2,1)}, bf16[512,512]{1,0:T(8,128)(2,1)}, bf16[512,512]{1,0:T(8,128)(2,1)}, bf16...) custom-call(bf16[512,1024]{1,0:T(8,128)(2,1)} %get-tuple-element.168, ...), custom_call_target="tpu_custom_call" | custom-call | tf_op jit(solution)/shard_map/forward_step/pallas_call | solution.py:986
  161.6 28.7 %forward_step.5 = (bf16[512,1024]{1,0:T(8,128)(2,1)}, bf16[512,512]{1,0:T(8,128)(2,1)}, bf16[512,512]{1,0:T(8,128)(2,1)}, bf16[512,512]{1,0:T(8,128)(2,1)}, bf16...) custom-call(bf16[512,1024]{1,0:T(8,128)(2,1)} %get-tuple-element.168, ...), custom_call_target="tpu_custom_call" | custom-call | tf_op jit(solution)/shard_map/forward_step/pallas_call | solution.py:986
  190.5 0.9 constant_dynamic-slice_fusion.2
  191.4 1.3 collective-permute-start.1
  192.7 0.8 constant_dynamic-slice_fusion.4
  193.5 1.3 collective-permute-start
  194.8 1.1 broadcast_1_refs_19__refs_20_.2.refs_19_.refs_20_
  195.9 48.9 %backward_step.3 = (bf16[512,1536]{1,0:T(8,128)(2,1)}, bf16[512,1024]{1,0:T(8,128)(2,1)}, bf16[512,2048]{1,0:T(8,128)(2,1)}, bf16[512,1024]{1,0:T(8,128)(2,1)}, ...) custom-call(bf16[512,1024]{1,0:T(8,128)(2,1)} %get-tuple-element.167.refs_0_.refs_1_.re, ...), custom_call_target="tpu_custom_call" | custom-call | tf_op jit(solution)/shard_map/backward_step/pallas_call | solution.py:1219
  244.8 34.9 %backward_step.4 = (bf16[512,1536]{1,0:T(8,128)(2,1)}, bf16[512,1024]{1,0:T(8,128)(2,1)}, bf16[512,2048]{1,0:T(8,128)(2,1)}, bf16[512,1024]{1,0:T(8,128)(2,1)}, ...) custom-call(bf16[512,1024]{1,0:T(8,128)(2,1)} %get-tuple-element.112.refs_0_, ...), custom_call_target="tpu_custom_call" | custom-call | tf_op jit(solution)/shard_map/backward_step/pallas_call | solution.py:1219
  279.7 25.2 %backward_step.5 = (bf16[512,1536]{1,0:T(8,128)(2,1)}, bf16[512,1024]{1,0:T(8,128)(2,1)}, bf16[512,2048]{1,0:T(8,128)(2,1)}, bf16[512,1024]{1,0:T(8,128)(2,1)}, ...) custom-call(bf16[512,1024]{1,0:T(8,128)(2,1)} %get-tuple-element.121.refs_0_, ...), custom_call_target="tpu_custom_call" | custom-call | tf_op jit(solution)/shard_map/backward_step/pallas_call | solution.py:1219
  305.0 0.9 select_add_fusion
  305.9 1.9 collective-permute-start.4
  307.9 1.9 broadcast_select_fusion.8
  309.8 0.8 constant_dynamic-slice_fusion.3
  310.6 1.6 collective-permute-start.3
  312.2 0.8 constant_dynamic-slice_fusion.1
  313.1 1.4 collective-permute-start.2
  314.9 1.3 copy-done.13
  316.2 0.6 copy-done.14
  317.1 1.0 copy-done.23
  318.1 0.3 copy-done.25
  318.7 0.3 copy-done.24
  319.2 0.6 copy-done.26
  320.2 0.6 copy-done.15
  320.8 0.6 copy-done.16
  321.7 1.2 copy-done.19
  322.8 0.5 copy-done.20
  323.5 0.6 copy-done.36
  324.3 6.5 %fusion.11 = bf16[1024,2048]{1,0:T(8,128)(2,1)} fusion(bf16[512,2048]{1,0:T(8,128)(2,1)S(1)} %broadcast_select_fusion.1, bf16[512,2048]{1,0:T(8,128)(2,1)S(1)} %copy-done.36, bf16[512,1024]{1,0:T(8,128)(2,1)S(1)} %broadcast_select_fusion.5, bf16[512,1024]{1,0:T(8,128)(2,1)S(1)} %copy-done.39), kind=kOutput, calls=%fused_computation.12 | convolution fusion | flops 4309647360 | bytes 10485760 | tf_op jit(solution)/shard_map/dot_general | solution.py:27
  330.8 5.0 convolution_convert_fusion
  335.8 6.2 fusion.8
  342.0 2.2 fusion.30
  344.3 2.3 copy.37
  346.6 4.8 copy.36
  351.4 0.6 broadcast_select_fusion.12.refs_4_
  352.0 127.0 %ring_scatter.1 = (bf16[2,64,1536]{2,1,0:T(8,128)(2,1)}, bf16[2,64,2048]{2,1,0:T(8,128)(2,1)}, bf16[2,32,1024]{2,1,0:T(8,128)(2,1)}, bf16[2,128,1024]{2,1,0:T(8,128)(2,1)}, f32[8,48,128]{2,1,0:T(8,128)}) custom-call(bf16[2,8,64,1536]{3,2,1,0:T(8,128)(2,1)} %bitcast.78, bf16[2,8,64,2048]{3,2,1,0:T(8,128)(2,1)} %bitcast.73, bf16[2,8,32,1024]{3,2,1,0:T(8,128)(2,1)} %bitcast.77, ...), custom_call_target="tpu_custom_call" | custom-call | tf_op jit(solution)/shard_map/ring_scatter/pallas_call | solution.py:180
  479.0 0.9 reduce_sum.9
  480.0 0.6 slice.111
  480.6 130.8 %ring_gather.1 = (bf16[8,64,3072]{2,1,0:T(8,128)(2,1)}, bf16[8,64,4096]{2,1,0:T(8,128)(2,1)}, bf16[8,64,1024]{2,1,0:T(8,128)(2,1)}, bf16[8,256,1024]{2,1,0:T(8,128)(2,1)}) custom-call(bf16[2,64,1536]{2,1,0:T(8,128)(2,1)} %get-tuple-element.155.refs_0_, bf16[2,64,2048]{2,1,0:T(8,128)(2,1)} %get-tuple-element.156.refs_1_, ...), custom_call_target="tpu_custom_call" | custom-call | tf_op jit(solution)/shard_map/ring_gather/pallas_call | solution.py:334
  611.4 5.5 bitcast_convert_fusion.2
  617.0 4.5 bitcast_convert_fusion.1
  621.5 4.4 bitcast_convert_fusion
  625.9 0.6 fusion.40
  626.5 1.6 bitcast_convert_fusion.3
  628.1 1.4 select_bitcast_fusion.2
  629.6 1.4 select_bitcast_fusion.3
  631.0 1.1 maximum_bitcast_fusion
  632.6 1.1 maximum_bitcast_fusion.1
  (111 shorter events, 5.0 us)
Async XLA Ops:
  8.7 0.6 copy-start.34
  161.6 28.7 %copy-start.29 = (bf16[512,1024]{1,0:T(8,128)(2,1)S(1)}, bf16[512,1024]{1,0:T(8,128)(2,1)}, u32[]{:S(2)}) copy-start(bf16[512,1024]{1,0:T(8,128)(2,1)} %get-tuple-element.95) | copy-start | bytes 3145732
  161.6 28.7 %copy-start.30 = (bf16[512,1024]{1,0:T(8,128)(2,1)S(1)}, bf16[512,1024]{1,0:T(8,128)(2,1)}, u32[]{:S(2)}) copy-start(bf16[512,1024]{1,0:T(8,128)(2,1)} %get-tuple-element.99) | copy-start | bytes 3145732
  190.5 54.3 %copy-start.7 = (bf16[512,1024]{1,0:T(8,128)(2,1)}, bf16[512,1024]{1,0:T(8,128)(2,1)S(1)}, u32[]{:S(2)}) copy-start(bf16[512,1024]{1,0:T(8,128)(2,1)S(1)} %get-tuple-element.172) | copy-start | bytes 3145732
  191.4 436.7 %collective-permute-start.1 = (bf16[256,1024]{1,0:T(8,128)(2,1)}, bf16[256,1024]{1,0:T(8,128)(2,1)}, u32[]{:S(2)}, u32[]{:S(2)}) collective-permute-start(bf16[256,1024]{1,0:T(8,128)(2,1)} %constant_dynamic-slice_fusion.2), channel_id=1, source_target_pairs={{24,16},{25,17},{26,18},{27,19},{28,20},{29,21},{30,22},{31,23}} | collective-permute-start | bytes 1572872 | tf_op jit(solution)/shard_map/ppermute | solution.py:1263
  193.5 436.0 %collective-permute-start = (bf16[256,1024]{1,0:T(8,128)(2,1)}, bf16[256,1024]{1,0:T(8,128)(2,1)}, u32[]{:S(2)}, u32[]{:S(2)}) collective-permute-start(bf16[256,1024]{1,0:T(8,128)(2,1)} %constant_dynamic-slice_fusion.4), channel_id=1, source_target_pairs={{24,16},{25,17},{26,18},{27,19},{28,20},{29,21},{30,22},{31,23}} | collective-permute-start | bytes 1572872 | tf_op jit(solution)/shard_map/ppermute | solution.py:1263
  279.7 25.2 %copy-start.32 = (f32[16,1024]{1,0:T(8,128)S(1)}, f32[16,1024]{1,0:T(8,128)}, u32[]{:S(2)}) copy-start(f32[16,1024]{1,0:T(8,128)} %get-tuple-element.151) | copy-start | bytes 196612
  279.7 25.2 %copy-start.33 = (f32[16,1024]{1,0:T(8,128)S(1)}, f32[16,1024]{1,0:T(8,128)}, u32[]{:S(2)}) copy-start(f32[16,1024]{1,0:T(8,128)} %get-tuple-element.152) | copy-start | bytes 196612
  279.7 28.1 %copy-start.28 = (bf16[512,1024]{1,0:T(8,128)(2,1)S(1)}, bf16[512,1024]{1,0:T(8,128)(2,1)}, u32[]{:S(2)}) copy-start(bf16[512,1024]{1,0:T(8,128)(2,1)} %get-tuple-element.132) | copy-start | bytes 3145732
  305.9 45.4 %collective-permute-start.4 = (f32[48,128]{1,0:T(8,128)S(1)}, f32[48,128]{1,0:T(8,128)S(1)}, u32[]{:S(2)}, u32[]{:S(2)}) collective-permute-start(f32[48,128]{1,0:T(8,128)S(1)} %constant_dynamic-update-slice_fusion.1), channel_id=1, source_target_pairs={{8,16},{16,8},{9,17},{17,9},{10,18},{18,10},{11,19},{19,11},{12,20... | collective-permute-start | bytes 73736 | tf_op jit(solution)/shard_map/ppermute | solution.py:1263
  307.9 6.6 %copy-start.17 = (bf16[512,512]{1,0:T(8,128)(2,1)S(1)}, bf16[512,512]{1,0:T(8,128)(2,1)}, u32[]{:S(2)}) copy-start(bf16[512,512]{1,0:T(8,128)(2,1)} %get-tuple-element.123.refs_14_) | copy-start | bytes 1572868
  307.9 6.6 %copy-start.18 = (bf16[512,512]{1,0:T(8,128)(2,1)S(1)}, bf16[512,512]{1,0:T(8,128)(2,1)}, u32[]{:S(2)}) copy-start(bf16[512,512]{1,0:T(8,128)(2,1)} %get-tuple-element.107.refs_14_) | copy-start | bytes 1572868
  307.9 6.7 %copy-start.2 = (bf16[512,1024]{1,0:T(8,128)(2,1)S(1)}, bf16[512,1024]{1,0:T(8,128)(2,1)}, u32[]{:S(2)}) copy-start(bf16[512,1024]{1,0:T(8,128)(2,1)} %get-tuple-element.121.refs_0_) | copy-start | bytes 3145732
  309.8 2.5 copy-start.9
  309.8 3.3 copy-start.11
  309.8 4.8 copy-start
  309.8 4.8 copy-start.1
  310.6 321.4 %collective-permute-start.3 = (bf16[256,1024]{1,0:T(8,128)(2,1)}, bf16[256,1024]{1,0:T(8,128)(2,1)}, u32[]{:S(2)}, u32[]{:S(2)}) collective-permute-start(bf16[256,1024]{1,0:T(8,128)(2,1)} %constant_dynamic-slice_fusion.3), channel_id=1, source_target_pairs={{0,8},{1,9},{2,10},{3,11},{4,12},{5,13},{6,14},{7,15}} | collective-permute-start | bytes 1572872 | tf_op jit(solution)/shard_map/ppermute | solution.py:1263
  313.1 319.3 %collective-permute-start.2 = (bf16[256,1024]{1,0:T(8,128)(2,1)}, bf16[256,1024]{1,0:T(8,128)(2,1)}, u32[]{:S(2)}, u32[]{:S(2)}) collective-permute-start(bf16[256,1024]{1,0:T(8,128)(2,1)} %constant_dynamic-slice_fusion.1), channel_id=1, source_target_pairs={{0,8},{1,9},{2,10},{3,11},{4,12},{5,13},{6,14},{7,15}} | collective-permute-start | bytes 1572872 | tf_op jit(solution)/shard_map/ppermute | solution.py:1263
  314.6 1.6 copy-start.13
  314.6 2.2 copy-start.14
  316.8 1.2 copy-start.23
  316.8 1.5 copy-start.25
  317.0 1.7 copy-start.22
  317.1 2.0 copy-start.24
  318.4 1.4 copy-start.26
  318.4 1.7 copy-start.27
  319.1 1.7 copy-start.15
  319.1 2.4 copy-start.16
  321.4 1.4 copy-start.19
  321.4 1.9 copy-start.20
  321.7 2.4 copy-start.36
  321.7 2.6 copy-start.39
  324.3 6.5 %copy-start.37 = (bf16[512,1536]{1,0:T(8,128)(2,1)S(1)}, bf16[512,1536]{1,0:T(8,128)(2,1)}, u32[]{:S(2)}) copy-start(bf16[512,1536]{1,0:T(8,128)(2,1)} %get-tuple-element.136) | copy-start | bytes 4718596
  324.3 6.5 %copy-start.38 = (bf16[512,1024]{1,0:T(8,128)(2,1)S(1)}, bf16[512,1024]{1,0:T(8,128)(2,1)}, u32[]{:S(2)}) copy-start(bf16[512,1024]{1,0:T(8,128)(2,1)} %get-tuple-element.133) | copy-start | bytes 3145732
  330.7 5.0 copy-start.35
  335.8 6.2 copy-start.31
  335.8 6.2 copy-start.40
  611.4 5.6 copy-start.6
  617.0 4.5 copy-start.5
  621.5 5.1 copy-start.21
  625.9 2.2 copy-start.4
  625.9 2.2 copy-start.8
  625.9 3.6 copy-start.3
  628.1 3.9 copy-start.12
  629.5 2.8 copy-start.10

commit v4 on v3

--- a/solution.py
+++ b/solution.py
@@ -102,13 +102,37 @@
 
 
 def scatter_kernel(size, count, *refs):
-    own, refs = refs[: count + 1], refs[count + 1 :]
+    sources, refs = refs[: 6 * count], refs[6 * count :]
+    small, refs = refs[0], refs[1:]
     out, refs = refs[: count + 1], refs[count + 1 :]
+    held, refs = refs[: 2 * count], refs[2 * count :]
+    own, refs = refs[:count], refs[count:]
     landed, refs = refs[:count], refs[count:]
-    send_sem, recv_sem, small_send, small_recv = refs
-    small, small_out = own[count], out[count]
+    load_sem, send_sem, recv_sem, small_send, small_recv = refs
+    small_out = out[count]
     place, following, previous = ring_place(size)
     targets = ({"replica": following}, {"replica": previous})
+    layer = lax.axis_index("shard")
+
+    def load(number, which):
+        rows = held[number].shape[0] // 2
+        source = sources[3 * number + which]
+        part = pl.ds(0 if which == 1 else rows, rows)
+        return pltpu.make_async_copy(
+            source, held[number].at[part], load_sem.at[number, 0 if which == 1 else 1]
+        )
+
+    for number in range(2 * count):
+        load(number, 1).start()
+
+        @pl.when(layer == 0)
+        def _(number=number):
+            load(number, 0).start()
+
+        @pl.when(layer != 0)
+        def _(number=number):
+            load(number, 2).start()
+
     greet(targets)
 
     def send(way, item, source, slot):
@@ -136,11 +160,29 @@
             return (place + 2 * size - 2 - slot) % size
         return (place + 2 + slot) % size
 
-    for item in range(count):
-        send(0, item, own[item].at[0, (place + size - 1) % size], 0).start()
-        send(1, item, own[item].at[1, (place + 1) % size], 0).start()
+    first = ((place + size - 1) % size, (place + 1) % size)
+    group = size // 2
+
+    def product(item, way, part):
+        deep = own[item].shape[2]
+        columns = pl.multiple_of((way * size + part * group) * deep, 128)
+        left = held[2 * item][:, pl.ds(columns, group * deep)]
+        result = rows_product(left, held[2 * item + 1][...])
+        for index in range(group):
+            own[item][way, part * group + index] = result[index * deep : (index + 1) * deep].astype(BF)
+
     small_out[place] = small[...]
     send_small(place, 0).start()
+    for item in range(count):
+        for number in (2 * item, 2 * item + 1):
+            load(number, 1).wait()
+            load(number, 0).wait()
+        for way in range(2):
+            product(item, way, first[way] // group)
+            send(way, item, own[item].at[way, first[way]], 0).start()
+    for item in range(count):
+        for way in range(2):
+            product(item, way, 1 - first[way] // group)
 
     def step(slot, carry):
         for item in range(count):
@@ -173,24 +215,32 @@
     lax.fori_loop(0, size - 1, finish, 0)
 
 
-def ring_scatter(pieces, small):
-    size = pieces[0].shape[1]
-    count = len(pieces)
+def ring_scatter(factors, small, size):
+    count = len(factors)
+    flat = [item for pair in factors for item in pair]
+    shapes = [(2 * item[0].shape[0], item[0].shape[1]) for item in flat]
+    chunks = [
+        (shapes[2 * i][1] // (2 * size), shapes[2 * i + 1][1]) for i in range(count)
+    ]
     whole = pl.BlockSpec(memory_space=pltpu.VMEM)
+    spot = pl.BlockSpec(memory_space=pl.ANY)
     return pl.pallas_call(
         functools.partial(scatter_kernel, size, count),
-        out_shape=[jax.ShapeDtypeStruct((2,) + item.shape[2:], BF) for item in pieces]
+        out_shape=[jax.ShapeDtypeStruct((2,) + chunk, BF) for chunk in chunks]
         + [jax.ShapeDtypeStruct((size,) + small.shape, small.dtype)],
-        in_specs=[whole] * (count + 1),
+        in_specs=[spot] * (6 * count) + [whole],
         out_specs=[whole] * (count + 1),
-        scratch_shapes=[pltpu.VMEM((2, size - 1) + item.shape[2:], BF) for item in pieces]
+        scratch_shapes=[pltpu.VMEM(shape, BF) for shape in shapes]
+        + [pltpu.VMEM((2, size) + chunk, BF) for chunk in chunks]
+        + [pltpu.VMEM((2, size - 1) + chunk, BF) for chunk in chunks]
+        + [pltpu.SemaphoreType.DMA((2 * count, 2))]
         + [pltpu.SemaphoreType.DMA((2, count, size - 1))] * 2
         + [pltpu.SemaphoreType.DMA((size - 1,))] * 2,
         compiler_params=pltpu.CompilerParams(
             collective_id=0, has_side_effects=True, vmem_limit_bytes=VMEM_LIMIT
         ),
         name="ring_scatter",
-    )(*pieces, small)
+    )(*[block for item in flat for block in item], small)
 
 
 def gather_kernel(size, groups, *refs):
@@ -213,9 +263,8 @@
                     out[item].at[place, :, pl.ds(start, width)],
                 )
         else:
-            deep = own[item].shape[1]
             for half in range(2):
-                yield own[item].at[half], out[item].at[place, pl.ds(half * deep, deep)]
+                yield own[item].at[half], out[item].at[half, place]
 
     def copies(item, source_half, lane, kind, device=None):
         for number, (source, target) in enumerate(parts(item, source_half, core)):
@@ -251,8 +300,11 @@
                     copy.start()
 
     def send(way, item, chunk, slot):
-        deep = out[item].shape[1] // 2
-        here = out[item].at[chunk, pl.ds(way * deep, deep)]
+        if item < len(groups):
+            deep = out[item].shape[1] // 2
+            here = out[item].at[chunk, pl.ds(way * deep, deep)]
+        else:
+            here = out[item].at[way, chunk]
         return pltpu.make_async_remote_copy(
             src_ref=here,
             dst_ref=here,
@@ -329,7 +381,7 @@
 def ring_gather(pieces, groups, size):
     spot = pl.BlockSpec(memory_space=pl.ANY)
     shapes = [(size, item.shape[1], 2 * item.shape[2]) for item in pieces[: len(groups)]]
-    shapes += [(size, 2 * item.shape[1], item.shape[2]) for item in pieces[len(groups) :]]
+    shapes += [(2, size) + item.shape[1:] for item in pieces[len(groups) :]]
     count = len(pieces)
     return pl.pallas_call(
         functools.partial(gather_kernel, size, groups),
@@ -348,9 +400,9 @@
 
 def fetch_kernel(*refs):
     tokens, cotangent, small, qkv, fc, out, proj = refs[:7]
-    outer, small_out, w_qkv, w_fc, w_out, w_proj = refs[7:13]
-    send_sem, recv_sem, extra_send, extra_recv, local_sem = refs[13:18]
-    buffers = refs[18:]
+    *outer, small_out, w_qkv, w_fc, w_out, w_proj = refs[7:14]
+    send_sem, recv_sem, extra_send, extra_recv, local_sem = refs[14:19]
+    buffers = refs[19:]
     core, layer, sibling, across, diagonal = neighbours()
     index = lax.axis_index("replica")
     quarter = index % 4
@@ -432,8 +484,8 @@
 
     def through(source, dest, number):
         return (
-            pltpu.make_async_copy(source, buffers[number], local_sem.at[number]),
-            pltpu.make_async_copy(buffers[number], dest, local_sem.at[number]),
+            lambda: pltpu.make_async_copy(source, buffers[number], local_sem.at[number]),
+            lambda: pltpu.make_async_copy(buffers[number], dest, local_sem.at[number]),
         )
 
     def keep_local(item):
@@ -459,7 +511,7 @@
         def copy(source):
             return pltpu.make_async_remote_copy(
                 src_ref=source.at[block, place],
-                dst_ref=outer.at[block, outer_rows(layer, core)],
+                dst_ref=outer[block].at[outer_rows(layer, core)],
                 send_sem=extra_send.at[block],
                 recv_sem=extra_recv.at[block],
                 device_id=across,
@@ -469,7 +521,7 @@
         return copy
 
     def outer_pass(block):
-        here = outer.at[block, outer_rows(1 - layer, core)]
+        here = outer[block].at[outer_rows(1 - layer, core)]
         return pltpu.make_async_remote_copy(
             src_ref=here,
             dst_ref=here,
@@ -479,9 +531,9 @@
             device_id_type=MESH,
         )
 
-    def outer_local(source):
+    def outer_local(source, block):
         place = pl.ds(pl.multiple_of(layer * part, part), part)
-        return through(source, outer.at[:, place], 7)
+        return through(source.at[block], outer[block].at[place], 7 + block)
 
     def small_swap():
         return pltpu.make_async_remote_copy(
@@ -504,7 +556,7 @@
         )
 
     def small_local():
-        return through(small, small_out.at[core], 8)
+        return through(small, small_out.at[core], 9)
 
     def start_outer(block):
         @pl.when(layer == 0)
@@ -522,7 +574,7 @@
 
     @pl.when(same)
     def _():
-        small_local()[0].start()
+        small_local()[0]().start()
 
     @pl.when(core != layer)
     def _():
@@ -537,33 +589,37 @@
 
     @pl.when(layer == 0)
     def _():
-        outer_local(tokens)[0].start()
+        for block in range(2):
+            outer_local(tokens, block)[0]().start()
 
     @pl.when(layer == 1)
     def _():
-        outer_local(cotangent)[0].start()
+        for block in range(2):
+            outer_local(cotangent, block)[0]().start()
 
     @pl.when(same)
     def _():
         for item in range(4):
             to_sibling(item).start()
         load, store = small_local()
-        load.wait()
-        store.start()
-        store.wait()
+        load().wait()
+        store().start()
+        store().wait()
 
     @pl.when(core != layer)
     def _():
         small_swap().wait_recv()
 
     small_pass().start()
-    outer_local(tokens)[0].wait()
-    outer_local(tokens)[1].start()
+    for block in range(2):
+        load, store = outer_local(tokens, block)
+        load().wait()
+        store().start()
 
     @pl.when(same)
     def _():
         for item in range(7):
-            keep_local(item)[0].start()
+            keep_local(item)[0]().start()
 
     def relay(sequence, ahead):
         def onward(item):
@@ -597,13 +653,13 @@
     def _():
         for item in range(7):
             load, store = keep_local(item)
-            load.wait()
-            store.start()
+            load().wait()
+            store().start()
         relay([0, 1, 2, 3], False)
         for item in range(4):
             to_sibling(item).wait_send()
         for item in range(7):
-            keep_local(item)[1].wait()
+            keep_local(item)[1]().wait()
 
     @pl.when(core != layer)
     def _():
@@ -617,7 +673,8 @@
 
     outer_cross(1)(tokens).wait_recv()
     outer_pass(1).start()
-    outer_local(tokens)[1].wait()
+    for block in range(2):
+        outer_local(tokens, block)[1]().wait()
     small_pass().wait()
     for block in range(2):
         outer_cross(block)(tokens).wait_send()
@@ -626,9 +683,10 @@
 
 def fetch_inputs(tokens, cotangent, small, qkv, fc, out, proj):
     spot = pl.BlockSpec(memory_space=pl.ANY)
-    micro, part, width = tokens.shape
+    _, part, width = tokens.shape
     shapes = [
-        (micro, 2 * part, width),
+        (2 * part, width),
+        (2 * part, width),
         (2,) + small.shape,
         (2 * qkv.shape[0], qkv.shape[1] // 2),
         (2 * fc.shape[0], fc.shape[1] // 2),
@@ -639,13 +697,13 @@
         fetch_kernel,
         out_shape=[jax.ShapeDtypeStruct(shape, BF) for shape in shapes],
         in_specs=[spot] * 7,
-        out_specs=[spot] * 6,
+        out_specs=[spot] * 7,
         scratch_shapes=[
             pltpu.SemaphoreType.DMA((7, 7)),
             pltpu.SemaphoreType.DMA((7, 7)),
             pltpu.SemaphoreType.DMA((6,)),
             pltpu.SemaphoreType.DMA((6,)),
-            pltpu.SemaphoreType.DMA((9,)),
+            pltpu.SemaphoreType.DMA((10,)),
         ]
         + [pltpu.VMEM((qkv.shape[0], qkv.shape[1] // 6), BF)] * 3
         + [
@@ -653,7 +711,8 @@
             pltpu.VMEM(out.shape, BF),
             pltpu.VMEM((proj.shape[0] // 2, width), BF),
             pltpu.VMEM((proj.shape[0] // 2, width), BF),
-            pltpu.VMEM(tokens.shape, BF),
+            pltpu.VMEM(tokens.shape[1:], BF),
+            pltpu.VMEM(tokens.shape[1:], BF),
             pltpu.VMEM(small.shape, BF),
         ],
         compiler_params=pltpu.CompilerParams(
@@ -679,20 +738,6 @@
     def wait(self, *names):
         for name in names:
             self.made.pop(name).wait()
-
-
-def chosen_load(first_ref, other_ref, buffer, sem):
-    layer = lax.axis_index("shard")
-
-    @pl.when(layer == 0)
-    def _():
-        pltpu.make_async_copy(first_ref, buffer, sem).start()
-
-    @pl.when(layer != 0)
-    def _():
-        pltpu.make_async_copy(other_ref, buffer, sem).start()
-
-    return pltpu.make_async_copy(first_ref, buffer, sem)
 
 
 def greet_step(sender, passing):
@@ -764,6 +809,13 @@
         def _():
             self.copy(tile, 0).start()
 
+    def receive(self, tile):
+        @pl.when(self.layer != self.sender)
+        def _():
+            self.copy(tile, 0).wait_recv()
+            self.copy(tile, 1).start()
+            self.copy(tile, 1).wait_recv()
+
     def finish(self):
         @pl.when(self.layer == self.sender)
         def _():
@@ -773,10 +825,45 @@
         @pl.when(self.layer != self.sender)
         def _():
             for tile in range(TILES):
-                self.copy(tile, 0).wait_recv()
-                self.copy(tile, 1).start()
+                self.copy(tile, 1).wait_send()
+
+
+class Opening:
+    def __init__(self, passing, sender, first_ref, other_ref, earlier, buffer, sem, sems):
+        self.passing, self.sender, self.layer = passing, sender, lax.axis_index("shard")
+        self.load = lambda ref: pltpu.make_async_copy(ref, buffer, sem)
+        self.refs = (first_ref, other_ref)
+        self.across = Across(sender, earlier, buffer, sems)
+
+    def start(self):
+        for layer, ref in enumerate(self.refs):
+            if self.passing and layer != self.sender:
+                continue
+
+            @pl.when(self.layer == layer)
+            def _(ref=ref):
+                self.load(ref).start()
+
+    def send(self):
+        if self.passing:
             for tile in range(TILES):
-                self.copy(tile, 1).wait()
+                self.across.send(tile)
+
+    def take(self, tile):
+        if self.passing:
+            if tile == 0:
+
+                @pl.when(self.layer == self.sender)
+                def _():
+                    self.load(self.refs[0]).wait()
+
+            self.across.receive(tile)
+        elif tile == 0:
+            self.load(self.refs[0]).wait()
+
+    def finish(self):
+        if self.passing:
+            self.across.finish()
 
 
 def by_past(mode, body):
@@ -798,21 +885,22 @@
 
 
 def forward_kernel(mode, passing, *refs):
-    x_first, x_other, params, w_qkv, w_out, w_fc, w_proj, k_past, v_past = refs[:9]
-    refs = refs[9:]
-    (normed1, query, keys, values, mixed, lse, scaled2, inverse2, normed2, slope, act, out, passed) = refs[:13]
-    refs = refs[13:]
+    x_first, x_other, earlier, params, w_qkv, w_out, w_fc, w_proj, k_past, v_past = refs[:10]
+    refs = refs[10:]
+    (x_used, normed1, query, keys, values, mixed, lse, scaled2, inverse2, normed2, slope, act, out, passed) = refs[:14]
+    refs = refs[14:]
     (x_v, wq_v, wo_v, wf_v, wp_v, k_v, v_v, hid_v, part_v, send_v, recv_v) = refs[:11]
     refs = refs[11:]
     (n1_v, q_v, m_v, lse_v, s2_v, i2_v, n2_v, sl_v, a_v, o_v) = refs[:10]
-    load_sem, store_sem, send_sem, recv_sem, across_sem = refs[10:]
+    load_sem, store_sem, send_sem, recv_sem, open_sem, across_sem = refs[10:]
     rows, width = x_v.shape
     half = q_v.shape[1]
     tile_rows = rows // TILES
     wide = a_v.shape[1]
 
     loads = Loads(load_sem)
-    load_x = chosen_load(x_first, x_other, x_v, load_sem.at[FORWARD_LOADS])
+    opening = Opening(passing, 0, x_first, x_other, earlier, x_v, load_sem.at[FORWARD_LOADS], open_sem)
+    opening.start()
     loads.start("qkv", w_qkv, wq_v)
     if mode is not False:
         loads.start("k", k_past, k_v.at[pl.ds(0, rows)])
@@ -821,6 +909,7 @@
     loads.start("fc", w_fc, wf_v)
     loads.start("proj", w_proj, wp_v)
     greet_step(0, passing)
+    opening.send()
     exchange = Exchange(send_v, recv_v, send_sem, recv_sem)
     across = Across(0, o_v, passed, across_sem)
     stores = []
@@ -833,24 +922,24 @@
     def vector(row, start=0, size=None):
         return params[row : row + 1, start : start + (size or width)]
 
-    load_x.wait()
-    for tile in range(TILES):
-        span = pl.ds(tile * tile_rows, tile_rows)
-        scaled, _ = norm_parts(x_v[span, :].astype(F32))
-        n1_v[span, :] = (scaled * vector(0) + vector(1)).astype(BF)
-    store(n1_v, normed1)
-    loads.wait("qkv")
     own_rows = pl.ds(rows, rows)
     for tile in range(TILES):
         span = pl.ds(tile * tile_rows, tile_rows)
         later = pl.ds(rows + tile * tile_rows, tile_rows)
-        normed = n1_v[span, :]
+        opening.take(tile)
+        scaled, _ = norm_parts(x_v[span, :].astype(F32))
+        normed = (scaled * vector(0) + vector(1)).astype(BF)
+        n1_v[span, :] = normed
+        if tile == 0:
+            loads.wait("qkv")
         piece = jnp.dot(normed, wq_v[:, :half], preferred_element_type=F32)
         q_v[span, :] = (piece + vector(6, 0, half)).astype(BF)
         piece = jnp.dot(normed, wq_v[:, half : 2 * half], preferred_element_type=F32)
         k_v[later, :] = piece.astype(BF)
         piece = jnp.dot(normed, wq_v[:, 2 * half :], preferred_element_type=F32)
         v_v[later, :] = (piece + vector(6, half, half)).astype(BF)
+    store(x_v, x_used)
+    store(n1_v, normed1)
     store(q_v, query)
     store(k_v.at[own_rows], keys)
     store(v_v.at[own_rows], values)
@@ -890,6 +979,14 @@
     store(m_v, mixed)
     store(lse_v, lse)
     loads.wait("fc", "proj")
+
+    def conclude(tile):
+        span = pl.ds(tile * tile_rows, tile_rows)
+        total = part_v[TILES + tile] + exchange.take(TILES + tile)
+        o_v[span, :] = (hid_v[span, :] + total + vector(5)).astype(BF)
+        if passing:
+            across.send(tile)
+
     for tile in range(TILES):
         span = pl.ds(tile * tile_rows, tile_rows)
         hidden = x_v[span, :].astype(F32) + (part_v[tile] + exchange.take(tile)) + vector(2)
@@ -907,6 +1004,8 @@
             activated, inclined = gelu_pair(pre + bias)
             a_v[span, columns] = activated.astype(BF)
             sl_v[span, columns] = inclined.astype(BF)
+        if tile > 0:
+            conclude(tile - 1)
         partial = jnp.dot(a_v[span, :], wp_v[...], preferred_element_type=F32)
         part_v[TILES + tile] = partial
         exchange.give(TILES + tile, partial)
@@ -915,17 +1014,15 @@
     store(n2_v, normed2)
     store(sl_v, slope)
     store(a_v, act)
-    for tile in range(TILES):
-        span = pl.ds(tile * tile_rows, tile_rows)
-        total = part_v[TILES + tile] + exchange.take(TILES + tile)
-        o_v[span, :] = (hid_v[span, :] + total + vector(5)).astype(BF)
-        if passing:
-            across.send(tile)
+    conclude(TILES - 1)
     store(o_v, out)
     for copy in stores:
         copy.wait()
     exchange.finish(2 * TILES)
+    opening.finish()
     if passing:
+        for tile in range(TILES):
+            across.receive(tile)
         across.finish()
 
 
@@ -936,11 +1033,12 @@
         pltpu.SemaphoreType.DMA((2 * TILES,)),
         pltpu.SemaphoreType.DMA((2 * TILES,)),
         pltpu.SemaphoreType.DMA((4, TILES)),
+        pltpu.SemaphoreType.DMA((4, TILES)),
     ]
 
 
-def forward_step(mode, passing, x_first, x_other, params, weights, past):
-    rows, width = x_first.shape
+def forward_step(mode, passing, inputs, params, weights, past):
+    rows, width = inputs[0].shape
     half = width // 2
     wide = weights[2].shape[1]
     pairs = half // 128
@@ -949,6 +1047,7 @@
     low = lambda columns: ((rows, columns), BF)
     outs = [
         low(width),
+        low(width),
         low(half),
         low(half),
         low(half),
@@ -982,11 +1081,11 @@
         low(wide),
         low(width),
     ]
-    number = {(False, True): 3, (None, True): 4, (True, False): 5}[(mode, passing)]
+    number = {False: 3, None: 4, True: 5}[mode]
     return pl.pallas_call(
         functools.partial(forward_kernel, mode, passing),
         out_shape=[jax.ShapeDtypeStruct(*item) for item in outs],
-        in_specs=[spot] * 2 + [pl.BlockSpec(memory_space=pltpu.VMEM)] + [spot] * 6,
+        in_specs=[spot] * 3 + [pl.BlockSpec(memory_space=pltpu.VMEM)] + [spot] * 6,
         out_specs=[spot] * len(outs),
         scratch_shapes=[pltpu.VMEM(*item) for item in scratch]
         + step_sems(FORWARD_LOADS + 1, len(outs)),
@@ -994,22 +1093,22 @@
             collective_id=number, has_side_effects=True, vmem_limit_bytes=VMEM_LIMIT
         ),
         name="forward_step",
-    )(x_first, x_other, params, *weights, *past)
-
-
-BACKWARD_LOADS = 16
+    )(*inputs, params, *weights, *past)
+
+
+BACKWARD_LOADS = 17
 
 
 def backward_kernel(mode, passing, *refs):
-    (g_first, g_other, x_first, x_other, params, w_qkv, w_out, w_fc, w_proj) = refs[:9]
+    (g_first, g_other, earlier, x_used, params, w_qkv, w_out, w_fc, w_proj) = refs[:9]
     (query, keys, values, k_past, v_past, mixed, lse, scaled2, inverse2, slope, pend_k, pend_v) = refs[9:21]
     refs = refs[21:]
-    (d_qkv, d_branch, d_pre, out, next_k, next_v, sums, passed) = refs[:8]
-    refs = refs[8:]
+    (g_used, d_qkv, d_branch, d_pre, out, next_k, next_v, sums, passed) = refs[:9]
+    refs = refs[9:]
     (g_v, x_v, wq_v, wo_v, wf_v, wp_v, q_v, k_v, v_v, m_v, lse_v, s2_v, i2_v, sl_v) = refs[:14]
     refs = refs[14:]
     (dk_v, dv_v, hid_v, part_v, send_v, recv_v, dqkv_v, db_v, dp_v, dm_v, o_v, sum_v) = refs[:12]
-    load_sem, store_sem, send_sem, recv_sem, across_sem = refs[12:]
+    load_sem, store_sem, send_sem, recv_sem, open_sem, across_sem = refs[12:]
     rows, width = x_v.shape
     half = q_v.shape[1]
     wide = dp_v.shape[1]
@@ -1018,7 +1117,8 @@
     scale = HEAD_DIM**-0.5
 
     loads = Loads(load_sem)
-    load_g = chosen_load(g_first, g_other, g_v, load_sem.at[BACKWARD_LOADS])
+    opening = Opening(passing, 1, g_first, g_other, earlier, g_v, load_sem.at[BACKWARD_LOADS], open_sem)
+    opening.start()
     loads.start("proj", w_proj, wp_v)
     loads.start("slope", slope, sl_v)
     loads.start("fc", w_fc, wf_v)
@@ -1037,8 +1137,9 @@
         loads.start("pend_k", pend_k, dk_v.at[own_rows])
         loads.start("pend_v", pend_v, dv_v.at[own_rows])
     loads.start("qkv", w_qkv, wq_v)
-    load_x = chosen_load(x_first, x_other, x_v, load_sem.at[BACKWARD_LOADS + 1])
+    loads.start("x", x_used, x_v)
     greet_step(1, passing)
+    opening.send()
     exchange = Exchange(send_v, recv_v, send_sem, recv_sem)
     across = Across(1, o_v, passed, across_sem)
     stores = []
@@ -1057,11 +1158,11 @@
         place = (slice(row, row + 1), slice(start, start + piece.shape[1]))
         sum_v[place] += jnp.sum(piece, axis=0, keepdims=True)
 
-    load_g.wait()
     loads.wait("proj", "slope", "fc")
     chunk = width // 2
     for tile in range(TILES):
         span = pl.ds(tile * tile_rows, tile_rows)
+        opening.take(tile)
         grad = g_v[span, :]
         for part in range(wide // chunk):
             columns = pl.ds(part * chunk, chunk)
@@ -1073,6 +1174,7 @@
         part_v[tile] = partial
         exchange.give(tile, partial)
         tally(5, grad.astype(F32))
+    store(g_v, g_used)
     store(dp_v, d_pre)
     loads.wait("scaled2", "inverse2", "out")
     for tile in range(TILES):
@@ -1139,8 +1241,7 @@
     if mode is not False:
         store(dk_v.at[past_rows], next_k)
         store(dv_v.at[past_rows], next_v)
-    loads.wait("qkv")
-    load_x.wait()
+    loads.wait("qkv", "x")
     for tile in range(TILES):
         span = pl.ds(tile * tile_rows, tile_rows)
         later = pl.ds(rows + tile * tile_rows, tile_rows)
@@ -1168,12 +1269,15 @@
     for copy in stores:
         copy.wait()
     exchange.finish(2 * TILES)
+    opening.finish()
     if passing:
+        for tile in range(TILES):
+            across.receive(tile)
         across.finish()
 
 
 def backward_step(mode, passing, grads, inputs, params, weights, kept, pending):
-    rows, width = inputs[0].shape
+    rows, width = inputs.shape
     half = width // 2
     wide = weights[2].shape[1]
     pairs = half // 128
@@ -1181,6 +1285,7 @@
     spot = pl.BlockSpec(memory_space=pl.ANY)
     low = lambda columns: ((rows, columns), BF)
     outs = [
+        low(width),
         low(3 * half),
         low(width),
         low(wide),
@@ -1215,19 +1320,19 @@
         low(width),
         ((16, width), F32),
     ]
-    number = {(True, True): 6, (None, True): 7, (False, False): 8}[(mode, passing)]
+    number = {True: 6, None: 7, False: 8}[mode]
     return pl.pallas_call(
         functools.partial(backward_kernel, mode, passing),
         out_shape=[jax.ShapeDtypeStruct(*item) for item in outs],
         in_specs=[spot] * 4 + [pl.BlockSpec(memory_space=pltpu.VMEM)] + [spot] * 16,
         out_specs=[spot] * len(outs),
         scratch_shapes=[pltpu.VMEM(*item) for item in scratch]
-        + step_sems(BACKWARD_LOADS + 2, len(outs)),
+        + step_sems(BACKWARD_LOADS + 1, len(outs)),
         compiler_params=pltpu.CompilerParams(
             collective_id=number, has_side_effects=True, vmem_limit_bytes=VMEM_LIMIT
         ),
         name="backward_step",
-    )(*grads, *inputs, params, *weights, *kept, *pending)
+    )(*grads, inputs, params, *weights, *kept, *pending)
 
 
 def shards(
@@ -1257,7 +1362,6 @@
     assert micro == 2
     rows = 2 * part
     half = width // 2
-    hidden_half = fc_weight.shape[2] // 2
 
     def pair_permute(value, pairs):
         return lax.ppermute(value, PAIR, pairs)
@@ -1278,7 +1382,7 @@
             )
         ]
     ).reshape(-1, 128)
-    outer, small_both, w_qkv, w_fc, w_out, w_proj = fetch_inputs(
+    *outer, small_both, w_qkv, w_fc, w_out, w_proj = fetch_inputs(
         tokens[0], cotangent[0], small, qkv_weight[0], fc_weight[0], out_weight[0], proj_weight[0]
     )
     flat = small_both.reshape(2, -1).astype(F32)
@@ -1296,69 +1400,56 @@
     weights = (w_qkv, w_out, w_fc, w_proj)
 
     empty = jnp.zeros((rows, half), BF)
-    received, kept_list, outputs, past = [outer[0]], [], [], (empty, empty)
+    received, kept_list, outputs, past, got = [], [], [], (empty, empty), outer[0]
     for step in range(micro + 1):
-        mode = (False, None, True)[step]
-        normed1, query, keys, values, mixed, lse, scaled2, inverse2, normed2, slope, act, output, got = (
-            forward_step(
-                mode,
-                step < micro,
-                outer[min(step, micro - 1)],
-                received[step],
-                params,
-                weights,
-                past,
-            )
+        output = outputs[-1] if outputs else outer[0]
+        used, normed1, *state, normed2, slope, act, output, got = forward_step(
+            (False, None, True)[step],
+            step == 1,
+            (outer[min(step, micro - 1)], got, output),
+            params,
+            weights,
+            past,
         )
+        query, keys, values, mixed, lse, scaled2, inverse2 = state
         outputs.append(output)
+        received.append(used)
         kept = (query, keys, values, *past, mixed, lse, scaled2, inverse2, slope)
         kept_list.append((kept, normed1, normed2, act))
         past = (keys, values)
-        received.append(got)
 
     pending = (jnp.zeros((rows, half), F32), jnp.zeros((rows, half), F32))
-    grad_received = [outer[0]]
-    terms_list, results, sums = [], [], None
+    grad_received, terms_list, results, sums, got = [], [], [], None, outer[1]
     for step in range(micro + 1):
-        mode = (True, None, False)[step]
         active = jnp.where(first, step >= 1, step < micro)
         last = micro - step
         kept, normed1, normed2, act = kept_list[last]
-        grads = (grad_received[step], outer[max(micro - 1 - step, 0)])
-        d_qkv, d_branch, d_pre, result, *pending, vector, got = backward_step(
-            mode,
-            step < micro,
-            grads,
-            (outer[min(last, micro - 1)], received[last]),
+        result = results[-1] if results else outer[1]
+        grad, d_qkv, d_branch, d_pre, result, *pending, vector, got = backward_step(
+            (True, None, False)[step],
+            step == 1,
+            (got, outer[max(micro - 1 - step, 0)], result),
+            received[last],
             params,
             weights,
             kept,
             pending,
         )
         results.append(result)
-        grad_received.append(got)
+        grad_received.append(grad)
         vector = jnp.where(active, vector, 0.0)
         sums = vector if sums is None else sums + vector
-        grad = jnp.where(first, *grads)
         terms_list.append((normed1, d_qkv, kept[5], d_branch, normed2, d_pre, act, grad))
     full = lax.dynamic_slice_in_dim(sums[:6], core * half, half, 1)
     sums = jnp.concatenate([full.reshape(-1), sums[6:9].reshape(-1)])
 
-    late = [jnp.where(first, a, b) for a, b in zip(terms_list[2], terms_list[0])]
-    both = [jnp.concatenate([a, b], axis=0) for a, b in zip(terms_list[1], late)]
-    chunk = half // size
-    wide = hidden_half // size
-    pieces = [
-        rows_product(both[0], both[1]).astype(BF).reshape(2, size, chunk, 3 * half),
-        rows_product(both[4], both[5]).astype(BF).reshape(2, size, chunk, hidden_half),
-        rows_product(both[2], both[3]).astype(BF).reshape(size, 2, chunk // 2, width),
-        rows_product(both[6], both[7]).astype(BF).reshape(size, 2, wide // 2, width),
-    ]
-    pieces[2] = jnp.swapaxes(pieces[2], 0, 1)
-    pieces[3] = jnp.swapaxes(pieces[3], 0, 1)
+    def factor(number):
+        return tuple(terms_list[step][number] for step in (2, 1, 0))
+
+    factors = [(factor(i), factor(i + 1)) for i in (0, 4, 2, 6)]
     sums = sums.reshape(-1, 128)
     sums = jnp.where(own, sums, pair_permute(sums, CROSS_SWAP))
-    *reduced, sums = ring_scatter(pieces, sums)
+    *reduced, sums = ring_scatter(factors, sums, size)
     sums = jnp.sum(sums, axis=0).reshape(-1)
     vectors = [sums[i * half : (i + 1) * half][None] for i in range(8)] + [sums[8 * half :][None]]
     qkv_grad, fc_grad, out_grad, proj_grad = (

time: 638 us -> 585 us (0.917)
  matrix products: 20 us -> 0 us
  local copies, waits for them, and re-layouts: 27.7 us -> 10.1 us
  Pallas kernels: 542 us -> 525 us
    dot_general x4 -> x0, matrix products: 20 us -> none  [rows_product(): lax.dot_general(left, right, ROWS_CONTRACT, preferred_element_type=F32)]
    pallas_call x3, Pallas kernels: 101 us -> 90.8 us  [forward_step(): pl.pallas_call(functools.partial(forward_kernel, mode, passing), out_shap...]
    unnamed x92 -> x42, local copies, waits for them, and re-layouts: 10.8 us -> 3.35 us
    reshape x2 -> x0, local copies, waits for them, and re-layouts: 7.09 us -> none  [the longest x1 4.8 us: shards(): rows_product(both[6], both[7]).astype(BF).reshape(size, 2, wide // 2, width)]
  transfers between devices with their start and end apart: 5 -> 5, of which waited for: 0 -> 1; matrix products, arithmetic and copies ran while one was open for 9% -> 5% of each run, Pallas kernels for 58% -> 62%
where the time goes in v4:
time: 585 us; the launch traced here: 581 us
  Pallas kernels  525 us (90%)
  other arithmetic  35.5 us (6%)
  local copies, waits for them, and re-layouts  10.1 us (2%)
  starting transfers between devices  7.83 us (1%)
    pallas_call x1, Pallas kernels, ring_gather(): pl.pallas_call(functools.partial(gather_kernel, size, groups), out_shape=...  129 us
    pallas_call x1, Pallas kernels, ring_scatter(): pl.pallas_call(functools.partial(scatter_kernel, size, count), out_shape=...  127 us
    pallas_call x3, Pallas kernels, backward_step(): pl.pallas_call(functools.partial(backward_kernel, mode, passing), out_sha...  103 us
    pallas_call x3, Pallas kernels, forward_step(): pl.pallas_call(functools.partial(forward_kernel, mode, passing), out_shap...  90.8 us
    pallas_call x1, Pallas kernels, fetch_inputs(): pl.pallas_call(fetch_kernel, out_shape=[jax.ShapeDtypeStruct(shape, BF) f...  74.8 us
    reshape x4, other arithmetic, shards(): item.astype(F32).reshape(1, -1, item.shape[-1])  19.9 us
  transfers between devices with their start and end apart: 5, of which 1 were waited for; matrix products, arithmetic and copies ran while one was open for 5% of the time, Pallas kernels for 62%

profile of v4, /device:TPU:1, one launch (start us, length us, event | category | flops | bytes accessed | tf_op | source)
XLA Modules:
  0.0 581.0 jit_solution(9971259118514456497)
XLA Ops:
  0.7 0.7 reduce
  1.4 0.7 reduce.1
  2.1 0.7 reduce.2
  2.8 0.7 reduce.3
  3.5 0.7 reduce.4
  4.2 0.7 reduce.5
  4.9 0.7 reduce.6
  5.6 0.7 reduce.7
  6.3 0.7 reduce.8
  7.0 0.2 dynamic-update-slice.2
  7.2 0.2 dynamic-update-slice.3
  7.5 0.2 dynamic-update-slice.4
  7.7 0.2 dynamic-update-slice.5
  7.9 0.2 dynamic-update-slice.6
  8.1 0.2 dynamic-update-slice.7
  8.3 0.2 dynamic-update-slice.8
  8.5 0.2 dynamic-update-slice.9
  8.7 0.6 copy-done.15
  9.3 74.8 %fetch_inputs.1 = (bf16[512,1024]{1,0:T(8,128)(2,1)}, bf16[512,1024]{1,0:T(8,128)(2,1)}, bf16[2,48,128]{2,1,0:T(8,128)(2,1)}, bf16[1024,1536]{1,0:T(8,128)(2,1)}...) custom-call(bf16[2,256,1024]{2,1,0:T(8,128)(2,1)} %bitcast.53, ...), custom_call_target="tpu_custom_call" | custom-call | tf_op jit(solution)/shard_map/fetch_inputs/pallas_call | solution.py:696
  84.1 0.7 convert_bitcast_fusion
  84.9 0.1 slice_reduce_fusion.2
  85.1 0.1 pad.7.clone
  85.2 0.7 maximum_maximum_fusion.refs_3_.refs_4_
  85.9 0.8 broadcast_in_dim.46.refs_8_.refs_9_.refs_12_.refs_13_
  86.7 24.7 %forward_step.3 = (bf16[512,1024]{1,0:T(8,128)(2,1)}, bf16[512,1024]{1,0:T(8,128)(2,1)}, bf16[512,512]{1,0:T(8,128)(2,1)}, bf16[512,512]{1,0:T(8,128)(2,1)}, bf1...) custom-call(bf16[512,1024]{1,0:T(8,128)(2,1)} %get-tuple-element.96., ...), custom_call_target="tpu_custom_call" | custom-call | tf_op jit(solution)/shard_map/forward_step/pallas_call | solution.py:1085
  111.5 36.4 %forward_step.4 = (bf16[512,1024]{1,0:T(8,128)(2,1)}, bf16[512,1024]{1,0:T(8,128)(2,1)}, bf16[512,512]{1,0:T(8,128)(2,1)}, bf16[512,512]{1,0:T(8,128)(2,1)}, bf1...) custom-call(bf16[512,1024]{1,0:T(8,128)(2,1)} %get-tuple-element.103, ...), custom_call_target="tpu_custom_call" | custom-call | tf_op jit(solution)/shard_map/forward_step/pallas_call | solution.py:1085
  147.9 29.6 %forward_step.5 = (bf16[512,1024]{1,0:T(8,128)(2,1)}, bf16[512,1024]{1,0:T(8,128)(2,1)}, bf16[512,512]{1,0:T(8,128)(2,1)}, bf16[512,512]{1,0:T(8,128)(2,1)}, bf1...) custom-call(bf16[512,1024]{1,0:T(8,128)(2,1)} %get-tuple-element.103, ...), custom_call_target="tpu_custom_call" | custom-call | tf_op jit(solution)/shard_map/forward_step/pallas_call | solution.py:1085
  177.5 0.2 broadcast_select_fusion.3
  177.7 0.8 constant_dynamic-slice_fusion.2
  178.6 1.3 collective-permute-start.1
  179.9 0.8 constant_dynamic-slice_fusion.4
  180.7 1.5 collective-permute-start
  182.2 1.1 broadcast_1_refs_19__refs_20_.2.refs_19_.refs_20_
  183.3 29.8 %backward_step.3 = (bf16[512,1024]{1,0:T(8,128)(2,1)}, bf16[512,1536]{1,0:T(8,128)(2,1)}, bf16[512,1024]{1,0:T(8,128)(2,1)}, bf16[512,2048]{1,0:T(8,128)(2,1)}, ...) custom-call(bf16[512,1024]{1,0:T(8,128)(2,1)} %get-tuple-element.103, ...), custom_call_target="tpu_custom_call" | custom-call | tf_op jit(solution)/shard_map/backward_step/pallas_call | solution.py:1324
  213.1 48.3 %backward_step.4 = (bf16[512,1024]{1,0:T(8,128)(2,1)}, bf16[512,1536]{1,0:T(8,128)(2,1)}, bf16[512,1024]{1,0:T(8,128)(2,1)}, bf16[512,2048]{1,0:T(8,128)(2,1)}, ...) custom-call(bf16[512,1024]{1,0:T(8,128)(2,1)} %get-tuple-element.122, ...), custom_call_target="tpu_custom_call" | custom-call | tf_op jit(solution)/shard_map/backward_step/pallas_call | solution.py:1324
  261.4 25.1 %backward_step.5 = (bf16[512,1024]{1,0:T(8,128)(2,1)}, bf16[512,1536]{1,0:T(8,128)(2,1)}, bf16[512,1024]{1,0:T(8,128)(2,1)}, bf16[512,2048]{1,0:T(8,128)(2,1)}, ...) custom-call(bf16[512,1024]{1,0:T(8,128)(2,1)} %get-tuple-element.132, ...), custom_call_target="tpu_custom_call" | custom-call | tf_op jit(solution)/shard_map/backward_step/pallas_call | solution.py:1324
  286.6 1.5 broadcast_select_fusion.1
  288.0 0.0 copy-start.4
  288.0 1.0 copy-done.4
  289.0 0.8 constant_dynamic-slice_fusion.3
  289.8 1.5 collective-permute-start.3
  291.4 1.9 collective-permute-start.4
  293.4 0.9 constant_dynamic-slice_fusion.1
  294.2 1.7 collective-permute-start.2
  295.9 0.7 collective-permute-done.4
  296.6 0.6 broadcast_select_fusion.4.refs_24_
  297.2 127.5 %ring_scatter.1 = (bf16[2,64,1536]{2,1,0:T(8,128)(2,1)}, bf16[2,64,2048]{2,1,0:T(8,128)(2,1)}, bf16[2,32,1024]{2,1,0:T(8,128)(2,1)}, bf16[2,128,1024]{2,1,0:T(8,128)(2,1)}, f32[8,48,128]{2,1,0:T(8,128)}) custom-call(bf16[512,1024]{1,0:T(8,128)(2,1)} %get-tuple-element.146.refs_0_, bf16[512,1024]{1,0:T(8,128)(2,1)} %get-tuple-element.147.refs_1_, ...), custom_call_target="tpu_custom_call" | custom-call | tf_op jit(solution)/shard_map/ring_scatter/pallas_call | solution.py:227
  424.7 129.2 %ring_gather.1 = (bf16[8,64,3072]{2,1,0:T(8,128)(2,1)}, bf16[8,64,4096]{2,1,0:T(8,128)(2,1)}, bf16[2,8,32,1024]{3,2,1,0:T(8,128)(2,1)}, bf16[2,8,128,1024]{3,2,1,0:T(8,128)(2,1)}) custom-call(bf16[2,64,1536]{2,1,0:T(8,128)(2,1)} %get-tuple-element.169.refs_0_, bf16[2,64,2048]{2,1,0:T(8,128)(2,1)} %get-tuple-element.170.refs_1_, ...), custom_call_target="tpu_custom_call" | custom-call | tf_op jit(solution)/shard_map/ring_gather/pallas_call | solution.py:386
  553.9 6.8 %bitcast_convert_fusion = f32[1,512,4096]{2,1,0:T(8,128)} fusion(bf16[1,512,4096]{2,1,0:T(8,128)(2,1)} %bitcast.47), kind=kLoop, calls=%fused_computation | loop fusion | flops 2097152 | bytes 12582912 | tf_op jit(solution)/shard_map/reshape | solution.py:1456
  560.8 3.5 bitcast_convert_fusion.1
  564.3 2.8 convert.5
  567.1 0.6 slice.94
  567.7 6.8 %convert.7 = f32[1,2048,1024]{2,1,0:T(8,128)} convert(bf16[1,2048,1024]{2,1,0:T(8,128)(2,1)} %bitcast.46) | non-fusion elementwise | flops 2097152 | bytes 12582912 | tf_op jit(solution)/shard_map/reshape | solution.py:1456
  574.5 0.6 fusion
  575.1 0.0 collective-permute-done.1
  575.1 1.5 select_bitcast_fusion.2
  576.6 0.0 collective-permute-done
  576.6 1.4 select_bitcast_fusion.3
  578.0 1.1 maximum_bitcast_fusion
  579.1 0.0 collective-permute-done.3
  579.1 0.3 select_bitcast_fusion
  579.4 0.0 collective-permute-done.2
  579.4 0.3 select_bitcast_fusion.1
  579.7 1.1 maximum_bitcast_fusion.1
  (46 shorter events, 0.2 us)
Async XLA Ops:
  8.7 0.6 copy-start.15
  147.8 29.7 %copy-start.2 = (bf16[512,1024]{1,0:T(8,128)(2,1)S(1)}, bf16[512,1024]{1,0:T(8,128)(2,1)}, u32[]{:S(2)}) copy-start(bf16[512,1024]{1,0:T(8,128)(2,1)} %get-tuple-element.102.refs_2_) | copy-start | bytes 3145732
  147.8 29.7 %copy-start.3 = (bf16[512,1024]{1,0:T(8,128)(2,1)S(1)}, bf16[512,1024]{1,0:T(8,128)(2,1)}, u32[]{:S(2)}) copy-start(bf16[512,1024]{1,0:T(8,128)(2,1)} %get-tuple-element.107.refs_2_) | copy-start | bytes 3145732
  178.6 396.5 %collective-permute-start.1 = (bf16[256,1024]{1,0:T(8,128)(2,1)}, bf16[256,1024]{1,0:T(8,128)(2,1)}, u32[]{:S(2)}, u32[]{:S(2)}) collective-permute-start(bf16[256,1024]{1,0:T(8,128)(2,1)} %constant_dynamic-slice_fusion.2), channel_id=1, source_target_pairs={{24,16},{25,17},{26,18},{27,19},{28,20},{29,21},{30,22},{31,23}} | collective-permute-start | bytes 1572872 | tf_op jit(solution)/shard_map/ppermute | solution.py:1367
  180.7 395.9 %collective-permute-start = (bf16[256,1024]{1,0:T(8,128)(2,1)}, bf16[256,1024]{1,0:T(8,128)(2,1)}, u32[]{:S(2)}, u32[]{:S(2)}) collective-permute-start(bf16[256,1024]{1,0:T(8,128)(2,1)} %constant_dynamic-slice_fusion.4), channel_id=1, source_target_pairs={{24,16},{25,17},{26,18},{27,19},{28,20},{29,21},{30,22},{31,23}} | collective-permute-start | bytes 1572872 | tf_op jit(solution)/shard_map/ppermute | solution.py:1367
  261.4 25.1 %copy-start = (bf16[512,1024]{1,0:T(8,128)(2,1)S(1)}, bf16[512,1024]{1,0:T(8,128)(2,1)}, u32[]{:S(2)}) copy-start(bf16[512,1024]{1,0:T(8,128)(2,1)} %get-tuple-element.123.refs_2_) | copy-start | bytes 3145732
  261.4 25.1 %copy-start.1 = (bf16[512,1024]{1,0:T(8,128)(2,1)S(1)}, bf16[512,1024]{1,0:T(8,128)(2,1)}, u32[]{:S(2)}) copy-start(bf16[512,1024]{1,0:T(8,128)(2,1)} %get-tuple-element.133.refs_2_) | copy-start | bytes 3145732
  286.5 4.8 copy-start.12
  286.5 4.8 copy-start.13
  286.6 4.8 copy-start.14
  288.0 1.0 copy-start.4
  289.8 289.2 %collective-permute-start.3 = (bf16[256,1024]{1,0:T(8,128)(2,1)}, bf16[256,1024]{1,0:T(8,128)(2,1)}, u32[]{:S(2)}, u32[]{:S(2)}) collective-permute-start(bf16[256,1024]{1,0:T(8,128)(2,1)} %constant_dynamic-slice_fusion.3), channel_id=1, source_target_pairs={{0,8},{1,9},{2,10},{3,11},{4,12},{5,13},{6,14},{7,15}} | collective-permute-start | bytes 1572872 | tf_op jit(solution)/shard_map/ppermute | solution.py:1367
  291.4 5.1 collective-permute-start.4
  294.2 285.1 %collective-permute-start.2 = (bf16[256,1024]{1,0:T(8,128)(2,1)}, bf16[256,1024]{1,0:T(8,128)(2,1)}, u32[]{:S(2)}, u32[]{:S(2)}) collective-permute-start(bf16[256,1024]{1,0:T(8,128)(2,1)} %constant_dynamic-slice_fusion.1), channel_id=1, source_target_pairs={{0,8},{1,9},{2,10},{3,11},{4,12},{5,13},{6,14},{7,15}} | collective-permute-start | bytes 1572872 | tf_op jit(solution)/shard_map/ppermute | solution.py:1367
  553.9 6.8 %copy-start.6 = (bf16[8,64,3072]{2,1,0:T(8,128)(2,1)S(1)}, bf16[8,64,3072]{2,1,0:T(8,128)(2,1)}, u32[]{:S(2)}) copy-start(bf16[8,64,3072]{2,1,0:T(8,128)(2,1)} %get-tuple-element.173) | copy-start | bytes 9437188
  560.8 3.5 copy-start.11
  567.7 7.4 %copy-start.8 = (bf16[512,1024]{1,0:T(8,128)(2,1)S(1)}, bf16[512,1024]{1,0:T(8,128)(2,1)}, u32[]{:S(2)}) copy-start(bf16[512,1024]{1,0:T(8,128)(2,1)} %get-tuple-element.113.refs_3_) | copy-start | bytes 3145732
  567.7 8.9 %copy-start.7 = (bf16[512,1024]{1,0:T(8,128)(2,1)S(1)}, bf16[512,1024]{1,0:T(8,128)(2,1)}, u32[]{:S(2)}) copy-start(bf16[512,1024]{1,0:T(8,128)(2,1)} %get-tuple-element.108.refs_3_) | copy-start | bytes 3145732
  575.1 4.0 copy-start.5
  575.1 4.0 copy-start.9
  576.6 2.8 copy-start.10

commit v5 on v4

--- a/solution.py
+++ b/solution.py
@@ -19,9 +19,6 @@
 QTILE = 256
 VMEM_LIMIT = 56 * 1024 * 1024
 
-CROSS_SWAP = [(1, 2), (2, 1)]
-PAIR = ("section", "shard")
-
 
 def rows_product(left, right):
     return lax.dot_general(left, right, ROWS_CONTRACT, preferred_element_type=F32)
@@ -103,16 +100,16 @@
 
 def scatter_kernel(size, count, *refs):
     sources, refs = refs[: 6 * count], refs[6 * count :]
-    small, refs = refs[0], refs[1:]
-    out, refs = refs[: count + 1], refs[count + 1 :]
+    tallies, refs = refs[:3], refs[3:]
+    out, refs = refs[:count], refs[count:]
+    packed, refs = refs[0], refs[1:]
     held, refs = refs[: 2 * count], refs[2 * count :]
     own, refs = refs[:count], refs[count:]
     landed, refs = refs[:count], refs[count:]
-    load_sem, send_sem, recv_sem, small_send, small_recv = refs
-    small_out = out[count]
+    load_sem, send_sem, recv_sem, small_send, small_recv, swap_sem, total, small, small_out = refs
     place, following, previous = ring_place(size)
     targets = ({"replica": following}, {"replica": previous})
-    layer = lax.axis_index("shard")
+    core, layer, _, _, diagonal = neighbours()
 
     def load(number, which):
         rows = held[number].shape[0] // 2
@@ -133,7 +130,7 @@
         def _(number=number):
             load(number, 2).start()
 
-    greet(targets)
+    greet(targets + (diagonal,))
 
     def send(way, item, source, slot):
         return pltpu.make_async_remote_copy(
@@ -171,8 +168,41 @@
         for index in range(group):
             own[item][way, part * group + index] = result[index * deep : (index + 1) * deep].astype(BF)
 
-    small_out[place] = small[...]
-    send_small(place, 0).start()
+    half = small.shape[1]
+
+    @pl.when(layer == 0)
+    def _():
+        total[...] = tallies[1][...] + tallies[2][...]
+
+    @pl.when(layer != 0)
+    def _():
+        total[...] = tallies[0][...] + tallies[1][...]
+
+    small[...] = jnp.zeros_like(small)
+    small[0:6, :] = total[0:6, pl.ds(pl.multiple_of(core * half, half), half)]
+    for row in range(3):
+        for side in range(2):
+            line = 6 + 2 * row + side
+            small[line : line + 1, :] = total[6 + row : 7 + row, side * half : (side + 1) * half]
+
+    def swap():
+        return pltpu.make_async_remote_copy(
+            src_ref=small,
+            dst_ref=small_out.at[place],
+            send_sem=swap_sem.at[0],
+            recv_sem=swap_sem.at[1],
+            device_id=diagonal,
+            device_id_type=MESH,
+        )
+
+    @pl.when(core == layer)
+    def _():
+        small_out[place] = small[...]
+
+    @pl.when(core != layer)
+    def _():
+        swap().start()
+
     for item in range(count):
         for number in (2 * item, 2 * item + 1):
             load(number, 1).wait()
@@ -180,6 +210,12 @@
         for way in range(2):
             product(item, way, first[way] // group)
             send(way, item, own[item].at[way, first[way]], 0).start()
+
+    @pl.when(core != layer)
+    def _():
+        swap().wait()
+
+    send_small(place, 0).start()
     for item in range(count):
         for way in range(2):
             product(item, way, 1 - first[way] // group)
@@ -204,6 +240,10 @@
             send(way, item, here, last).wait_recv()
             out[item][way] = here[...] + own[item][way, place]
     send_small((place + 1) % size, last).wait_recv()
+    gathered = small_out[0]
+    for index in range(1, size):
+        gathered = gathered + small_out[index]
+    packed[...] = gathered
 
     def finish(slot, carry):
         for item in range(count):
@@ -215,9 +255,10 @@
     lax.fori_loop(0, size - 1, finish, 0)
 
 
-def ring_scatter(factors, small, size):
+def ring_scatter(factors, tallies, size):
     count = len(factors)
     flat = [item for pair in factors for item in pair]
+    half = tallies[0].shape[1] // 2
     shapes = [(2 * item[0].shape[0], item[0].shape[1]) for item in flat]
     chunks = [
         (shapes[2 * i][1] // (2 * size), shapes[2 * i + 1][1]) for i in range(count)
@@ -227,26 +268,35 @@
     return pl.pallas_call(
         functools.partial(scatter_kernel, size, count),
         out_shape=[jax.ShapeDtypeStruct((2,) + chunk, BF) for chunk in chunks]
-        + [jax.ShapeDtypeStruct((size,) + small.shape, small.dtype)],
-        in_specs=[spot] * (6 * count) + [whole],
+        + [jax.ShapeDtypeStruct((16, half), F32)],
+        in_specs=[spot] * (6 * count) + [whole] * 3,
         out_specs=[whole] * (count + 1),
         scratch_shapes=[pltpu.VMEM(shape, BF) for shape in shapes]
         + [pltpu.VMEM((2, size) + chunk, BF) for chunk in chunks]
         + [pltpu.VMEM((2, size - 1) + chunk, BF) for chunk in chunks]
         + [pltpu.SemaphoreType.DMA((2 * count, 2))]
         + [pltpu.SemaphoreType.DMA((2, count, size - 1))] * 2
-        + [pltpu.SemaphoreType.DMA((size - 1,))] * 2,
+        + [pltpu.SemaphoreType.DMA((size - 1,))] * 2
+        + [pltpu.SemaphoreType.DMA((2,))]
+        + [
+            pltpu.VMEM((16, 2 * half), F32),
+            pltpu.VMEM((16, half), F32),
+            pltpu.VMEM((size, 16, half), F32),
+        ],
         compiler_params=pltpu.CompilerParams(
             collective_id=0, has_side_effects=True, vmem_limit_bytes=VMEM_LIMIT
         ),
         name="ring_scatter",
-    )(*[block for item in flat for block in item], small)
+    )(*[block for item in flat for block in item], *tallies)
 
 
 def gather_kernel(size, groups, *refs):
     count = 4
-    own, out = refs[:count], refs[count : 2 * count]
-    swap_send, swap_recv, send_sem, recv_sem = refs[2 * count :]
+    own, refs = refs[:count], refs[count:]
+    near, refs = refs[:12], refs[12:]
+    out, refs = refs[:count], refs[count:]
+    placed, refs = refs[:2], refs[2:]
+    swap_send, swap_recv, send_sem, recv_sem, place_send, place_recv, load_sem, bounce = refs
     place, following, previous = ring_place(size)
     targets = ({"replica": following}, {"replica": previous})
     core, layer, sibling, across, diagonal = neighbours()
@@ -299,6 +349,54 @@
                 for copy in copies(item, layer, 1, 1, sibling):
                     copy.start()
 
+    part = placed[0].shape[1]
+
+    def near_rows(number, block, shard):
+        return near[6 * block + number].at[pl.ds(shard * part, part)]
+
+    def place_remote(kind, block):
+        number, shard = ((1, 0), (3, 1))[kind]
+        return pltpu.make_async_remote_copy(
+            src_ref=near_rows(number, block, shard),
+            dst_ref=placed[kind].at[block],
+            send_sem=place_send.at[block],
+            recv_sem=place_recv.at[block],
+            device_id=across,
+            device_id_type=MESH,
+        )
+
+    def place_load(number, block, shard):
+        lane = 2 * (number // 3) + block
+        return pltpu.make_async_copy(near_rows(number, block, shard), bounce.at[lane], load_sem.at[lane])
+
+    def place_store(number, block):
+        kind = number // 3
+        lane = 2 * kind + block
+        return pltpu.make_async_copy(bounce.at[lane], placed[kind].at[block], load_sem.at[lane])
+
+    local = {(0, 0): (0, 3), (0, 1): (2,), (1, 0): (5,), (1, 1): (1, 4)}
+
+    def on_device(action):
+        for (at_core, at_layer), numbers in local.items():
+
+            @pl.when((core == at_core) & (layer == at_layer))
+            def _(numbers=numbers, at_layer=at_layer):
+                for number in numbers:
+                    for block in range(2):
+                        action(number, block, at_layer)
+
+    @pl.when(same & (layer == 1))
+    def _():
+        for block in range(2):
+            place_remote(0, block).start()
+
+    @pl.when(same & (layer == 0))
+    def _():
+        for block in range(2):
+            place_remote(1, block).start()
+
+    on_device(lambda number, block, shard: place_load(number, block, shard).start())
+
     def send(way, item, chunk, slot):
         if item < len(groups):
             deep = out[item].shape[1] // 2
@@ -348,11 +446,32 @@
                 send(way, item, chunk, slot + 1).start()
         return carry
 
+    def moved(number, block, shard):
+        place_load(number, block, shard).wait()
+        place_store(number, block).start()
+
+    on_device(moved)
     lax.fori_loop(0, size - 2, step, 0)
     last = size - 2
     for item in range(count):
         for way in range(2):
             send(way, item, chunk_of(way, last), last).wait_recv()
+    on_device(lambda number, block, shard: place_store(number, block).wait())
+
+    @pl.when(same)
+    def _():
+        for block in range(2):
+            place_remote(0, block).wait_send()
+
+    @pl.when((core != layer) & (layer == 0))
+    def _():
+        for block in range(2):
+            place_remote(0, block).wait_recv()
+
+    @pl.when((core != layer) & (layer == 1))
+    def _():
+        for block in range(2):
+            place_remote(1, block).wait_recv()
 
     @pl.when(same)
     def _():
@@ -378,31 +497,111 @@
     lax.fori_loop(0, size - 1, finish, 0)
 
 
-def ring_gather(pieces, groups, size):
+def ring_gather(pieces, groups, near, size):
     spot = pl.BlockSpec(memory_space=pl.ANY)
     shapes = [(size, item.shape[1], 2 * item.shape[2]) for item in pieces[: len(groups)]]
     shapes += [(2, size) + item.shape[1:] for item in pieces[len(groups) :]]
     count = len(pieces)
+    rows = (near[0].shape[0] // 2, near[0].shape[1])
+    whole = pl.BlockSpec(memory_space=pltpu.VMEM)
     return pl.pallas_call(
         functools.partial(gather_kernel, size, groups),
-        out_shape=[jax.ShapeDtypeStruct(shape, BF) for shape in shapes],
-        in_specs=[pl.BlockSpec(memory_space=pltpu.VMEM)] * count,
-        out_specs=[spot] * count,
+        out_shape=[jax.ShapeDtypeStruct(shape, BF) for shape in shapes]
+        + [jax.ShapeDtypeStruct((2,) + rows, BF)] * 2,
+        in_specs=[whole] * count + [spot] * 12,
+        out_specs=[whole] * count + [spot] * 2,
         scratch_shapes=[
             pltpu.SemaphoreType.DMA((count, 2, 3)),
             pltpu.SemaphoreType.DMA((count, 4, 3)),
         ]
-        + [pltpu.SemaphoreType.DMA((2, count, size - 1))] * 2,
-        compiler_params=pltpu.CompilerParams(collective_id=1, has_side_effects=True),
+        + [pltpu.SemaphoreType.DMA((2, count, size - 1))] * 2
+        + [pltpu.SemaphoreType.DMA((2,))] * 2
+        + [pltpu.SemaphoreType.DMA((4,)), pltpu.VMEM((4,) + rows, BF)],
+        compiler_params=pltpu.CompilerParams(
+            collective_id=1, has_side_effects=True, vmem_limit_bytes=VMEM_LIMIT
+        ),
         name="ring_gather",
-    )(*pieces)
+    )(*pieces, *near)
+
+
+def finish_kernel(*refs):
+    gathered, packed, placed = refs[:4], refs[4], refs[5:7]
+    wide, vectors, moved = refs[7:11], refs[11:20], refs[20:22]
+    buffers, bounce = refs[22:26], refs[26]
+    store_sem, load_sem = refs[27:]
+    loads = [pltpu.make_async_copy(placed[i], bounce.at[i], load_sem.at[i]) for i in range(2)]
+    for copy in loads:
+        copy.start()
+    half = packed.shape[1]
+    for number in range(9):
+        for index in range(vectors[number].shape[1] // half):
+            row = number + index
+            vectors[number][:, index * half : (index + 1) * half] = packed[row : row + 1, :]
+    stores = [pltpu.make_async_copy(bounce.at[i], moved[i], load_sem.at[i]) for i in range(2)]
+    for i in range(2):
+        loads[i].wait()
+        stores[i].start()
+
+    def store(item, chunk):
+        deep = gathered[item].shape[1]
+        place = pl.ds(pl.multiple_of(chunk * deep, deep), deep)
+        return pltpu.make_async_copy(
+            buffers[item].at[chunk], wide[item].at[place], store_sem.at[item, chunk]
+        )
+
+    for item in range(4):
+
+        def step(chunk, carry, item=item):
+            buffers[item][chunk] = gathered[item][chunk].astype(F32)
+            store(item, chunk).start()
+            return carry
+
+        lax.fori_loop(0, gathered[item].shape[0], step, 0)
+    for item in range(4):
+
+        def drain(chunk, carry, item=item):
+            store(item, chunk).wait()
+            return carry
+
+        lax.fori_loop(0, gathered[item].shape[0], drain, 0)
+    for copy in stores:
+        copy.wait()
+
+
+def finish(gathered, packed, placed):
+    spot = pl.BlockSpec(memory_space=pl.ANY)
+    whole = pl.BlockSpec(memory_space=pltpu.VMEM)
+    gathered = [item.reshape((-1,) + item.shape[-2:]) for item in gathered]
+    half = packed.shape[1]
+    return pl.pallas_call(
+        finish_kernel,
+        out_shape=[
+            jax.ShapeDtypeStruct((item.shape[0] * item.shape[1], item.shape[2]), F32)
+            for item in gathered
+        ]
+        + [jax.ShapeDtypeStruct((1, half), F32)] * 8
+        + [jax.ShapeDtypeStruct((1, 4 * half), F32)]
+        + [jax.ShapeDtypeStruct(item.shape, BF) for item in placed],
+        in_specs=[whole] * 5 + [spot] * 2,
+        out_specs=[spot] * 4 + [whole] * 9 + [spot] * 2,
+        scratch_shapes=[pltpu.VMEM(item.shape, F32) for item in gathered]
+        + [pltpu.VMEM((2,) + placed[0].shape, BF)]
+        + [
+            pltpu.SemaphoreType.DMA((4, max(item.shape[0] for item in gathered))),
+            pltpu.SemaphoreType.DMA((2,)),
+        ],
+        compiler_params=pltpu.CompilerParams(vmem_limit_bytes=VMEM_LIMIT),
+        name="finish",
+    )(*gathered, packed, *placed)
 
 
 def fetch_kernel(*refs):
-    tokens, cotangent, small, qkv, fc, out, proj = refs[:7]
-    *outer, small_out, w_qkv, w_fc, w_out, w_proj = refs[7:14]
-    send_sem, recv_sem, extra_send, extra_recv, local_sem = refs[14:19]
-    buffers = refs[19:]
+    tokens, cotangent, qkv, fc, out, proj = refs[:6]
+    vectors, refs = refs[6:15], refs[15:]
+    *outer, params, w_qkv, w_fc, w_out, w_proj = refs[:7]
+    send_sem, recv_sem, extra_send, extra_recv, local_sem, vector_sem = refs[7:13]
+    raw, small, small_out = refs[13:22], refs[22], refs[23]
+    buffers = refs[24:]
     core, layer, sibling, across, diagonal = neighbours()
     index = lax.axis_index("replica")
     quarter = index % 4
@@ -413,6 +612,8 @@
     above_quarter = quarter + 2 - 4 * high
     same = core == layer
     far_quarter = 3 - quarter
+    for number in range(9):
+        pltpu.make_async_copy(vectors[number], raw[number], vector_sem.at[number]).start()
     greet((sibling, across, diagonal, beside, above))
 
     depth = qkv.shape[0]
@@ -555,9 +756,6 @@
             device_id_type=MESH,
         )
 
-    def small_local():
-        return through(small, small_out.at[core], 9)
-
     def start_outer(block):
         @pl.when(layer == 0)
         def _():
@@ -572,14 +770,6 @@
             cross_same(item).start()
         cross_swap(item).start()
 
-    @pl.when(same)
-    def _():
-        small_local()[0]().start()
-
-    @pl.when(core != layer)
-    def _():
-        small_swap().start()
-
     start_outer(0)
 
     @pl.when(core != layer)
@@ -601,13 +791,22 @@
     def _():
         for item in range(4):
             to_sibling(item).start()
-        load, store = small_local()
-        load().wait()
-        store().start()
-        store().wait()
+
+    span_small = small.shape[1]
+    for number in range(9):
+        pltpu.make_async_copy(vectors[number], raw[number], vector_sem.at[number]).wait()
+        values = raw[number][...].astype(F32)
+        for index in range(values.shape[1] // span_small):
+            row = number + index
+            small[row : row + 1, :] = values[:, index * span_small : (index + 1) * span_small]
+
+    @pl.when(same)
+    def _():
+        small_out[core] = small[...]
 
     @pl.when(core != layer)
     def _():
+        small_swap().start()
         small_swap().wait_recv()
 
     small_pass().start()
@@ -676,18 +875,24 @@
     for block in range(2):
         outer_local(tokens, block)[1]().wait()
     small_pass().wait()
+    params[...] = jnp.zeros_like(params)
+    for side in range(2):
+        lanes = slice(side * span_small, (side + 1) * span_small)
+        params[0:6, lanes] = small_out[side, 0:6]
+        for row in range(3):
+            line = 6 + 2 * row + side
+            params[6 + row : 7 + row, lanes] = small_out[core, line : line + 1]
     for block in range(2):
         outer_cross(block)(tokens).wait_send()
         outer_pass(block).wait()
 
 
-def fetch_inputs(tokens, cotangent, small, qkv, fc, out, proj):
+def fetch_inputs(tokens, cotangent, qkv, fc, out, proj, vectors):
     spot = pl.BlockSpec(memory_space=pl.ANY)
     _, part, width = tokens.shape
     shapes = [
         (2 * part, width),
         (2 * part, width),
-        (2,) + small.shape,
         (2 * qkv.shape[0], qkv.shape[1] // 2),
         (2 * fc.shape[0], fc.shape[1] // 2),
         out.shape,
@@ -695,16 +900,21 @@
     ]
     return pl.pallas_call(
         fetch_kernel,
-        out_shape=[jax.ShapeDtypeStruct(shape, BF) for shape in shapes],
-        in_specs=[spot] * 7,
-        out_specs=[spot] * 7,
+        out_shape=[jax.ShapeDtypeStruct(shape, BF) for shape in shapes[:2]]
+        + [jax.ShapeDtypeStruct((16, width), F32)]
+        + [jax.ShapeDtypeStruct(shape, BF) for shape in shapes[2:]],
+        in_specs=[spot] * 15,
+        out_specs=[spot] * 2 + [pl.BlockSpec(memory_space=pltpu.VMEM)] + [spot] * 4,
         scratch_shapes=[
             pltpu.SemaphoreType.DMA((7, 7)),
             pltpu.SemaphoreType.DMA((7, 7)),
             pltpu.SemaphoreType.DMA((6,)),
             pltpu.SemaphoreType.DMA((6,)),
-            pltpu.SemaphoreType.DMA((10,)),
+            pltpu.SemaphoreType.DMA((9,)),
+            pltpu.SemaphoreType.DMA((9,)),
         ]
+        + [pltpu.VMEM(item.shape, BF) for item in vectors]
+        + [pltpu.VMEM((16, width // 2), F32), pltpu.VMEM((2, 16, width // 2), F32)]
         + [pltpu.VMEM((qkv.shape[0], qkv.shape[1] // 6), BF)] * 3
         + [
             pltpu.VMEM((fc.shape[0], fc.shape[1] // 2), BF),
@@ -713,13 +923,12 @@
             pltpu.VMEM((proj.shape[0] // 2, width), BF),
             pltpu.VMEM(tokens.shape[1:], BF),
             pltpu.VMEM(tokens.shape[1:], BF),
-            pltpu.VMEM(small.shape, BF),
         ],
         compiler_params=pltpu.CompilerParams(
             collective_id=2, has_side_effects=True, vmem_limit_bytes=VMEM_LIMIT
         ),
         name="fetch_inputs",
-    )(tokens, cotangent, small, qkv, fc, out, proj)
+    )(tokens, cotangent, qkv, fc, out, proj, *vectors)
 
 
 TILES = 2
@@ -1352,55 +1561,31 @@
     proj_weight,
     proj_bias,
 ):
-    core = lax.axis_index("section")
-    layer = lax.axis_index("shard")
     size = lax.axis_size("replica")
-    own = core == layer
-    first = layer == 0
-    left = core == 0
-    micro, part, width = tokens.shape[1:]
+    micro = tokens.shape[1]
     assert micro == 2
-    rows = 2 * part
-    half = width // 2
-
-    def pair_permute(value, pairs):
-        return lax.ppermute(value, PAIR, pairs)
-
-    small = jnp.concatenate(
-        [
-            item[0]
-            for item in (
-                attn_gain,
-                attn_shift,
-                out_bias,
-                mlp_gain,
-                mlp_shift,
-                proj_bias,
-                query_bias,
-                value_bias,
-                fc_bias,
-            )
-        ]
-    ).reshape(-1, 128)
-    *outer, small_both, w_qkv, w_fc, w_out, w_proj = fetch_inputs(
-        tokens[0], cotangent[0], small, qkv_weight[0], fc_weight[0], out_weight[0], proj_weight[0]
-    )
-    flat = small_both.reshape(2, -1).astype(F32)
-    mine = jnp.where(left, flat[0], flat[1])
-    params = jnp.concatenate(
-        [
-            flat[0, : 6 * half].reshape(6, half),
-            flat[1, : 6 * half].reshape(6, half),
-        ],
-        axis=1,
-    )
-    params = jnp.concatenate(
-        [params, mine[6 * half :].reshape(-1, width), jnp.zeros((7, width), F32)], axis=0
+    *outer, params, w_qkv, w_fc, w_out, w_proj = fetch_inputs(
+        tokens[0],
+        cotangent[0],
+        qkv_weight[0],
+        fc_weight[0],
+        out_weight[0],
+        proj_weight[0],
+        (
+            attn_gain,
+            attn_shift,
+            out_bias,
+            mlp_gain,
+            mlp_shift,
+            proj_bias,
+            query_bias,
+            value_bias,
+            fc_bias,
+        ),
     )
     weights = (w_qkv, w_out, w_fc, w_proj)
 
-    empty = jnp.zeros((rows, half), BF)
-    received, kept_list, outputs, past, got = [], [], [], (empty, empty), outer[0]
+    received, kept_list, outputs, past, got = [], [], [], (w_out, w_out), outer[0]
     for step in range(micro + 1):
         output = outputs[-1] if outputs else outer[0]
         used, normed1, *state, normed2, slope, act, output, got = forward_step(
@@ -1418,10 +1603,9 @@
         kept_list.append((kept, normed1, normed2, act))
         past = (keys, values)
 
-    pending = (jnp.zeros((rows, half), F32), jnp.zeros((rows, half), F32))
-    grad_received, terms_list, results, sums, got = [], [], [], None, outer[1]
+    pending = (params, params)
+    grad_received, terms_list, results, tallies, got = [], [], [], [], outer[1]
     for step in range(micro + 1):
-        active = jnp.where(first, step >= 1, step < micro)
         last = micro - step
         kept, normed1, normed2, act = kept_list[last]
         result = results[-1] if results else outer[1]
@@ -1437,58 +1621,26 @@
         )
         results.append(result)
         grad_received.append(grad)
-        vector = jnp.where(active, vector, 0.0)
-        sums = vector if sums is None else sums + vector
+        tallies.append(vector)
         terms_list.append((normed1, d_qkv, kept[5], d_branch, normed2, d_pre, act, grad))
-    full = lax.dynamic_slice_in_dim(sums[:6], core * half, half, 1)
-    sums = jnp.concatenate([full.reshape(-1), sums[6:9].reshape(-1)])
-
     def factor(number):
         return tuple(terms_list[step][number] for step in (2, 1, 0))
 
     factors = [(factor(i), factor(i + 1)) for i in (0, 4, 2, 6)]
-    sums = sums.reshape(-1, 128)
-    sums = jnp.where(own, sums, pair_permute(sums, CROSS_SWAP))
-    *reduced, sums = ring_scatter(factors, sums, size)
-    sums = jnp.sum(sums, axis=0).reshape(-1)
-    vectors = [sums[i * half : (i + 1) * half][None] for i in range(8)] + [sums[8 * half :][None]]
-    qkv_grad, fc_grad, out_grad, proj_grad = (
-        item.astype(F32).reshape(1, -1, item.shape[-1])
-        for item in ring_gather(reduced, (3, 1), size)
-    )
-
-    def placed(mine, arrived, pairs, far):
-        near = lax.dynamic_slice_in_dim(mine, layer * part, part, 0)
-        give = lax.dynamic_slice_in_dim(mine, (1 - layer) * part, part, 0)
-        sent = pair_permute(give, pairs)
-        piped = lax.dynamic_slice_in_dim(arrived, layer * part, part, 0)
-        return jnp.where(own, near, jnp.where(far, piped, sent))
-
-    activations = jnp.stack(
-        [
-            placed(
-                jnp.where(first, outputs[i], outputs[i + 1]),
-                received[i + 1],
-                [(3, 2)],
-                layer == 1,
-            )
-            for i in range(micro)
-        ]
-    )[None, None]
-    input_grads = jnp.stack(
-        [
-            placed(
-                jnp.where(first, results[micro - i], results[micro - 1 - i]),
-                grad_received[micro - i],
-                [(0, 1)],
-                layer == 0,
-            )
-            for i in range(micro)
-        ]
-    )[None, None]
+    reduced = ring_scatter(factors, tallies, size)
+    reduced, packed = reduced[:4], reduced[4]
+    near = []
+    for i in range(micro):
+        near += [outputs[i], outputs[i + 1], received[i + 1]]
+        near += [results[micro - i], results[micro - 1 - i], grad_received[micro - i]]
+    *gathered, activations, input_grads = ring_gather(reduced, (3, 1), near, size)
+    finished = finish(gathered, packed, (activations, input_grads))
+    qkv_grad, fc_grad, out_grad, proj_grad = (item[None] for item in finished[:4])
+    vectors = finished[4:13]
+    activations, input_grads = finished[13:]
     return (
-        activations,
-        input_grads,
+        activations[None, None],
+        input_grads[None, None],
         vectors[0],
         vectors[1],
         qkv_grad,

time: 585 us -> 558 us (0.954)
  other arithmetic: 35.5 us -> 0 us
  Pallas kernels: 525 us -> 547 us
  local copies, waits for them, and re-layouts: 10.1 us -> 0 us
  starting transfers between devices: 7.83 us -> 0 us
    reshape x4 -> x0, other arithmetic: 19.9 us -> none  [shards(): item.astype(F32).reshape(1, -1, item.shape[-1])]
    pallas_call x0 -> x1, Pallas kernels: none -> 16 us  [finish(): pl.pallas_call(finish_kernel, out_shape=[jax.ShapeDtypeStruct((item.shape...]
    ppermute x5 -> x0, starting transfers between devices: 7.83 us -> none  [pair_permute(): return lax.ppermute(value, PAIR, pairs)]
    unnamed x11 -> x0, other arithmetic: 7.09 us -> none
  transfers between devices with their start and end apart: 5 -> 0, of which waited for: 1 -> 0; matrix products, arithmetic and copies ran while one was open for 5% -> 0% of each run, Pallas kernels for 62% -> 0%
where the time goes in v5:
time: 558 us; the launch traced here: 548 us
  Pallas kernels  547 us (98%)
    pallas_call x1, Pallas kernels, ring_scatter(): pl.pallas_call(functools.partial(scatter_kernel, size, count), out_shape=...  132 us
    pallas_call x1, Pallas kernels, ring_gather(): pl.pallas_call(functools.partial(gather_kernel, size, groups), out_shape=...  131 us
    pallas_call x3, Pallas kernels, backward_step(): pl.pallas_call(functools.partial(backward_kernel, mode, passing), out_sha...  99.9 us
    pallas_call x3, Pallas kernels, forward_step(): pl.pallas_call(functools.partial(forward_kernel, mode, passing), out_shap...  90.8 us
    pallas_call x1, Pallas kernels, fetch_inputs(): pl.pallas_call(fetch_kernel, out_shape=[jax.ShapeDtypeStruct(shape, BF) f...  77.5 us
    pallas_call x1, Pallas kernels, finish(): pl.pallas_call(finish_kernel, out_shape=[jax.ShapeDtypeStruct((item.shape...  16 us

profile of v5, /device:TPU:1, one launch (start us, length us, event | category | flops | bytes accessed | tf_op | source)
XLA Modules:
  0.0 548.5 jit_solution(5252497580595564939)
XLA Ops:
  0.7 77.5 %fetch_inputs.1 = (bf16[512,1024]{1,0:T(8,128)(2,1)}, bf16[512,1024]{1,0:T(8,128)(2,1)}, f32[16,1024]{1,0:T(8,128)}, bf16[1024,1536]{1,0:T(8,128)(2,1)}, bf16[10...) custom-call(bf16[2,256,1024]{2,1,0:T(8,128)(2,1)} %bitcast.19, ...), custom_call_target="tpu_custom_call" | custom-call | tf_op jit(solution)/shard_map/fetch_inputs/pallas_call | solution.py:901
  78.1 24.9 %forward_step.3 = (bf16[512,1024]{1,0:T(8,128)(2,1)}, bf16[512,1024]{1,0:T(8,128)(2,1)}, bf16[512,512]{1,0:T(8,128)(2,1)}, bf16[512,512]{1,0:T(8,128)(2,1)}, bf1...) custom-call(bf16[512,1024]{1,0:T(8,128)(2,1)} %get-tuple-element.113, ...), custom_call_target="tpu_custom_call" | custom-call | tf_op jit(solution)/shard_map/forward_step/pallas_call | solution.py:1294
  103.1 36.4 %forward_step.4 = (bf16[512,1024]{1,0:T(8,128)(2,1)}, bf16[512,1024]{1,0:T(8,128)(2,1)}, bf16[512,512]{1,0:T(8,128)(2,1)}, bf16[512,512]{1,0:T(8,128)(2,1)}, bf1...) custom-call(bf16[512,1024]{1,0:T(8,128)(2,1)} %get-tuple-element.120, ...), custom_call_target="tpu_custom_call" | custom-call | tf_op jit(solution)/shard_map/forward_step/pallas_call | solution.py:1294
  139.4 29.5 %forward_step.5 = (bf16[512,1024]{1,0:T(8,128)(2,1)}, bf16[512,1024]{1,0:T(8,128)(2,1)}, bf16[512,512]{1,0:T(8,128)(2,1)}, bf16[512,512]{1,0:T(8,128)(2,1)}, bf1...) custom-call(bf16[512,1024]{1,0:T(8,128)(2,1)} %get-tuple-element.120, ...), custom_call_target="tpu_custom_call" | custom-call | tf_op jit(solution)/shard_map/forward_step/pallas_call | solution.py:1294
  168.9 29.7 %backward_step.3 = (bf16[512,1024]{1,0:T(8,128)(2,1)}, bf16[512,1536]{1,0:T(8,128)(2,1)}, bf16[512,1024]{1,0:T(8,128)(2,1)}, bf16[512,2048]{1,0:T(8,128)(2,1)}, ...) custom-call(bf16[512,1024]{1,0:T(8,128)(2,1)} %get-tuple-element.120, ...), custom_call_target="tpu_custom_call" | custom-call | tf_op jit(solution)/shard_map/backward_step/pallas_call | solution.py:1533
  198.6 45.3 %backward_step.4 = (bf16[512,1024]{1,0:T(8,128)(2,1)}, bf16[512,1536]{1,0:T(8,128)(2,1)}, bf16[512,1024]{1,0:T(8,128)(2,1)}, bf16[512,2048]{1,0:T(8,128)(2,1)}, ...) custom-call(bf16[512,1024]{1,0:T(8,128)(2,1)} %get-tuple-element.140, ...), custom_call_target="tpu_custom_call" | custom-call | tf_op jit(solution)/shard_map/backward_step/pallas_call | solution.py:1533
  243.9 25.0 %backward_step.5 = (bf16[512,1024]{1,0:T(8,128)(2,1)}, bf16[512,1536]{1,0:T(8,128)(2,1)}, bf16[512,1024]{1,0:T(8,128)(2,1)}, bf16[512,2048]{1,0:T(8,128)(2,1)}, ...) custom-call(bf16[512,1024]{1,0:T(8,128)(2,1)} %get-tuple-element.151, ...), custom_call_target="tpu_custom_call" | custom-call | tf_op jit(solution)/shard_map/backward_step/pallas_call | solution.py:1533
  268.9 132.1 %ring_scatter.1 = (bf16[2,64,1536]{2,1,0:T(8,128)(2,1)}, bf16[2,64,2048]{2,1,0:T(8,128)(2,1)}, bf16[2,32,1024]{2,1,0:T(8,128)(2,1)}, bf16[2,128,1024]{2,1,0:T(8,128)(2,1)}, f32[16,512]{1,0:T(8,128)}) custom-call(bf16[512,1024]{1,0:T(8,128)(2,1)} %get-tuple-element.119.refs_0_, bf16[512,1024]{1,0:T(8,128)(2,1)} %get-tuple-element.125.refs_1_, ...), custom_call_target="tpu_custom_call" | custom-call | tf_op jit(solution)/shard_map/ring_scatter/pallas_call | solution.py:268
  401.0 131.1 %ring_gather.1 = (bf16[8,64,3072]{2,1,0:T(8,128)(2,1)}, bf16[8,64,4096]{2,1,0:T(8,128)(2,1)}, bf16[2,8,32,1024]{3,2,1,0:T(8,128)(2,1)}, bf16[2,8,128,1024]{3,2,1...) custom-call(bf16[2,64,1536]{2,1,0:T(8,128)(2,1)} %get-tuple-element.183.refs_0_, ...), custom_call_target="tpu_custom_call" | custom-call | tf_op jit(solution)/shard_map/ring_gather/pallas_call | solution.py:507
  532.1 16.0 %finish.1 = (f32[512,3072]{1,0:T(8,128)}, f32[512,4096]{1,0:T(8,128)}, f32[512,1024]{1,0:T(8,128)}, f32[2048,1024]{1,0:T(8,128)}, f32[1,512]{1,0:T(1,128)}, /*in...) custom-call(bf16[8,64,3072]{2,1,0:T(8,128)(2,1)} %get-tuple-element., ...), custom_call_target="tpu_custom_call" | custom-call | tf_op jit(solution)/shard_map/finish/pallas_call | solution.py:576

commit v6 on v5

--- a/solution.py
+++ b/solution.py
@@ -509,7 +509,7 @@
         out_shape=[jax.ShapeDtypeStruct(shape, BF) for shape in shapes]
         + [jax.ShapeDtypeStruct((2,) + rows, BF)] * 2,
         in_specs=[whole] * count + [spot] * 12,
-        out_specs=[whole] * count + [spot] * 2,
+        out_specs=[spot] * (count + 2),
         scratch_shapes=[
             pltpu.SemaphoreType.DMA((count, 2, 3)),
             pltpu.SemaphoreType.DMA((count, 4, 3)),
@@ -527,8 +527,36 @@
 def finish_kernel(*refs):
     gathered, packed, placed = refs[:4], refs[4], refs[5:7]
     wide, vectors, moved = refs[7:11], refs[11:20], refs[20:22]
-    buffers, bounce = refs[22:26], refs[26]
-    store_sem, load_sem = refs[27:]
+    low, high, bounce = refs[22:26], refs[26:30], refs[30]
+    fetch_sem, store_sem, load_sem = refs[31:]
+
+    def fetch(item, chunk):
+        return pltpu.make_async_copy(
+            gathered[item].at[chunk], low[item].at[chunk], fetch_sem.at[item, chunk]
+        )
+
+    def store(item, chunk):
+        deep = low[item].shape[1]
+        place = pl.ds(pl.multiple_of(chunk * deep, deep), deep)
+        return pltpu.make_async_copy(
+            high[item].at[chunk], wide[item].at[place], store_sem.at[item, chunk]
+        )
+
+    def every(action):
+        for item in range(4):
+
+            def step(chunk, carry, item=item):
+                action(item, chunk)
+                return carry
+
+            lax.fori_loop(0, low[item].shape[0], step, 0)
+
+    def widen(item, chunk):
+        fetch(item, chunk).wait()
+        high[item][chunk] = low[item][chunk].astype(F32)
+        store(item, chunk).start()
+
+    every(lambda item, chunk: fetch(item, chunk).start())
     loads = [pltpu.make_async_copy(placed[i], bounce.at[i], load_sem.at[i]) for i in range(2)]
     for copy in loads:
         copy.start()
@@ -537,33 +565,14 @@
         for index in range(vectors[number].shape[1] // half):
             row = number + index
             vectors[number][:, index * half : (index + 1) * half] = packed[row : row + 1, :]
-    stores = [pltpu.make_async_copy(bounce.at[i], moved[i], load_sem.at[i]) for i in range(2)]
+    every(widen)
+    stores = []
     for i in range(2):
         loads[i].wait()
-        stores[i].start()
-
-    def store(item, chunk):
-        deep = gathered[item].shape[1]
-        place = pl.ds(pl.multiple_of(chunk * deep, deep), deep)
-        return pltpu.make_async_copy(
-            buffers[item].at[chunk], wide[item].at[place], store_sem.at[item, chunk]
-        )
-
-    for item in range(4):
-
-        def step(chunk, carry, item=item):
-            buffers[item][chunk] = gathered[item][chunk].astype(F32)
-            store(item, chunk).start()
-            return carry
-
-        lax.fori_loop(0, gathered[item].shape[0], step, 0)
-    for item in range(4):
-
-        def drain(chunk, carry, item=item):
-            store(item, chunk).wait()
-            return carry
-
-        lax.fori_loop(0, gathered[item].shape[0], drain, 0)
+        copy = pltpu.make_async_copy(bounce.at[i], moved[i], load_sem.at[i])
+        copy.start()
+        stores.append(copy)
+    every(lambda item, chunk: store(item, chunk).wait())
     for copy in stores:
         copy.wait()
 
@@ -573,6 +582,7 @@
     whole = pl.BlockSpec(memory_space=pltpu.VMEM)
     gathered = [item.reshape((-1,) + item.shape[-2:]) for item in gathered]
     half = packed.shape[1]
+    most = max(item.shape[0] for item in gathered)
     return pl.pallas_call(
         finish_kernel,
         out_shape=[
@@ -582,12 +592,14 @@
         + [jax.ShapeDtypeStruct((1, half), F32)] * 8
         + [jax.ShapeDtypeStruct((1, 4 * half), F32)]
         + [jax.ShapeDtypeStruct(item.shape, BF) for item in placed],
-        in_specs=[whole] * 5 + [spot] * 2,
+        in_specs=[spot] * 4 + [whole] + [spot] * 2,
         out_specs=[spot] * 4 + [whole] * 9 + [spot] * 2,
-        scratch_shapes=[pltpu.VMEM(item.shape, F32) for item in gathered]
-        + [pltpu.VMEM((2,) + placed[0].shape, BF)]
+        scratch_shapes=[pltpu.VMEM(item.shape, BF) for item in gathered]
+        + [pltpu.VMEM(item.shape, F32) for item in gathered]
         + [
-            pltpu.SemaphoreType.DMA((4, max(item.shape[0] for item in gathered))),
+            pltpu.VMEM((2,) + placed[0].shape, BF),
+            pltpu.SemaphoreType.DMA((4, most)),
+            pltpu.SemaphoreType.DMA((4, most)),
             pltpu.SemaphoreType.DMA((2,)),
         ],
         compiler_params=pltpu.CompilerParams(vmem_limit_bytes=VMEM_LIMIT),
@@ -776,6 +788,7 @@
     def _():
         crossings(order[0])
         crossings(order[1])
+        crossings(order[2])
 
     @pl.when(layer == 0)
     def _():
@@ -829,8 +842,8 @@
 
         for number, item in enumerate(sequence):
             pass_on(0, item, quarter, beside).wait_recv()
-            if ahead and number + 2 < len(sequence):
-                crossings(sequence[number + 2])
+            if ahead and number + 3 < len(sequence):
+                crossings(sequence[number + 3])
             pass_on(1, item, quarter, beside).start()
             pass_on(2, item, quarter, above).start()
             if number >= 1:
@@ -838,6 +851,7 @@
             if number == 0:
                 outer_cross(0)(tokens).wait_recv()
                 outer_pass(0).start()
+            if number == len(sequence) - 2:
                 start_outer(1)
         onward(sequence[-1])
         for item in sequence:
@@ -1128,6 +1142,11 @@
         copy.start()
         stores.append(copy)
 
+    def store_rows(tile, *pairs):
+        place = pl.ds(tile * tile_rows, tile_rows)
+        for buffer, dest in pairs:
+            store(buffer.at[place], dest.at[place])
+
     def vector(row, start=0, size=None):
         return params[row : row + 1, start : start + (size or width)]
 
@@ -1147,9 +1166,7 @@
         k_v[later, :] = piece.astype(BF)
         piece = jnp.dot(normed, wq_v[:, 2 * half :], preferred_element_type=F32)
         v_v[later, :] = (piece + vector(6, half, half)).astype(BF)
-    store(x_v, x_used)
-    store(n1_v, normed1)
-    store(q_v, query)
+        store_rows(tile, (x_v, x_used), (n1_v, normed1), (q_v, query))
     store(k_v.at[own_rows], keys)
     store(v_v.at[own_rows], values)
     if mode is not False:
@@ -1179,7 +1196,7 @@
                 m_v[span, lanes] = jnp.transpose(jnp.concatenate(pieces, axis=0)).astype(BF)
                 return carry
 
-            lax.fori_loop(0, half // 128, pair, 0)
+            lax.fori_loop(0, half // 128, pair, 0, unroll=mode is not None)
             partial = jnp.dot(m_v[span, :], wo_v[...], preferred_element_type=F32)
             part_v[tile] = partial
             exchange.give(tile, partial)
@@ -1193,6 +1210,7 @@
         span = pl.ds(tile * tile_rows, tile_rows)
         total = part_v[TILES + tile] + exchange.take(TILES + tile)
         o_v[span, :] = (hid_v[span, :] + total + vector(5)).astype(BF)
+        store_rows(tile, (o_v, out))
         if passing:
             across.send(tile)
 
@@ -1205,6 +1223,7 @@
         i2_v[span, :] = jnp.broadcast_to(inverse, (tile_rows, 128))
         normed = (scaled * vector(3) + vector(4)).astype(BF)
         n2_v[span, :] = normed
+        store_rows(tile, (s2_v, scaled2), (i2_v, inverse2), (n2_v, normed2))
         chunk = width // 2
         for part in range(wide // chunk):
             columns = pl.ds(part * chunk, chunk)
@@ -1213,18 +1232,13 @@
             activated, inclined = gelu_pair(pre + bias)
             a_v[span, columns] = activated.astype(BF)
             sl_v[span, columns] = inclined.astype(BF)
+        store_rows(tile, (sl_v, slope), (a_v, act))
         if tile > 0:
             conclude(tile - 1)
         partial = jnp.dot(a_v[span, :], wp_v[...], preferred_element_type=F32)
         part_v[TILES + tile] = partial
         exchange.give(TILES + tile, partial)
-    store(s2_v, scaled2)
-    store(i2_v, inverse2)
-    store(n2_v, normed2)
-    store(sl_v, slope)
-    store(a_v, act)
     conclude(TILES - 1)
-    store(o_v, out)
     for copy in stores:
         copy.wait()
     exchange.finish(2 * TILES)
@@ -1297,7 +1311,7 @@
         in_specs=[spot] * 3 + [pl.BlockSpec(memory_space=pltpu.VMEM)] + [spot] * 6,
         out_specs=[spot] * len(outs),
         scratch_shapes=[pltpu.VMEM(*item) for item in scratch]
-        + step_sems(FORWARD_LOADS + 1, len(outs)),
+        + step_sems(FORWARD_LOADS + 1, 2 * len(outs)),
         compiler_params=pltpu.CompilerParams(
             collective_id=number, has_side_effects=True, vmem_limit_bytes=VMEM_LIMIT
         ),
@@ -1444,7 +1458,7 @@
                 dqkv_v[span, lanes] = d_query.astype(BF)
                 return carry
 
-            lax.fori_loop(0, half // 128, pair, 0)
+            lax.fori_loop(0, half // 128, pair, 0, unroll=mode is not None)
 
     by_past(mode, attention)
     if mode is not False:

time: 558 us -> 545 us (0.977)
  Pallas kernels: 547 us -> 535 us
where the time goes in v6:
time: 545 us; the launch traced here: 536 us
  Pallas kernels  535 us (98%)
    pallas_call x1, Pallas kernels, ring_scatter(): pl.pallas_call(functools.partial(scatter_kernel, size, count), out_shape=...  132 us
    pallas_call x1, Pallas kernels, ring_gather(): pl.pallas_call(functools.partial(gather_kernel, size, groups), out_shape=...  127 us
    pallas_call x3, Pallas kernels, backward_step(): pl.pallas_call(functools.partial(backward_kernel, mode, passing), out_sha...  97.5 us
    pallas_call x3, Pallas kernels, forward_step(): pl.pallas_call(functools.partial(forward_kernel, mode, passing), out_shap...  88.1 us
    pallas_call x1, Pallas kernels, fetch_inputs(): pl.pallas_call(fetch_kernel, out_shape=[jax.ShapeDtypeStruct(shape, BF) f...  74.5 us
    pallas_call x1, Pallas kernels, finish(): pl.pallas_call(finish_kernel, out_shape=[jax.ShapeDtypeStruct((item.shape...  16.3 us

profile of v6, /device:TPU:1, one launch (start us, length us, event | category | flops | bytes accessed | tf_op | source)
XLA Modules:
  0.0 535.9 jit_solution(3355435599768076204)
XLA Ops:
  0.7 74.5 %fetch_inputs.1 = (bf16[512,1024]{1,0:T(8,128)(2,1)}, bf16[512,1024]{1,0:T(8,128)(2,1)}, f32[16,1024]{1,0:T(8,128)}, bf16[1024,1536]{1,0:T(8,128)(2,1)}, bf16[10...) custom-call(bf16[2,256,1024]{2,1,0:T(8,128)(2,1)} %bitcast.19, ...), custom_call_target="tpu_custom_call" | custom-call | tf_op jit(solution)/shard_map/fetch_inputs/pallas_call | solution.py:915
  75.2 23.1 %forward_step.3 = (bf16[512,1024]{1,0:T(8,128)(2,1)}, bf16[512,1024]{1,0:T(8,128)(2,1)}, bf16[512,512]{1,0:T(8,128)(2,1)}, bf16[512,512]{1,0:T(8,128)(2,1)}, bf1...) custom-call(bf16[512,1024]{1,0:T(8,128)(2,1)} %get-tuple-element.113, ...), custom_call_target="tpu_custom_call" | custom-call | tf_op jit(solution)/shard_map/forward_step/pallas_call | solution.py:1308
  98.3 37.1 %forward_step.4 = (bf16[512,1024]{1,0:T(8,128)(2,1)}, bf16[512,1024]{1,0:T(8,128)(2,1)}, bf16[512,512]{1,0:T(8,128)(2,1)}, bf16[512,512]{1,0:T(8,128)(2,1)}, bf1...) custom-call(bf16[512,1024]{1,0:T(8,128)(2,1)} %get-tuple-element.120, ...), custom_call_target="tpu_custom_call" | custom-call | tf_op jit(solution)/shard_map/forward_step/pallas_call | solution.py:1308
  135.4 27.9 %forward_step.5 = (bf16[512,1024]{1,0:T(8,128)(2,1)}, bf16[512,1024]{1,0:T(8,128)(2,1)}, bf16[512,512]{1,0:T(8,128)(2,1)}, bf16[512,512]{1,0:T(8,128)(2,1)}, bf1...) custom-call(bf16[512,1024]{1,0:T(8,128)(2,1)} %get-tuple-element.120, ...), custom_call_target="tpu_custom_call" | custom-call | tf_op jit(solution)/shard_map/forward_step/pallas_call | solution.py:1308
  163.3 28.4 %backward_step.3 = (bf16[512,1024]{1,0:T(8,128)(2,1)}, bf16[512,1536]{1,0:T(8,128)(2,1)}, bf16[512,1024]{1,0:T(8,128)(2,1)}, bf16[512,2048]{1,0:T(8,128)(2,1)}, ...) custom-call(bf16[512,1024]{1,0:T(8,128)(2,1)} %get-tuple-element.120, ...), custom_call_target="tpu_custom_call" | custom-call | tf_op jit(solution)/shard_map/backward_step/pallas_call | solution.py:1547
  191.7 45.3 %backward_step.4 = (bf16[512,1024]{1,0:T(8,128)(2,1)}, bf16[512,1536]{1,0:T(8,128)(2,1)}, bf16[512,1024]{1,0:T(8,128)(2,1)}, bf16[512,2048]{1,0:T(8,128)(2,1)}, ...) custom-call(bf16[512,1024]{1,0:T(8,128)(2,1)} %get-tuple-element.140, ...), custom_call_target="tpu_custom_call" | custom-call | tf_op jit(solution)/shard_map/backward_step/pallas_call | solution.py:1547
  237.0 23.9 %backward_step.5 = (bf16[512,1024]{1,0:T(8,128)(2,1)}, bf16[512,1536]{1,0:T(8,128)(2,1)}, bf16[512,1024]{1,0:T(8,128)(2,1)}, bf16[512,2048]{1,0:T(8,128)(2,1)}, ...) custom-call(bf16[512,1024]{1,0:T(8,128)(2,1)} %get-tuple-element.151, ...), custom_call_target="tpu_custom_call" | custom-call | tf_op jit(solution)/shard_map/backward_step/pallas_call | solution.py:1547
  260.8 131.7 %ring_scatter.1 = (bf16[2,64,1536]{2,1,0:T(8,128)(2,1)}, bf16[2,64,2048]{2,1,0:T(8,128)(2,1)}, bf16[2,32,1024]{2,1,0:T(8,128)(2,1)}, bf16[2,128,1024]{2,1,0:T(8,128)(2,1)}, f32[16,512]{1,0:T(8,128)}) custom-call(bf16[512,1024]{1,0:T(8,128)(2,1)} %get-tuple-element.119.refs_0_, bf16[512,1024]{1,0:T(8,128)(2,1)} %get-tuple-element.125.refs_1_, ...), custom_call_target="tpu_custom_call" | custom-call | tf_op jit(solution)/shard_map/ring_scatter/pallas_call | solution.py:268
  392.5 126.9 %ring_gather.1 = (bf16[8,64,3072]{2,1,0:T(8,128)(2,1)}, bf16[8,64,4096]{2,1,0:T(8,128)(2,1)}, bf16[2,8,32,1024]{3,2,1,0:T(8,128)(2,1)}, bf16[2,8,128,1024]{3,2,1...) custom-call(bf16[2,64,1536]{2,1,0:T(8,128)(2,1)} %get-tuple-element.183.refs_0_, ...), custom_call_target="tpu_custom_call" | custom-call | tf_op jit(solution)/shard_map/ring_gather/pallas_call | solution.py:507
  519.4 16.3 %finish.1 = (f32[512,3072]{1,0:T(8,128)}, f32[512,4096]{1,0:T(8,128)}, f32[512,1024]{1,0:T(8,128)}, f32[2048,1024]{1,0:T(8,128)}, f32[1,512]{1,0:T(1,128)}, /*in...) custom-call(bf16[8,64,3072]{2,1,0:T(8,128)(2,1)} %get-tuple-element., ...), custom_call_target="tpu_custom_call" | custom-call | tf_op jit(solution)/shard_map/finish/pallas_call | solution.py:586

commit v7 on v6

--- a/solution.py
+++ b/solution.py
@@ -963,13 +963,10 @@
             self.made.pop(name).wait()
 
 
-def greet_step(sender, passing):
+def greet_step(sender):
     core, layer, sibling, across, _ = neighbours()
     barrier = pltpu.get_barrier_semaphore()
     pl.semaphore_signal(barrier, inc=1, device_id=sibling, device_id_type=MESH)
-    if not passing:
-        pl.semaphore_wait(barrier, 1)
-        return
 
     @pl.when(layer != sender)
     def _():
@@ -1037,56 +1034,61 @@
         def _():
             self.copy(tile, 0).wait_recv()
             self.copy(tile, 1).start()
+
+    def complete(self, tile):
+        @pl.when(self.layer != self.sender)
+        def _():
             self.copy(tile, 1).wait_recv()
 
-    def finish(self):
+    def finish(self, tile):
         @pl.when(self.layer == self.sender)
         def _():
-            for tile in range(TILES):
-                self.copy(tile, 0).wait_send()
+            self.copy(tile, 0).wait_send()
 
         @pl.when(self.layer != self.sender)
         def _():
-            for tile in range(TILES):
-                self.copy(tile, 1).wait_send()
+            self.copy(tile, 1).wait_send()
 
 
 class Opening:
-    def __init__(self, passing, sender, first_ref, other_ref, earlier, buffer, sem, sems):
-        self.passing, self.sender, self.layer = passing, sender, lax.axis_index("shard")
-        self.load = lambda ref: pltpu.make_async_copy(ref, buffer, sem)
-        self.refs = (first_ref, other_ref)
+    def __init__(self, starting, sender, late, refs, earlier, buffer, load_sems, sems):
+        self.starting, self.sender, self.late, self.refs = starting, sender, late, refs
+        self.buffer, self.load_sems, self.layer = buffer, load_sems, lax.axis_index("shard")
         self.across = Across(sender, earlier, buffer, sems)
+
+    def load(self, ref, tile):
+        rows = self.buffer.shape[0] // TILES
+        place = pl.ds(tile * rows, rows)
+        return pltpu.make_async_copy(ref.at[place], self.buffer.at[place], self.load_sems[tile])
 
     def start(self):
         for layer, ref in enumerate(self.refs):
-            if self.passing and layer != self.sender:
-                continue
 
             @pl.when(self.layer == layer)
-            def _(ref=ref):
-                self.load(ref).start()
+            def _(ref=ref, layer=layer):
+                for tile in range(TILES):
+                    if not (self.starting and layer != self.sender and tile == self.late):
+                        self.load(ref, tile).start()
 
     def send(self):
-        if self.passing:
-            for tile in range(TILES):
-                self.across.send(tile)
+        if self.starting:
+            self.across.send(self.late)
 
     def take(self, tile):
-        if self.passing:
-            if tile == 0:
-
-                @pl.when(self.layer == self.sender)
-                def _():
-                    self.load(self.refs[0]).wait()
+        if self.starting and tile == self.late:
+
+            @pl.when(self.layer == self.sender)
+            def _():
+                self.load(self.refs[0], tile).wait()
 
             self.across.receive(tile)
-        elif tile == 0:
-            self.load(self.refs[0]).wait()
+            self.across.complete(tile)
+        else:
+            self.load(self.refs[0], tile).wait()
 
     def finish(self):
-        if self.passing:
-            self.across.finish()
+        if self.starting:
+            self.across.finish(self.late)
 
 
 def by_past(mode, body):
@@ -1107,7 +1109,7 @@
 FORWARD_LOADS = 7
 
 
-def forward_kernel(mode, passing, *refs):
+def forward_kernel(mode, starting, ending, *refs):
     x_first, x_other, earlier, params, w_qkv, w_out, w_fc, w_proj, k_past, v_past = refs[:10]
     refs = refs[10:]
     (x_used, normed1, query, keys, values, mixed, lse, scaled2, inverse2, normed2, slope, act, out, passed) = refs[:14]
@@ -1122,7 +1124,8 @@
     wide = a_v.shape[1]
 
     loads = Loads(load_sem)
-    opening = Opening(passing, 0, x_first, x_other, earlier, x_v, load_sem.at[FORWARD_LOADS], open_sem)
+    opening_sems = [load_sem.at[FORWARD_LOADS + tile] for tile in range(TILES)]
+    opening = Opening(starting, 0, 1, (x_first, x_other), earlier, x_v, opening_sems, open_sem)
     opening.start()
     loads.start("qkv", w_qkv, wq_v)
     if mode is not False:
@@ -1131,7 +1134,7 @@
     loads.start("out", w_out, wo_v)
     loads.start("fc", w_fc, wf_v)
     loads.start("proj", w_proj, wp_v)
-    greet_step(0, passing)
+    greet_step(0)
     opening.send()
     exchange = Exchange(send_v, recv_v, send_sem, recv_sem)
     across = Across(0, o_v, passed, across_sem)
@@ -1150,8 +1153,7 @@
     def vector(row, start=0, size=None):
         return params[row : row + 1, start : start + (size or width)]
 
-    own_rows = pl.ds(rows, rows)
-    for tile in range(TILES):
+    def project(tile):
         span = pl.ds(tile * tile_rows, tile_rows)
         later = pl.ds(rows + tile * tile_rows, tile_rows)
         opening.take(tile)
@@ -1167,18 +1169,13 @@
         piece = jnp.dot(normed, wq_v[:, 2 * half :], preferred_element_type=F32)
         v_v[later, :] = (piece + vector(6, half, half)).astype(BF)
         store_rows(tile, (x_v, x_used), (n1_v, normed1), (q_v, query))
-    store(k_v.at[own_rows], keys)
-    store(v_v.at[own_rows], values)
-    if mode is not False:
-        loads.wait("k", "v")
-    loads.wait("out")
-
-    def attention(past):
-        first_key = 0 if past else rows
-        for tile in range(TILES):
-            span = pl.ds(tile * tile_rows, tile_rows)
+
+    def attend(tile):
+        span = pl.ds(tile * tile_rows, tile_rows)
+
+        def attention(past):
             length = (rows if past else 0) + (tile + 1) * tile_rows
-            reach = pl.ds(first_key, length)
+            reach = pl.ds(0 if past else rows, length)
 
             def pair(number, carry):
                 lanes = pl.ds(pl.multiple_of(number * 128, 128), 128)
@@ -1197,24 +1194,13 @@
                 return carry
 
             lax.fori_loop(0, half // 128, pair, 0, unroll=mode is not None)
-            partial = jnp.dot(m_v[span, :], wo_v[...], preferred_element_type=F32)
-            part_v[tile] = partial
-            exchange.give(tile, partial)
-
-    by_past(mode, attention)
-    store(m_v, mixed)
-    store(lse_v, lse)
-    loads.wait("fc", "proj")
-
-    def conclude(tile):
-        span = pl.ds(tile * tile_rows, tile_rows)
-        total = part_v[TILES + tile] + exchange.take(TILES + tile)
-        o_v[span, :] = (hid_v[span, :] + total + vector(5)).astype(BF)
-        store_rows(tile, (o_v, out))
-        if passing:
-            across.send(tile)
-
-    for tile in range(TILES):
+
+        by_past(mode, attention)
+        partial = jnp.dot(m_v[span, :], wo_v[...], preferred_element_type=F32)
+        part_v[tile] = partial
+        exchange.give(tile, partial)
+
+    def expand(tile):
         span = pl.ds(tile * tile_rows, tile_rows)
         hidden = x_v[span, :].astype(F32) + (part_v[tile] + exchange.take(tile)) + vector(2)
         hid_v[span, :] = hidden
@@ -1233,20 +1219,48 @@
             a_v[span, columns] = activated.astype(BF)
             sl_v[span, columns] = inclined.astype(BF)
         store_rows(tile, (sl_v, slope), (a_v, act))
-        if tile > 0:
-            conclude(tile - 1)
         partial = jnp.dot(a_v[span, :], wp_v[...], preferred_element_type=F32)
         part_v[TILES + tile] = partial
         exchange.give(TILES + tile, partial)
-    conclude(TILES - 1)
+
+    def conclude(tile):
+        span = pl.ds(tile * tile_rows, tile_rows)
+        total = part_v[TILES + tile] + exchange.take(TILES + tile)
+        o_v[span, :] = (hid_v[span, :] + total + vector(5)).astype(BF)
+        store_rows(tile, (o_v, out))
+
+    own_rows = pl.ds(rows, rows)
+    project(0)
+    if mode is not False:
+        loads.wait("k", "v")
+    loads.wait("out")
+    attend(0)
+    project(1)
+    store(k_v.at[own_rows], keys)
+    store(v_v.at[own_rows], values)
+    loads.wait("fc", "proj")
+    if ending:
+        expand(0)
+    attend(1)
+    store(m_v, mixed)
+    store(lse_v, lse)
+    if ending:
+        conclude(0)
+        across.send(0)
+        expand(1)
+        across.receive(0)
+    else:
+        expand(0)
+        expand(1)
+        conclude(0)
+    conclude(1)
     for copy in stores:
         copy.wait()
     exchange.finish(2 * TILES)
     opening.finish()
-    if passing:
-        for tile in range(TILES):
-            across.receive(tile)
-        across.finish()
+    if ending:
+        across.complete(0)
+        across.finish(0)
 
 
 def step_sems(loads, stores):
@@ -1260,7 +1274,7 @@
     ]
 
 
-def forward_step(mode, passing, inputs, params, weights, past):
+def forward_step(mode, starting, ending, inputs, params, weights, past):
     rows, width = inputs[0].shape
     half = width // 2
     wide = weights[2].shape[1]
@@ -1306,12 +1320,12 @@
     ]
     number = {False: 3, None: 4, True: 5}[mode]
     return pl.pallas_call(
-        functools.partial(forward_kernel, mode, passing),
+        functools.partial(forward_kernel, mode, starting, ending),
         out_shape=[jax.ShapeDtypeStruct(*item) for item in outs],
         in_specs=[spot] * 3 + [pl.BlockSpec(memory_space=pltpu.VMEM)] + [spot] * 6,
         out_specs=[spot] * len(outs),
         scratch_shapes=[pltpu.VMEM(*item) for item in scratch]
-        + step_sems(FORWARD_LOADS + 1, 2 * len(outs)),
+        + step_sems(FORWARD_LOADS + TILES, 2 * len(outs)),
         compiler_params=pltpu.CompilerParams(
             collective_id=number, has_side_effects=True, vmem_limit_bytes=VMEM_LIMIT
         ),
@@ -1322,7 +1336,7 @@
 BACKWARD_LOADS = 17
 
 
-def backward_kernel(mode, passing, *refs):
+def backward_kernel(mode, starting, ending, *refs):
     (g_first, g_other, earlier, x_used, params, w_qkv, w_out, w_fc, w_proj) = refs[:9]
     (query, keys, values, k_past, v_past, mixed, lse, scaled2, inverse2, slope, pend_k, pend_v) = refs[9:21]
     refs = refs[21:]
@@ -1340,7 +1354,8 @@
     scale = HEAD_DIM**-0.5
 
     loads = Loads(load_sem)
-    opening = Opening(passing, 1, g_first, g_other, earlier, g_v, load_sem.at[BACKWARD_LOADS], open_sem)
+    opening_sems = [load_sem.at[BACKWARD_LOADS + tile] for tile in range(TILES)]
+    opening = Opening(starting, 1, 0, (g_first, g_other), earlier, g_v, opening_sems, open_sem)
     opening.start()
     loads.start("proj", w_proj, wp_v)
     loads.start("slope", slope, sl_v)
@@ -1361,7 +1376,7 @@
         loads.start("pend_v", pend_v, dv_v.at[own_rows])
     loads.start("qkv", w_qkv, wq_v)
     loads.start("x", x_used, x_v)
-    greet_step(1, passing)
+    greet_step(1)
     opening.send()
     exchange = Exchange(send_v, recv_v, send_sem, recv_sem)
     across = Across(1, o_v, passed, across_sem)
@@ -1372,6 +1387,11 @@
         copy.start()
         stores.append(copy)
 
+    def store_rows(tile, *pairs):
+        place = pl.ds(tile * tile_rows, tile_rows)
+        for buffer, dest in pairs:
+            store(buffer.at[place], dest.at[place])
+
     def vector(row, start=0, size=None):
         return params[row : row + 1, start : start + (size or width)]
 
@@ -1381,12 +1401,11 @@
         place = (slice(row, row + 1), slice(start, start + piece.shape[1]))
         sum_v[place] += jnp.sum(piece, axis=0, keepdims=True)
 
-    loads.wait("proj", "slope", "fc")
-    chunk = width // 2
-    for tile in range(TILES):
+    def contract(tile):
         span = pl.ds(tile * tile_rows, tile_rows)
         opening.take(tile)
         grad = g_v[span, :]
+        chunk = width // 2
         for part in range(wide // chunk):
             columns = pl.ds(part * chunk, chunk)
             d_act = cols_product(grad, wp_v[columns, :])
@@ -1397,10 +1416,9 @@
         part_v[tile] = partial
         exchange.give(tile, partial)
         tally(5, grad.astype(F32))
-    store(g_v, g_used)
-    store(dp_v, d_pre)
-    loads.wait("scaled2", "inverse2", "out")
-    for tile in range(TILES):
+        store_rows(tile, (g_v, g_used), (dp_v, d_pre))
+
+    def branch(tile):
         span = pl.ds(tile * tile_rows, tile_rows)
         d_normed = part_v[tile] + exchange.take(tile)
         scaled = s2_v[span, :].astype(F32)
@@ -1410,26 +1428,21 @@
             d_normed, scaled, i2_v[span, 0:1], vector(3)
         )
         hid_v[span, :] = d_hidden
-        branch = d_hidden.astype(BF)
-        db_v[span, :] = branch
-        tally(2, branch.astype(F32))
-        dm_v[span, :] = cols_product(branch, wo_v[...]).astype(BF)
-    store(db_v, d_branch)
-    loads.wait("q", "k", "v", "mixed", "lse")
-    if mode is not False:
-        loads.wait("k_past", "v_past")
-    if mode is not True:
-        loads.wait("pend_k", "pend_v")
-
-    def attention(past):
-        first_key = 0 if past else rows
-        if past:
-            dk_v[...] = jnp.zeros_like(dk_v)
-            dv_v[...] = jnp.zeros_like(dv_v)
-        for tile in range(TILES):
-            span = pl.ds(tile * tile_rows, tile_rows)
+        low = d_hidden.astype(BF)
+        db_v[span, :] = low
+        tally(2, low.astype(F32))
+        dm_v[span, :] = cols_product(low, wo_v[...]).astype(BF)
+        store_rows(tile, (db_v, d_branch))
+
+    def attend(tile):
+        span = pl.ds(tile * tile_rows, tile_rows)
+
+        def attention(past):
+            if past and tile == TILES - 1:
+                dk_v[...] = jnp.zeros_like(dk_v)
+                dv_v[...] = jnp.zeros_like(dv_v)
             length = (rows if past else 0) + (tile + 1) * tile_rows
-            reach = pl.ds(first_key, length)
+            reach = pl.ds(0 if past else rows, length)
 
             def pair(number, carry):
                 lanes = pl.ds(pl.multiple_of(number * 128, 128), 128)
@@ -1460,12 +1473,9 @@
 
             lax.fori_loop(0, half // 128, pair, 0, unroll=mode is not None)
 
-    by_past(mode, attention)
-    if mode is not False:
-        store(dk_v.at[past_rows], next_k)
-        store(dv_v.at[past_rows], next_v)
-    loads.wait("qkv", "x")
-    for tile in range(TILES):
+        by_past(mode, attention)
+
+    def project(tile):
         span = pl.ds(tile * tile_rows, tile_rows)
         later = pl.ds(rows + tile * tile_rows, tile_rows)
         dqkv_v[span, half : 2 * half] = dk_v[later, :].astype(BF)
@@ -1476,8 +1486,9 @@
         exchange.give(TILES + tile, partial)
         tally(6, piece[:, :half].astype(F32))
         tally(6, piece[:, 2 * half :].astype(F32), half)
-    store(dqkv_v, d_qkv)
-    for tile in range(TILES):
+        store_rows(tile, (dqkv_v, d_qkv))
+
+    def conclude(tile):
         span = pl.ds(tile * tile_rows, tile_rows)
         scaled, inverse = norm_parts(x_v[span, :].astype(F32))
         d_normed = part_v[TILES + tile] + exchange.take(TILES + tile)
@@ -1485,21 +1496,54 @@
         tally(1, d_normed)
         d_inputs = hid_v[span, :] + norm_backward(d_normed, scaled, inverse, vector(0))
         o_v[span, :] = d_inputs.astype(BF)
-        if passing:
-            across.send(tile)
-    store(o_v, out)
+        store_rows(tile, (o_v, out))
+
+    loads.wait("proj", "slope", "fc")
+    contract(1)
+    if not starting:
+        contract(0)
+    loads.wait("scaled2", "inverse2", "out")
+    branch(1)
+    loads.wait("q", "k", "v", "mixed", "lse")
+    if mode is not False:
+        loads.wait("k_past", "v_past")
+    if mode is not True:
+        loads.wait("pend_k", "pend_v")
+    attend(1)
+    loads.wait("qkv", "x")
+    if starting and not ending:
+        contract(0)
+    project(1)
+    if starting and ending:
+        contract(0)
+    else:
+        branch(0)
+    if ending:
+        conclude(1)
+        across.send(1)
+    if starting and ending:
+        branch(0)
+    attend(0)
+    if mode is not False:
+        store(dk_v.at[past_rows], next_k)
+        store(dv_v.at[past_rows], next_v)
+    project(0)
+    if ending:
+        across.receive(1)
+    else:
+        conclude(1)
+    conclude(0)
     store(sum_v, sums)
     for copy in stores:
         copy.wait()
     exchange.finish(2 * TILES)
     opening.finish()
-    if passing:
-        for tile in range(TILES):
-            across.receive(tile)
-        across.finish()
-
-
-def backward_step(mode, passing, grads, inputs, params, weights, kept, pending):
+    if ending:
+        across.complete(1)
+        across.finish(1)
+
+
+def backward_step(mode, starting, ending, grads, inputs, params, weights, kept, pending):
     rows, width = inputs.shape
     half = width // 2
     wide = weights[2].shape[1]
@@ -1545,12 +1589,12 @@
     ]
     number = {True: 6, None: 7, False: 8}[mode]
     return pl.pallas_call(
-        functools.partial(backward_kernel, mode, passing),
+        functools.partial(backward_kernel, mode, starting, ending),
         out_shape=[jax.ShapeDtypeStruct(*item) for item in outs],
         in_specs=[spot] * 4 + [pl.BlockSpec(memory_space=pltpu.VMEM)] + [spot] * 16,
         out_specs=[spot] * len(outs),
         scratch_shapes=[pltpu.VMEM(*item) for item in scratch]
-        + step_sems(BACKWARD_LOADS + 1, len(outs)),
+        + step_sems(BACKWARD_LOADS + TILES, 2 * len(outs)),
         compiler_params=pltpu.CompilerParams(
             collective_id=number, has_side_effects=True, vmem_limit_bytes=VMEM_LIMIT
         ),
@@ -1604,7 +1648,8 @@
         output = outputs[-1] if outputs else outer[0]
         used, normed1, *state, normed2, slope, act, output, got = forward_step(
             (False, None, True)[step],
-            step == 1,
+            step > 0,
+            step < micro,
             (outer[min(step, micro - 1)], got, output),
             params,
             weights,
@@ -1625,7 +1670,8 @@
         result = results[-1] if results else outer[1]
         grad, d_qkv, d_branch, d_pre, result, *pending, vector, got = backward_step(
             (True, None, False)[step],
-            step == 1,
+            step > 0,
+            step < micro,
             (got, outer[max(micro - 1 - step, 0)], result),
             received[last],
             params,

time: 545 us -> 538 us (0.987)
  Pallas kernels: 535 us -> 527 us
    pallas_call x6, Pallas kernels: 186 us -> 178 us  [the longest x3 93.8 us: backward_step(): pl.pallas_call(functools.partial(backward_kernel, mode, starting, ending)...]
where the time goes in v7:
time: 538 us; the launch traced here: 528 us
  Pallas kernels  527 us (98%)
    pallas_call x1, Pallas kernels, ring_scatter(): pl.pallas_call(functools.partial(scatter_kernel, size, count), out_shape=...  131 us
    pallas_call x1, Pallas kernels, ring_gather(): pl.pallas_call(functools.partial(gather_kernel, size, groups), out_shape=...  127 us
    pallas_call x3, Pallas kernels, backward_step(): pl.pallas_call(functools.partial(backward_kernel, mode, starting, ending)...  93.8 us
    pallas_call x3, Pallas kernels, forward_step(): pl.pallas_call(functools.partial(forward_kernel, mode, starting, ending),...  83.7 us
    pallas_call x1, Pallas kernels, fetch_inputs(): pl.pallas_call(fetch_kernel, out_shape=[jax.ShapeDtypeStruct(shape, BF) f...  74.5 us
    pallas_call x1, Pallas kernels, finish(): pl.pallas_call(finish_kernel, out_shape=[jax.ShapeDtypeStruct((item.shape...  16.3 us

profile of v7, /device:TPU:1, one launch (start us, length us, event | category | flops | bytes accessed | tf_op | source)
XLA Modules:
  0.0 527.7 jit_solution(6076286224501335095)
XLA Ops:
  0.7 74.5 %fetch_inputs.1 = (bf16[512,1024]{1,0:T(8,128)(2,1)}, bf16[512,1024]{1,0:T(8,128)(2,1)}, f32[16,1024]{1,0:T(8,128)}, bf16[1024,1536]{1,0:T(8,128)(2,1)}, bf16[10...) custom-call(bf16[2,256,1024]{2,1,0:T(8,128)(2,1)} %bitcast.19, ...), custom_call_target="tpu_custom_call" | custom-call | tf_op jit(solution)/shard_map/fetch_inputs/pallas_call | solution.py:915
  75.2 24.9 %forward_step.3 = (bf16[512,1024]{1,0:T(8,128)(2,1)}, bf16[512,1024]{1,0:T(8,128)(2,1)}, bf16[512,512]{1,0:T(8,128)(2,1)}, bf16[512,512]{1,0:T(8,128)(2,1)}, bf1...) custom-call(bf16[512,1024]{1,0:T(8,128)(2,1)} %get-tuple-element.113, ...), custom_call_target="tpu_custom_call" | custom-call | tf_op jit(solution)/shard_map/forward_step/pallas_call | solution.py:1322
  100.1 30.6 %forward_step.4 = (bf16[512,1024]{1,0:T(8,128)(2,1)}, bf16[512,1024]{1,0:T(8,128)(2,1)}, bf16[512,512]{1,0:T(8,128)(2,1)}, bf16[512,512]{1,0:T(8,128)(2,1)}, bf1...) custom-call(bf16[512,1024]{1,0:T(8,128)(2,1)} %get-tuple-element.120, ...), custom_call_target="tpu_custom_call" | custom-call | tf_op jit(solution)/shard_map/forward_step/pallas_call | solution.py:1322
  130.8 28.1 %forward_step.5 = (bf16[512,1024]{1,0:T(8,128)(2,1)}, bf16[512,1024]{1,0:T(8,128)(2,1)}, bf16[512,512]{1,0:T(8,128)(2,1)}, bf16[512,512]{1,0:T(8,128)(2,1)}, bf1...) custom-call(bf16[512,1024]{1,0:T(8,128)(2,1)} %get-tuple-element.120, ...), custom_call_target="tpu_custom_call" | custom-call | tf_op jit(solution)/shard_map/forward_step/pallas_call | solution.py:1322
  158.9 32.6 %backward_step.3 = (bf16[512,1024]{1,0:T(8,128)(2,1)}, bf16[512,1536]{1,0:T(8,128)(2,1)}, bf16[512,1024]{1,0:T(8,128)(2,1)}, bf16[512,2048]{1,0:T(8,128)(2,1)}, ...) custom-call(bf16[512,1024]{1,0:T(8,128)(2,1)} %get-tuple-element.120, ...), custom_call_target="tpu_custom_call" | custom-call | tf_op jit(solution)/shard_map/backward_step/pallas_call | solution.py:1591
  191.5 34.8 %backward_step.4 = (bf16[512,1024]{1,0:T(8,128)(2,1)}, bf16[512,1536]{1,0:T(8,128)(2,1)}, bf16[512,1024]{1,0:T(8,128)(2,1)}, bf16[512,2048]{1,0:T(8,128)(2,1)}, ...) custom-call(bf16[512,1024]{1,0:T(8,128)(2,1)} %get-tuple-element.140, ...), custom_call_target="tpu_custom_call" | custom-call | tf_op jit(solution)/shard_map/backward_step/pallas_call | solution.py:1591
  226.3 26.5 %backward_step.5 = (bf16[512,1024]{1,0:T(8,128)(2,1)}, bf16[512,1536]{1,0:T(8,128)(2,1)}, bf16[512,1024]{1,0:T(8,128)(2,1)}, bf16[512,2048]{1,0:T(8,128)(2,1)}, ...) custom-call(bf16[512,1024]{1,0:T(8,128)(2,1)} %get-tuple-element.151, ...), custom_call_target="tpu_custom_call" | custom-call | tf_op jit(solution)/shard_map/backward_step/pallas_call | solution.py:1591
  252.8 131.1 %ring_scatter.1 = (bf16[2,64,1536]{2,1,0:T(8,128)(2,1)}, bf16[2,64,2048]{2,1,0:T(8,128)(2,1)}, bf16[2,32,1024]{2,1,0:T(8,128)(2,1)}, bf16[2,128,1024]{2,1,0:T(8,128)(2,1)}, f32[16,512]{1,0:T(8,128)}) custom-call(bf16[512,1024]{1,0:T(8,128)(2,1)} %get-tuple-element.119.refs_0_, bf16[512,1024]{1,0:T(8,128)(2,1)} %get-tuple-element.125.refs_1_, ...), custom_call_target="tpu_custom_call" | custom-call | tf_op jit(solution)/shard_map/ring_scatter/pallas_call | solution.py:268
  383.9 127.1 %ring_gather.1 = (bf16[8,64,3072]{2,1,0:T(8,128)(2,1)}, bf16[8,64,4096]{2,1,0:T(8,128)(2,1)}, bf16[2,8,32,1024]{3,2,1,0:T(8,128)(2,1)}, bf16[2,8,128,1024]{3,2,1...) custom-call(bf16[2,64,1536]{2,1,0:T(8,128)(2,1)} %get-tuple-element.183.refs_0_, ...), custom_call_target="tpu_custom_call" | custom-call | tf_op jit(solution)/shard_map/ring_gather/pallas_call | solution.py:507
  511.0 16.3 %finish.1 = (f32[512,3072]{1,0:T(8,128)}, f32[512,4096]{1,0:T(8,128)}, f32[512,1024]{1,0:T(8,128)}, f32[2048,1024]{1,0:T(8,128)}, f32[1,512]{1,0:T(1,128)}, /*in...) custom-call(bf16[8,64,3072]{2,1,0:T(8,128)(2,1)} %get-tuple-element., ...), custom_call_target="tpu_custom_call" | custom-call | tf_op jit(solution)/shard_map/finish/pallas_call | solution.py:586

commit v8 on v7

--- a/solution.py
+++ b/solution.py
@@ -119,17 +119,19 @@
             source, held[number].at[part], load_sem.at[number, 0 if which == 1 else 1]
         )
 
-    for number in range(2 * count):
-        load(number, 1).start()
-
-        @pl.when(layer == 0)
-        def _(number=number):
-            load(number, 0).start()
-
-        @pl.when(layer != 0)
-        def _(number=number):
-            load(number, 2).start()
-
+    def load_item(item):
+        for number in (2 * item, 2 * item + 1):
+            load(number, 1).start()
+
+            @pl.when(layer == 0)
+            def _(number=number):
+                load(number, 0).start()
+
+            @pl.when(layer != 0)
+            def _(number=number):
+                load(number, 2).start()
+
+    load_item(0)
     greet(targets + (diagonal,))
 
     def send(way, item, source, slot):
@@ -207,6 +209,8 @@
         for number in (2 * item, 2 * item + 1):
             load(number, 1).wait()
             load(number, 0).wait()
+        if item + 1 < count:
+            load_item(item + 1)
         for way in range(2):
             product(item, way, first[way] // group)
             send(way, item, own[item].at[way, first[way]], 0).start()
@@ -216,23 +220,32 @@
         swap().wait()
 
     send_small(place, 0).start()
+
+    def relay(item, way, slot):
+        here = landed[item].at[way, slot]
+        send(way, item, here, slot).wait_recv()
+        here[...] += own[item][way, chunk_of(way, slot)]
+        send(way, item, here, slot + 1).start()
+
+    def relay_small(slot):
+        chunk = (place + size - 1 - slot) % size
+        send_small(chunk, slot).wait_recv()
+        send_small(chunk, slot + 1).start()
+
     for item in range(count):
         for way in range(2):
             product(item, way, 1 - first[way] // group)
+            relay(item, way, 0)
+    relay_small(0)
 
     def step(slot, carry):
         for item in range(count):
             for way in range(2):
-                here = landed[item].at[way, slot]
-                send(way, item, here, slot).wait_recv()
-                here[...] += own[item][way, chunk_of(way, slot)]
-                send(way, item, here, slot + 1).start()
-        chunk = (place + size - 1 - slot) % size
-        send_small(chunk, slot).wait_recv()
-        send_small(chunk, slot + 1).start()
+                relay(item, way, slot)
+        relay_small(slot)
         return carry
 
-    lax.fori_loop(0, size - 2, step, 0)
+    lax.fori_loop(1, size - 2, step, 0)
     last = size - 2
     for item in range(count):
         for way in range(2):
@@ -525,38 +538,8 @@
 
 
 def finish_kernel(*refs):
-    gathered, packed, placed = refs[:4], refs[4], refs[5:7]
-    wide, vectors, moved = refs[7:11], refs[11:20], refs[20:22]
-    low, high, bounce = refs[22:26], refs[26:30], refs[30]
-    fetch_sem, store_sem, load_sem = refs[31:]
-
-    def fetch(item, chunk):
-        return pltpu.make_async_copy(
-            gathered[item].at[chunk], low[item].at[chunk], fetch_sem.at[item, chunk]
-        )
-
-    def store(item, chunk):
-        deep = low[item].shape[1]
-        place = pl.ds(pl.multiple_of(chunk * deep, deep), deep)
-        return pltpu.make_async_copy(
-            high[item].at[chunk], wide[item].at[place], store_sem.at[item, chunk]
-        )
-
-    def every(action):
-        for item in range(4):
-
-            def step(chunk, carry, item=item):
-                action(item, chunk)
-                return carry
-
-            lax.fori_loop(0, low[item].shape[0], step, 0)
-
-    def widen(item, chunk):
-        fetch(item, chunk).wait()
-        high[item][chunk] = low[item][chunk].astype(F32)
-        store(item, chunk).start()
-
-    every(lambda item, chunk: fetch(item, chunk).start())
+    packed, placed, vectors, moved = refs[0], refs[1:3], refs[3:12], refs[12:14]
+    bounce, load_sem = refs[14:]
     loads = [pltpu.make_async_copy(placed[i], bounce.at[i], load_sem.at[i]) for i in range(2)]
     for copy in loads:
         copy.start()
@@ -565,46 +548,33 @@
         for index in range(vectors[number].shape[1] // half):
             row = number + index
             vectors[number][:, index * half : (index + 1) * half] = packed[row : row + 1, :]
-    every(widen)
     stores = []
     for i in range(2):
         loads[i].wait()
         copy = pltpu.make_async_copy(bounce.at[i], moved[i], load_sem.at[i])
         copy.start()
         stores.append(copy)
-    every(lambda item, chunk: store(item, chunk).wait())
     for copy in stores:
         copy.wait()
 
 
-def finish(gathered, packed, placed):
+def finish(packed, placed):
     spot = pl.BlockSpec(memory_space=pl.ANY)
     whole = pl.BlockSpec(memory_space=pltpu.VMEM)
-    gathered = [item.reshape((-1,) + item.shape[-2:]) for item in gathered]
     half = packed.shape[1]
-    most = max(item.shape[0] for item in gathered)
     return pl.pallas_call(
         finish_kernel,
-        out_shape=[
-            jax.ShapeDtypeStruct((item.shape[0] * item.shape[1], item.shape[2]), F32)
-            for item in gathered
-        ]
-        + [jax.ShapeDtypeStruct((1, half), F32)] * 8
+        out_shape=[jax.ShapeDtypeStruct((1, half), F32)] * 8
         + [jax.ShapeDtypeStruct((1, 4 * half), F32)]
         + [jax.ShapeDtypeStruct(item.shape, BF) for item in placed],
-        in_specs=[spot] * 4 + [whole] + [spot] * 2,
-        out_specs=[spot] * 4 + [whole] * 9 + [spot] * 2,
-        scratch_shapes=[pltpu.VMEM(item.shape, BF) for item in gathered]
-        + [pltpu.VMEM(item.shape, F32) for item in gathered]
-        + [
+        in_specs=[whole] + [spot] * 2,
+        out_specs=[whole] * 9 + [spot] * 2,
+        scratch_shapes=[
             pltpu.VMEM((2,) + placed[0].shape, BF),
-            pltpu.SemaphoreType.DMA((4, most)),
-            pltpu.SemaphoreType.DMA((4, most)),
             pltpu.SemaphoreType.DMA((2,)),
         ],
-        compiler_params=pltpu.CompilerParams(vmem_limit_bytes=VMEM_LIMIT),
         name="finish",
-    )(*gathered, packed, *placed)
+    )(packed, *placed)
 
 
 def fetch_kernel(*refs):
@@ -631,17 +601,22 @@
     depth = qkv.shape[0]
     span = qkv.shape[1] // 6
     wide = fc.shape[1] // 2
-    turn = proj.shape[0] // 2
+    strip, turn = wide // 2, proj.shape[0] // 4
     cols = [
         (qkv, w_qkv, lambda s, g=g: pl.multiple_of((2 * g + s) * span, span), g * span, span)
         for g in range(3)
     ]
-    cols.append((fc, w_fc, lambda s: pl.multiple_of(s * wide, wide), 0, wide))
-    rows = [(out, w_out, 0, out.shape[0]), (proj, w_proj, 0, turn), (proj, w_proj, turn, turn)]
-    order = [0, 1, 2, 4, 3, 5, 6]
+    cols += [
+        (fc, w_fc, lambda s, g=g: pl.multiple_of(s * wide + g * strip, strip), g * strip, strip)
+        for g in range(2)
+    ]
+    rows = [(out, w_out, 0, out.shape[0])]
+    rows += [(proj, w_proj, g * turn, turn) for g in range(4)]
+    narrow, total = len(cols), len(cols) + len(rows)
+    order = [0, 1, 2, 5, 3, 4, 6, 7, 8, 9]
 
     def rows_of(item):
-        return depth if item < 4 else rows[item - 4][3]
+        return depth if item < narrow else rows[item - narrow][3]
 
     def target(item, base, which, part=None):
         deep = rows_of(item) // 4
@@ -650,12 +625,12 @@
             deep = deep // 2
             start = start + part * deep
         place = pl.ds(pl.multiple_of(start, deep), deep)
-        if item < 4:
+        if item < narrow:
             return cols[item][1].at[place, pl.ds(cols[item][3], cols[item][4])]
-        return rows[item - 4][1].at[place]
+        return rows[item - narrow][1].at[place]
 
     def base_of(item, shard):
-        return shard * depth if item < 4 else rows[item - 4][2]
+        return shard * depth if item < narrow else rows[item - narrow][2]
 
     def remote(stage, item, source, dest, device, lane=0):
         return pltpu.make_async_remote_copy(
@@ -671,11 +646,11 @@
         deep = rows_of(item) // 4
         place = pl.multiple_of(base_of(item, 0) + quarter * deep, deep)
         dest = target(item, base_of(item, layer), quarter)
-        if item < 4:
+        if item < narrow:
             columns = cols[item][2](receiver)
             source = cols[item][0].at[pl.ds(place, deep), pl.ds(columns, cols[item][4])]
         else:
-            source = rows[item - 4][0].at[pl.ds(place, deep)]
+            source = rows[item - narrow][0].at[pl.ds(place, deep)]
         return source, dest
 
     def cross_same(item):
@@ -702,13 +677,13 @@
         )
 
     def keep_local(item):
-        if item < 4:
+        if item < narrow:
             columns = cols[item][2](core)
             source = cols[item][0].at[:, pl.ds(columns, cols[item][4])]
             start = pl.multiple_of(layer * depth, depth)
             dest = cols[item][1].at[pl.ds(start, depth), pl.ds(cols[item][3], cols[item][4])]
         else:
-            source, dest, start, deep = rows[item - 4]
+            source, dest, start, deep = rows[item - narrow]
             source, dest = source.at[pl.ds(start, deep)], dest.at[pl.ds(start, deep)]
         return through(source, dest, item)
 
@@ -746,7 +721,7 @@
 
     def outer_local(source, block):
         place = pl.ds(pl.multiple_of(layer * part, part), part)
-        return through(source.at[block], outer[block].at[place], 7 + block)
+        return through(source.at[block], outer[block].at[place], total + block)
 
     def small_swap():
         return pltpu.make_async_remote_copy(
@@ -778,7 +753,7 @@
             outer_cross(block)(tokens).start()
 
     def crossings(item):
-        if item < 4:
+        if item < narrow:
             cross_same(item).start()
         cross_swap(item).start()
 
@@ -802,7 +777,7 @@
 
     @pl.when(same)
     def _():
-        for item in range(4):
+        for item in range(narrow):
             to_sibling(item).start()
 
     span_small = small.shape[1]
@@ -830,7 +805,7 @@
 
     @pl.when(same)
     def _():
-        for item in range(7):
+        for item in range(total):
             keep_local(item)[0]().start()
 
     def relay(sequence, ahead):
@@ -864,23 +839,23 @@
 
     @pl.when(same)
     def _():
-        for item in range(7):
+        for item in range(total):
             load, store = keep_local(item)
             load().wait()
             store().start()
-        relay([0, 1, 2, 3], False)
-        for item in range(4):
+        relay(list(range(narrow)), False)
+        for item in range(narrow):
             to_sibling(item).wait_send()
-        for item in range(7):
+        for item in range(total):
             keep_local(item)[1]().wait()
 
     @pl.when(core != layer)
     def _():
         relay(order, True)
-        for item in range(4):
+        for item in range(narrow):
             to_sibling(item).wait_recv()
             cross_same(item).wait_send()
-        for item in range(7):
+        for item in range(total):
             cross_swap(item).wait_send()
         small_swap().wait_send()
 
@@ -920,21 +895,20 @@
         in_specs=[spot] * 15,
         out_specs=[spot] * 2 + [pl.BlockSpec(memory_space=pltpu.VMEM)] + [spot] * 4,
         scratch_shapes=[
-            pltpu.SemaphoreType.DMA((7, 7)),
-            pltpu.SemaphoreType.DMA((7, 7)),
+            pltpu.SemaphoreType.DMA((7, 10)),
+            pltpu.SemaphoreType.DMA((7, 10)),
             pltpu.SemaphoreType.DMA((6,)),
             pltpu.SemaphoreType.DMA((6,)),
-            pltpu.SemaphoreType.DMA((9,)),
+            pltpu.SemaphoreType.DMA((12,)),
             pltpu.SemaphoreType.DMA((9,)),
         ]
         + [pltpu.VMEM(item.shape, BF) for item in vectors]
         + [pltpu.VMEM((16, width // 2), F32), pltpu.VMEM((2, 16, width // 2), F32)]
         + [pltpu.VMEM((qkv.shape[0], qkv.shape[1] // 6), BF)] * 3
+        + [pltpu.VMEM((fc.shape[0], fc.shape[1] // 4), BF)] * 2
+        + [pltpu.VMEM(out.shape, BF)]
+        + [pltpu.VMEM((proj.shape[0] // 4, width), BF)] * 4
         + [
-            pltpu.VMEM((fc.shape[0], fc.shape[1] // 2), BF),
-            pltpu.VMEM(out.shape, BF),
-            pltpu.VMEM((proj.shape[0] // 2, width), BF),
-            pltpu.VMEM((proj.shape[0] // 2, width), BF),
             pltpu.VMEM(tokens.shape[1:], BF),
             pltpu.VMEM(tokens.shape[1:], BF),
         ],
@@ -1694,10 +1668,10 @@
         near += [outputs[i], outputs[i + 1], received[i + 1]]
         near += [results[micro - i], results[micro - 1 - i], grad_received[micro - i]]
     *gathered, activations, input_grads = ring_gather(reduced, (3, 1), near, size)
-    finished = finish(gathered, packed, (activations, input_grads))
-    qkv_grad, fc_grad, out_grad, proj_grad = (item[None] for item in finished[:4])
-    vectors = finished[4:13]
-    activations, input_grads = finished[13:]
+    *vectors, activations, input_grads = finish(packed, (activations, input_grads))
+    qkv_grad, fc_grad, out_grad, proj_grad = (
+        item.reshape(1, -1, item.shape[-1]).astype(F32) for item in gathered
+    )
     return (
         activations[None, None],
         input_grads[None, None],

time: 538 us -> 541 us (level)
  other arithmetic: 0 us -> 15.2 us
  Pallas kernels: 527 us -> 514 us
    convert_element_type x0 -> x4, other arithmetic: none -> 15.2 us  [shards(): item.reshape(1, -1, item.shape[-1]).astype(F32)]
    pallas_call x1, Pallas kernels: 16.3 us -> 4.14 us  [finish(): pl.pallas_call(finish_kernel, out_shape=[jax.ShapeDtypeStruct((1, half),...]
where the time goes in v8:
time: 541 us; the launch traced here: 531 us
  Pallas kernels  514 us (95%)
  other arithmetic  15.2 us (3%)
    pallas_call x1, Pallas kernels, ring_scatter(): pl.pallas_call(functools.partial(scatter_kernel, size, count), out_shape=...  132 us
    pallas_call x1, Pallas kernels, ring_gather(): pl.pallas_call(functools.partial(gather_kernel, size, groups), out_shape=...  127 us
    pallas_call x3, Pallas kernels, backward_step(): pl.pallas_call(functools.partial(backward_kernel, mode, starting, ending)...  93.8 us
    pallas_call x3, Pallas kernels, forward_step(): pl.pallas_call(functools.partial(forward_kernel, mode, starting, ending),...  84.6 us
    pallas_call x1, Pallas kernels, fetch_inputs(): pl.pallas_call(fetch_kernel, out_shape=[jax.ShapeDtypeStruct(shape, BF) f...  72.7 us
    convert_element_type x4, other arithmetic, shards(): item.reshape(1, -1, item.shape[-1]).astype(F32)  15.2 us

profile of v8, /device:TPU:1, one launch (start us, length us, event | category | flops | bytes accessed | tf_op | source)
XLA Modules:
  0.0 530.5 jit_solution(13286039901568333119)
XLA Ops:
  0.7 72.7 %fetch_inputs.1 = (bf16[512,1024]{1,0:T(8,128)(2,1)}, bf16[512,1024]{1,0:T(8,128)(2,1)}, f32[16,1024]{1,0:T(8,128)}, bf16[1024,1536]{1,0:T(8,128)(2,1)}, bf16[10...) custom-call(bf16[2,256,1024]{2,1,0:T(8,128)(2,1)} %bitcast.27, ...), custom_call_target="tpu_custom_call" | custom-call | tf_op jit(solution)/shard_map/fetch_inputs/pallas_call | solution.py:890
  73.4 25.9 %forward_step.3 = (bf16[512,1024]{1,0:T(8,128)(2,1)}, bf16[512,1024]{1,0:T(8,128)(2,1)}, bf16[512,512]{1,0:T(8,128)(2,1)}, bf16[512,512]{1,0:T(8,128)(2,1)}, bf1...) custom-call(bf16[512,1024]{1,0:T(8,128)(2,1)} %get-tuple-element.109, ...), custom_call_target="tpu_custom_call" | custom-call | tf_op jit(solution)/shard_map/forward_step/pallas_call | solution.py:1296
  99.3 30.5 %forward_step.4 = (bf16[512,1024]{1,0:T(8,128)(2,1)}, bf16[512,1024]{1,0:T(8,128)(2,1)}, bf16[512,512]{1,0:T(8,128)(2,1)}, bf16[512,512]{1,0:T(8,128)(2,1)}, bf1...) custom-call(bf16[512,1024]{1,0:T(8,128)(2,1)} %get-tuple-element.116, ...), custom_call_target="tpu_custom_call" | custom-call | tf_op jit(solution)/shard_map/forward_step/pallas_call | solution.py:1296
  129.8 28.2 %forward_step.5 = (bf16[512,1024]{1,0:T(8,128)(2,1)}, bf16[512,1024]{1,0:T(8,128)(2,1)}, bf16[512,512]{1,0:T(8,128)(2,1)}, bf16[512,512]{1,0:T(8,128)(2,1)}, bf1...) custom-call(bf16[512,1024]{1,0:T(8,128)(2,1)} %get-tuple-element.116, ...), custom_call_target="tpu_custom_call" | custom-call | tf_op jit(solution)/shard_map/forward_step/pallas_call | solution.py:1296
  158.0 32.6 %backward_step.3 = (bf16[512,1024]{1,0:T(8,128)(2,1)}, bf16[512,1536]{1,0:T(8,128)(2,1)}, bf16[512,1024]{1,0:T(8,128)(2,1)}, bf16[512,2048]{1,0:T(8,128)(2,1)}, ...) custom-call(bf16[512,1024]{1,0:T(8,128)(2,1)} %get-tuple-element.116, ...), custom_call_target="tpu_custom_call" | custom-call | tf_op jit(solution)/shard_map/backward_step/pallas_call | solution.py:1565
  190.5 34.5 %backward_step.4 = (bf16[512,1024]{1,0:T(8,128)(2,1)}, bf16[512,1536]{1,0:T(8,128)(2,1)}, bf16[512,1024]{1,0:T(8,128)(2,1)}, bf16[512,2048]{1,0:T(8,128)(2,1)}, ...) custom-call(bf16[512,1024]{1,0:T(8,128)(2,1)} %get-tuple-element.136, ...), custom_call_target="tpu_custom_call" | custom-call | tf_op jit(solution)/shard_map/backward_step/pallas_call | solution.py:1565
  225.1 26.7 %backward_step.5 = (bf16[512,1024]{1,0:T(8,128)(2,1)}, bf16[512,1536]{1,0:T(8,128)(2,1)}, bf16[512,1024]{1,0:T(8,128)(2,1)}, bf16[512,2048]{1,0:T(8,128)(2,1)}, ...) custom-call(bf16[512,1024]{1,0:T(8,128)(2,1)} %get-tuple-element.147, ...), custom_call_target="tpu_custom_call" | custom-call | tf_op jit(solution)/shard_map/backward_step/pallas_call | solution.py:1565
  251.8 131.9 %ring_scatter.1 = (bf16[2,64,1536]{2,1,0:T(8,128)(2,1)}, bf16[2,64,2048]{2,1,0:T(8,128)(2,1)}, bf16[2,32,1024]{2,1,0:T(8,128)(2,1)}, bf16[2,128,1024]{2,1,0:T(8,128)(2,1)}, f32[16,512]{1,0:T(8,128)}) custom-call(bf16[512,1024]{1,0:T(8,128)(2,1)} %get-tuple-element.115.refs_0_, bf16[512,1024]{1,0:T(8,128)(2,1)} %get-tuple-element.121.refs_1_, ...), custom_call_target="tpu_custom_call" | custom-call | tf_op jit(solution)/shard_map/ring_scatter/pallas_call | solution.py:281
  383.7 127.2 %ring_gather.1 = (bf16[8,64,3072]{2,1,0:T(8,128)(2,1)}, bf16[8,64,4096]{2,1,0:T(8,128)(2,1)}, bf16[2,8,32,1024]{3,2,1,0:T(8,128)(2,1)}, bf16[2,8,128,1024]{3,2,1...) custom-call(bf16[2,64,1536]{2,1,0:T(8,128)(2,1)} %get-tuple-element.180.refs_0_, ...), custom_call_target="tpu_custom_call" | custom-call | tf_op jit(solution)/shard_map/ring_gather/pallas_call | solution.py:520
  510.9 0.0 copy-start.2
  510.9 4.1 finish.1
  515.1 2.8 convert.5
  517.8 0.0 copy-done.2
  517.8 0.0 copy-start.1
  517.9 3.5 bitcast_convert_fusion.1
  521.4 0.0 copy-done.1
  521.4 0.0 copy-start
  521.4 4.5 bitcast_convert_fusion
  525.8 0.0 copy-done
  525.8 4.4 convert.7
Async XLA Ops:
  510.9 6.9 %copy-start.2 = (bf16[8,64,3072]{2,1,0:T(8,128)(2,1)S(1)}, bf16[8,64,3072]{2,1,0:T(8,128)(2,1)}, u32[]{:S(2)}) copy-start(bf16[8,64,3072]{2,1,0:T(8,128)(2,1)} %get-tuple-element.192) | copy-start | bytes 9437188
  517.8 3.5 copy-start.1
  521.4 4.5 copy-start
